TPU v7x, 32 devices: a whole 2x2x4 slice. The times are simulated.
32 devices in a mesh: groups: 2 (over y), tok: 4 (over z), slot: 2 (over x), hid: 2 (over core).
Axes of the slice: x: 2, y: 2, z: 4, core: 2. Of those that a mesh axis runs over, the one named last changes fastest.
Arguments:
- tokens: bfloat16 [8192, 1024], P(('groups', 'tok', 'slot', 'hid')), parts along dimension 0, may hold values from -12 to 12
- slot_keys: bfloat16 [2048, 512], P('groups', 'slot'), parts along dimension 0, may hold values from -12 to 12
- w_in: bfloat16 [4, 4, 1024, 4096], P(('groups', 'slot'), 'tok', None, 'hid'), parts along dimension 0, may hold values from -0.1875 to 0.1875
- w_out: bfloat16 [4, 4, 4096, 1024], P(('groups', 'slot'), 'tok', 'hid'), parts along dimension 0, may hold values from -0.09375 to 0.09375
Outputs:
- mixed: float32 [8192, 1024], P(('groups', 'tok', 'slot', 'hid')), parts along dimension 0
There are 2 independent parts, one for each index of `groups`. A program takes and returns all parts, laid end to end along the dimension named above; each array names one. Nothing has to cross between parts.
All inputs are finite; a program needn't handle non-finite values.
Results may differ from a plain program's by a relative error of at most 0.0022.
Values may be sent and summed in bfloat16 or wider, within the bound.
No kernel may reach another device: no remote copies, remote signals or barrier semaphores. Data moves between devices by JAX's collectives and lax.ppermute only.
A program may use at most 64 MiB of HBM per device.

v0:
```python
import jax
import jax.numpy as jnp
from jax import lax
from jax.sharding import PartitionSpec as P

epsilon = 1e-06


def local(tokens, slot_keys, w_in, w_out):
    model_width = tokens.shape[1]
    block_width = slot_keys.shape[1]
    owned_slots = block_width // (lax.axis_size("tok") * lax.axis_size("hid"))
    key_scale = lax.rsqrt(jnp.mean(jnp.square(slot_keys.astype(jnp.float32)), axis=0) + epsilon)
    fragment = lax.all_gather(tokens, "slot", axis=0, tiled=True)
    token_scale = lax.rsqrt(jnp.mean(jnp.square(fragment.astype(jnp.float32)), axis=1) + epsilon)
    logits = (
        4.0
        * token_scale[:, None]
        * key_scale[None, :]
        * jnp.dot(fragment, slot_keys, preferred_element_type=jnp.float32)
        / model_width
    )
    weights_exp = jnp.exp(logits)
    weights_low = weights_exp.astype(jnp.bfloat16)
    slot_numer = lax.dot_general(
        weights_low, fragment, (((0,), (0,)), ((), ())), preferred_element_type=jnp.float32
    )
    slot_denom = jnp.sum(weights_exp, axis=0)
    weights_all = weights_low
    token_denom = jnp.sum(weights_exp, axis=1)
    slot_numer, slot_denom, weights_all, token_denom = (
        slot_numer,
        slot_denom,
        weights_all,
        token_denom,
    )
    summed_numer, summed_denom = lax.psum((slot_numer, slot_denom), ("tok", "hid"))
    first_slot = lax.axis_index(("tok", "hid")) * owned_slots
    owned_numer = lax.dynamic_slice_in_dim(summed_numer, first_slot, owned_slots, 0)
    owned_denom = lax.dynamic_slice_in_dim(summed_denom, first_slot, owned_slots, 0)
    owned_inputs = (owned_numer / owned_denom[:, None]).astype(jnp.bfloat16)
    expert_inputs = lax.all_gather(owned_inputs, "hid", axis=0, tiled=True)
    hidden = jax.nn.gelu(
        jnp.dot(expert_inputs, w_in[0, 0], preferred_element_type=jnp.float32), approximate=True
    ).astype(jnp.bfloat16)
    half_outputs = jnp.dot(hidden, w_out[0, 0], preferred_element_type=jnp.float32)
    owned_outputs = lax.psum_scatter(half_outputs, "hid", scatter_dimension=0, tiled=True).astype(
        jnp.bfloat16
    )
    block_outputs = lax.all_gather(owned_outputs, ("tok", "hid"), axis=0, tiled=True)
    token_numer = jnp.dot(weights_all, block_outputs, preferred_element_type=jnp.float32)
    mine_numer, mine_denom = (
        lax.psum_scatter(token_numer, "slot", scatter_dimension=0, tiled=True),
        lax.psum_scatter(token_denom, "slot", scatter_dimension=0, tiled=True),
    )
    return mine_numer / mine_denom[:, None]


def solution(mesh):
    in_specs = (
        P(("groups", "tok", "slot", "hid"), None),
        P("groups", "slot"),
        P(("groups", "slot"), "tok", None, "hid"),
        P(("groups", "slot"), "tok", "hid", None),
    )
    out_specs = P(("groups", "tok", "slot", "hid"), None)
    return jax.shard_map(local, mesh=mesh, in_specs=in_specs, out_specs=out_specs, check_vma=False)
```

profile of v0, /device:TPU:0, one launch (start us, length us, event | category | flops | bytes accessed | tf_op | source)
XLA Modules:
  0.0 172.2 jit_solution(18349934714928174129)
XLA Ops:
  6.5 0.0 all-gather.2.cloned.1.call-start
  6.5 0.7 all-gather.2.cloned.1.call-update
  7.3 0.0 all-reduce.3.cloned.1.call-start
  7.3 1.2 multiply_reduce_fusion.1
  8.5 24.4 %all-gather.2.cloned.1.call-done = bf16[512,1024]{1,0:T(8,128)(2,1)} async-done(((bf16[256,1024]{1,0:T(8,128)(2,1)}), bf16[512,1024]{1,0:T(8,128)(2,1)}) %all-gather.2.cloned.1.call-update) | async-done | bytes 1048592 | tf_op jit(solution)/shard_map/all_gather | solution.py:14
  32.9 0.0 copy-start
  32.9 1.6 multiply_reduce_fusion
  34.5 1.9 %fusion.32 = (f32[512]{0:T(512)S(1)}, f32[256]{0:T(256)S(1)}, bf16[512,256]{1,0:T(8,128)(2,1)S(1)}) fusion(bf16[512,1024]{1,0:T(8,128)(2,1)} %all-gather.2.cloned.1.call-done, bf16[1024,256]{1,0:T(8,128)(2,1)} %param.5, f32[256]{0:T(256)S(1)} %add_rsqrt_fusion, f32[512]{0:T(512)S(1)} %rsqrt_multiply_fusion), kind=kOutput, calls=%fused_computation.34 | convolution fusion | flops 269221120 | bytes 1841152 | tf_op jit(solution)/shard_map/dot_general | solution.py:20
  36.4 0.0 copy-done
  36.4 1.4 fusion.26
  37.9 0.0 all-reduce.3.cloned.1.call-update
  37.9 0.0 reduce-scatter.3.cloned.1.call-start
  38.0 16.4 %psum.15 = f32[256]{0:T(256)S(1)} all-reduce(f32[256]{0:T(256)S(1)} %get-tuple-element.6), channel_id=1, replica_groups=mesh['groups'=2,'tok'=4,'slot'=2,'hid'=2] {'tok','hid'}, use_global_device_ids=true, to_apply=%region_4.0 | all-reduce | flops 256 | bytes 2048 | tf_op jit(solution)/shard_map/psum | solution.py:37
  54.4 0.1 dynamic_slice.7
  54.5 42.5 %all-reduce.3.cloned.1.call-done = f32[256,1024]{1,0:T(8,128)} async-done(((f32[256,1024]{1,0:T(8,128)}), f32[256,1024]{1,0:T(8,128)}) %all-reduce.3.cloned.1.call-update) | async-done | bytes 1048592 | tf_op jit(solution)/shard_map/psum | solution.py:37
  97.0 1.0 divide_convert_fusion
  98.0 1.9 %all_gather.10 = bf16[64,1024]{1,0:T(8,128)(2,1)S(1)} all-gather(bf16[32,1024]{1,0:T(8,128)(2,1)S(1)} %divide_convert_fusion), channel_id=1, replica_groups=mesh['groups'=2,'tok'=4,'slot'=2,'hid'=2] {'hid'}, dimensions={0}, use_global_device_ids=true | all-gather | bytes 196608 | tf_op jit(solution)/shard_map/all_gather | solution.py:42
  99.9 5.9 %fusion = f32[64,1024]{1,0:T(8,128)} fusion(bf16[1,1,2048,1024]{3,2,1,0:T(8,128)(2,1)} %param.7, bf16[64,1024]{1,0:T(8,128)(2,1)S(1)} %all_gather.10, bf16[1,1,1024,2048]{3,2,1,0:T(8,128)(2,1)} %param.6), kind=kOutput, calls=%fused_computation | convolution fusion | flops 538050560 | bytes 8781824 | tf_op jit(solution)/shard_map/dot_general | solution.py:46
  105.7 0.0 copy-start.1
  105.7 0.0 reduce-scatter.3.cloned.1.call-update
  105.7 0.0 reduce-scatter.5.cloned.1.call-start
  105.8 6.7 %reduce-scatter.3.cloned.1.call-done = f32[32,1024]{1,0:T(8,128)} async-done(((f32[64,1024]{1,0:T(8,128)}), f32[32,1024]{1,0:T(8,128)}) %reduce-scatter.3.cloned.1.call-update) | async-done | bytes 131088 | tf_op jit(solution)/shard_map/reduce_scatter | solution.py:47
  112.5 0.9 convert_element_type.23
  113.4 15.0 %all_gather.11 = bf16[256,1024]{1,0:T(8,128)(2,1)S(1)} all-gather(bf16[32,1024]{1,0:T(8,128)(2,1)S(1)} %convert_element_type.23), channel_id=1, replica_groups=mesh['groups'=2,'tok'=4,'slot'=2,'hid'=2] {'tok','hid'}, dimensions={0}, use_global_device_ids=true | all-gather | bytes 589824 | tf_op jit(solution)/shard_map/all_gather | solution.py:50
  128.4 1.8 %fusion.24 = f32[512,1024]{1,0:T(8,128)} fusion(bf16[256,1024]{1,0:T(8,128)(2,1)S(1)} %all_gather.11, bf16[512,256]{1,0:T(8,128)(2,1)S(1)} %get-tuple-element.7), kind=kOutput, calls=%fused_computation.24 | convolution fusion | flops 268435456 | bytes 2883584 | tf_op jit(solution)/shard_map/dot_general | solution.py:51
  130.2 0.0 reduce-scatter.5.cloned.1.call-update
  130.2 0.0 copy-done.1
  130.3 0.6 dynamic-slice
  131.5 4.9 %all-reduce = f32[512]{0:T(512)S(1)} all-reduce(f32[512]{0:T(512)S(1)} %get-tuple-element.5), channel_id=4, replica_groups=mesh['groups'=2,'tok'=4,'slot'=2,'hid'=2] {'slot'}, use_global_device_ids=true, to_apply=%region_8.0.clone | all-reduce | flops 512 | bytes 4096
  136.4 0.1 dynamic-slice.1
  136.5 26.8 %reduce-scatter.5.cloned.1.call-done = f32[256,1024]{1,0:T(8,128)} async-done(((f32[512,1024]{1,0:T(8,128)}), f32[256,1024]{1,0:T(8,128)}) %reduce-scatter.5.cloned.1.call-update) | async-done | bytes 1048592 | tf_op jit(solution)/shard_map/reduce_scatter | solution.py:53
  163.3 2.3 %broadcast_divide_fusion = f32[256,1024]{1,0:T(8,128)} fusion(f32[256,1024]{1,0:T(8,128)} %reduce-scatter.5.cloned.1.call-done, f32[256]{0:T(256)S(1)} %dynamic-slice.1), kind=kLoop, calls=%fused_computation.18 | loop fusion | flops 262144 | bytes 2098176 | tf_op jit(solution)/shard_map/div | solution.py:56
  (2 shorter events, 0.0 us)
Async XLA Ops:
  6.5 26.4 %all-gather.2.cloned.1.call-start = ((), (), s32[]{:S(2)}) async-start(), calls=%async_computation.2 | async-start | bytes 1572864 | tf_op jit(solution)/shard_map/all_gather | solution.py:14
  7.3 89.7 %all-reduce.3.cloned.1.call-start = ((), (), s32[]{:S(2)}) async-start(), calls=%async_computation.3 | async-start | bytes 2097152 | tf_op jit(solution)/shard_map/psum | solution.py:37
  32.9 3.5 %copy-start = (bf16[512,1024]{1,0:T(8,128)(2,1)S(1)}, bf16[512,1024]{1,0:T(8,128)(2,1)}, u32[]{:S(2)}) copy-start(bf16[512,1024]{1,0:T(8,128)(2,1)} %all-gather.2.cloned.1.call-done) | copy-start | bytes 3145732
  37.9 74.6 %reduce-scatter.3.cloned.1.call-start = ((), (), s32[]{:S(2)}) async-start(), calls=%async_computation.4 | async-start | bytes 393216 | tf_op jit(solution)/shard_map/reduce_scatter | solution.py:47
  105.7 24.5 %copy-start.1 = (u32[32]{0:T(128)S(1)}, u32[32]{0:T(128)}, u32[]{:S(2)}) copy-start(u32[32]{0:T(128)} %constant.43) | copy-start | bytes 388
  105.7 57.6 %reduce-scatter.5.cloned.1.call-start = ((), (), s32[]{:S(2)}) async-start(), calls=%async_computation.5 | async-start | bytes 3145728 | tf_op jit(solution)/shard_map/reduce_scatter | solution.py:53
Sparse Core Ops, SparseCore 0:
  8.9 23.9 all-gather.1
  38.0 58.8 all-reduce.2
  105.9 6.6 reduce-scatter.2
  130.4 32.8 reduce-scatter.4
where the time goes:
time: 173 us; the launch traced here: 172 us
  waiting for transfers between devices  101 us (58%)
  blocking collectives  38.2 us (22%)
  between operations  13.8 us (8%)
  matrix products  11 us (6%)
  other arithmetic  7.06 us (4%)
    psum x1, waiting for transfers between devices, local(): lax.psum((slot_numer, slot_denom), ('tok', 'hid'))  42.5 us
    reduce_scatter x1, waiting for transfers between devices, local(): lax.psum_scatter(token_numer, 'slot', scatter_dimension=0, tiled=True)  26.8 us
    all_gather x1, waiting for transfers between devices, local(): fragment = lax.all_gather(tokens, 'slot', axis=0, tiled=True)  24.4 us
    psum x1, blocking collectives, local(): lax.psum((slot_numer, slot_denom), ('tok', 'hid'))  16.4 us
    all_gather x1, blocking collectives, local(): lax.all_gather(owned_outputs, ('tok', 'hid'), axis=0, tiled=True)  15 us
    reduce_scatter x1, waiting for transfers between devices, local(): lax.psum_scatter(half_outputs, 'hid', scatter_dimension=0, tiled=True)  6.72 us
    dot_general x1, matrix products, local(): jnp.dot(hidden, w_out[0, 0], preferred_element_type=jnp.float32)  5.86 us
    unnamed x1, blocking collectives  4.94 us
  transfers between devices with their start and end apart: 4, of which 4 were waited for; matrix products, arithmetic and copies ran while one was open for 1% of the time, Pallas kernels for 0%

commit v1 on v0

v1 whole, which is shorter than its diff:
```python
import functools

import jax
import jax.numpy as jnp
from jax import lax
from jax.experimental import pallas as pl
from jax.experimental.pallas import tpu as pltpu
from jax.sharding import PartitionSpec as P

epsilon = 1e-06
bf16, f32 = jnp.bfloat16, jnp.float32
VMEM = pl.BlockSpec(memory_space=pltpu.VMEM)


def call(body, outs, *args, name, flops=0, nbytes=0):
    return pl.pallas_call(
        body,
        out_shape=[jax.ShapeDtypeStruct(s, d) for s, d in outs],
        in_specs=[VMEM] * len(args),
        out_specs=[VMEM] * len(outs),
        name=name,
        compiler_params=pltpu.CompilerParams(vmem_limit_bytes=40 * 2**20),
        cost_estimate=pl.CostEstimate(flops=flops, bytes_accessed=nbytes, transcendentals=0),
    )(*args)


def shift(value, axis, step):
    count = lax.axis_size(axis)
    return lax.ppermute(value, axis, [(i, (i + step) % count) for i in range(count)])


def dispatch_body(first, half, *refs):
    if first:
        tok_ref, key_ref, low_ref, keep_ref, send_ref = refs
    else:
        tok_ref, key_ref, keep_in, send_in, low_ref, keep_ref, send_ref = refs
    width = tok_ref.shape[1]
    slots = key_ref.shape[1]
    core = lax.axis_index("hid")
    tok = tok_ref[...].astype(f32)
    key = key_ref[...].astype(f32)
    tok_scale = lax.rsqrt(jnp.sum(tok * tok, axis=1, keepdims=True) / width + epsilon)
    key_scale = lax.rsqrt(jnp.sum(key * key, axis=0, keepdims=True) / width + epsilon)
    logits = jnp.dot(tok_ref[...], key_ref[...], preferred_element_type=f32)
    weights = jnp.exp(logits * (tok_scale * (4.0 / width)) * key_scale)
    low = weights.astype(bf16)
    low_ref[...] = low
    mine = pl.ds(pl.multiple_of(core * half, half), half)
    other = pl.ds(pl.multiple_of((1 - core) * half, half), half)
    dims = (((0,), (0,)), ((), ()))
    keep = lax.dot_general(low, tok_ref[:, mine], dims, preferred_element_type=f32)
    send = lax.dot_general(low, tok_ref[:, other], dims, preferred_element_type=f32)
    total = jnp.broadcast_to(jnp.sum(weights, axis=0, keepdims=True), (8, slots))
    if first:
        keep_ref[0:slots, :] = keep
        send_ref[0:slots, :] = send
        for ref in (keep_ref, send_ref):
            for at in range(0, slots, half):
                wide = min(half, slots - at)
                ref[slots + 8 * (at // half) : slots + 8 * (at // half) + 8, 0:wide] = total[:, at : at + wide]
    else:
        keep_ref[0:slots, :] = keep + keep_in[0:slots, :]
        send_ref[0:slots, :] = send + send_in[0:slots, :]
        for ref, old in ((keep_ref, keep_in), (send_ref, send_in)):
            for at in range(0, slots, half):
                wide = min(half, slots - at)
                rows = slice(slots + 8 * (at // half), slots + 8 * (at // half) + 8)
                ref[rows, 0:wide] = total[:, at : at + wide] + old[rows, 0:wide]


def share_body(owned, slots, keep_ref, recv_ref, mine_ref, total_ref, *send_refs):
    half = keep_ref.shape[1]
    row = lax.axis_index("tok")
    count = slots // owned
    for at in range(0, slots, half):
        wide = min(half, slots - at)
        rows = slice(slots + 8 * (at // half), slots + 8 * (at // half) + 8)
        total_ref[:, at : at + wide] = keep_ref[rows, 0:wide] + recv_ref[rows, 0:wide]
    for step in range(count):
        start = pl.multiple_of(lax.rem(row + step, count) * owned, owned)
        piece = keep_ref[pl.ds(start, owned), :] + recv_ref[pl.ds(start, owned), :]
        if step == 0:
            mine_ref[...] = piece
        else:
            send_refs[step - 1][...] = piece.astype(bf16)


def inputs_body(others, mine_ref, total_ref, *refs):
    piece_refs, total_refs, out_ref = refs[:others], refs[others : 2 * others], refs[2 * others]
    owned = mine_ref.shape[0]
    slots = total_ref.shape[1]
    numer = mine_ref[...]
    total = total_ref[0:1, :]
    for ref in piece_refs:
        numer = numer + ref[...].astype(f32)
    for ref in total_refs:
        total = total + ref[0:1, :]
    lane = lax.broadcasted_iota(jnp.int32, (owned, slots), 1)
    wanted = lax.broadcasted_iota(jnp.int32, (owned, slots), 0) + lax.axis_index("tok") * owned
    denom = jnp.sum(jnp.where(lane == wanted, jnp.broadcast_to(total, (owned, slots)), 0.0), axis=1, keepdims=True)
    out_ref[...] = (numer / denom).astype(bf16)


def expert_body(mine_ref, other_ref, in_ref, out_w_ref, out_ref):
    half = mine_ref.shape[1]
    core = lax.axis_index("hid")
    mine = pl.ds(pl.multiple_of(core * half, half), half)
    other = pl.ds(pl.multiple_of((1 - core) * half, half), half)
    value = jnp.dot(mine_ref[...], in_ref[mine, :], preferred_element_type=f32)
    value = value + jnp.dot(other_ref[...], in_ref[other, :], preferred_element_type=f32)
    hidden = jax.nn.gelu(value, approximate=True).astype(bf16)
    out_ref[...] = jnp.dot(hidden, out_w_ref[...], preferred_element_type=f32)


def outputs_body(part_ref, recv_ref, full_ref, half_ref):
    half = half_ref.shape[1]
    core = lax.axis_index("hid")
    full_ref[...] = (part_ref[...] + recv_ref[...]).astype(bf16)
    mine = pl.ds(pl.multiple_of(core * half, half), half)
    half_ref[...] = (part_ref[:, mine] + recv_ref[:, mine]).astype(bf16)


def combine_body(blocks, rows, *refs):
    low_refs = refs[:blocks]
    full_ref = refs[blocks]
    pieces = refs[blocks + 1 : -2]
    out_ref, all_ref = refs[-2], refs[-1]
    owned = full_ref.shape[0]
    half = full_ref.shape[1] // 2
    core = lax.axis_index("hid")
    row = lax.axis_index("tok")
    mine = pl.ds(pl.multiple_of(core * half, half), half)
    other = pl.ds(pl.multiple_of((1 - core) * half, half), half)
    at = 0
    for block in range(blocks):
        for step in range(rows):
            start = pl.ds(pl.multiple_of(lax.rem(row - step + rows, rows) * owned, owned), owned)
            if block == 0 and step == 0:
                all_ref[block, start, :] = full_ref[...]
                continue
            all_ref[block, start, mine] = pieces[at][...]
            all_ref[block, start, other] = pieces[at + 1][...]
            at += 2
    numer = None
    denom = None
    for block in range(blocks):
        low = low_refs[block][...]
        part = jnp.dot(low, all_ref[block], preferred_element_type=f32)
        total = jnp.sum(low.astype(f32), axis=1, keepdims=True)
        numer = part if numer is None else numer + part
        denom = total if denom is None else denom + total
    out_ref[...] = numer / denom


def local(tokens, slot_keys, w_in, w_out):
    count, width = tokens.shape
    slots = slot_keys.shape[1]
    rows, blocks = lax.axis_size("tok"), lax.axis_size("slot")
    owned = slots // rows
    half = width // 2
    extra = 8 * pl.cdiv(slots, half)
    part = ((slots + extra, half), f32)

    arrived = [shift(tokens, "slot", step) for step in range(1, blocks)]
    mac = 4 * count * width * slots
    low, keep, send = call(
        functools.partial(dispatch_body, True, half),
        [((count, slots), bf16), part, part],
        tokens, slot_keys, name="dispatch_own", flops=mac, nbytes=2 * count * width,
    )
    lows = [low]
    for step in range(1, blocks):
        low, keep, send = call(
            functools.partial(dispatch_body, False, half),
            [((count, slots), bf16), part, part],
            arrived[step - 1], slot_keys, keep, send, name="dispatch_other", flops=mac, nbytes=2 * count * width,
        )
        lows.append(shift(low, "slot", -step))
    recv = shift(send, "hid", 1)
    mine, total, *sends = call(
        functools.partial(share_body, owned, slots),
        [((owned, half), f32), ((8, slots), f32)] + [((owned, half), bf16)] * (rows - 1),
        keep, recv, name="share", nbytes=12 * slots * half,
    )
    totals = [shift(total, "tok", step) for step in range(1, rows)]
    pieces = [shift(sends[step - 1], "tok", step) for step in range(1, rows)]
    (inputs,) = call(
        functools.partial(inputs_body, rows - 1),
        [((owned, half), bf16)],
        mine, total, *pieces, *totals, name="slot_inputs", nbytes=8 * owned * width,
    )
    inputs_other = shift(inputs, "hid", 1)
    (outputs_part,) = call(
        expert_body, [((owned, width), f32)],
        inputs, inputs_other, w_in[0, 0], w_out[0, 0],
        name="expert", flops=4 * owned * width * w_in.shape[3], nbytes=4 * width * w_in.shape[3],
    )
    outputs_recv = shift(outputs_part, "hid", 1)
    full, mine_half = call(
        outputs_body, [((owned, width), bf16), ((owned, half), bf16)],
        outputs_part, outputs_recv, name="slot_outputs", nbytes=8 * owned * width,
    )
    chunks = [[mine_half] + [shift(mine_half, "tok", step) for step in range(1, rows)]]
    for step in range(1, blocks):
        chunks.append([shift(piece, "slot", step) for piece in chunks[0]])
    flat = [piece for block in range(blocks) for piece in chunks[block]][1:]
    pairs = []
    for piece in flat:
        pairs += [piece, shift(piece, "hid", 1)]
    order = [lows[0]] + [lows[(blocks - step) % blocks] for step in range(1, blocks)]
    return pl.pallas_call(
        functools.partial(combine_body, blocks, rows),
        out_shape=jax.ShapeDtypeStruct((count, width), f32),
        in_specs=[VMEM] * (blocks + 1 + len(pairs)),
        out_specs=VMEM,
        scratch_shapes=[pltpu.VMEM((blocks, slots, width), bf16)],
        name="combine",
        compiler_params=pltpu.CompilerParams(vmem_limit_bytes=40 * 2**20),
    )(*order, full, *pairs)


def solution(mesh):
    in_specs = (
        P(("groups", "tok", "slot", "hid"), None),
        P("groups", "slot"),
        P(("groups", "slot"), "tok", None, "hid"),
        P(("groups", "slot"), "tok", "hid", None),
    )
    out_specs = P(("groups", "tok", "slot", "hid"), None)
    return jax.shard_map(local, mesh=mesh, in_specs=in_specs, out_specs=out_specs, check_vma=False)
```

time: 173 us -> 58.6 us (0.34)
  waiting for transfers between devices: 101 us -> 26.2 us
  blocking collectives: 38.2 us -> 0 us
  starting transfers between devices: 0.12 us -> 21.7 us
  between operations: 13.8 us -> 0.09 us
  matrix products: 11 us -> 0 us
  other arithmetic: 7.06 us -> 0 us
  Pallas kernels: 0 us -> 4.99 us
  local copies, waits for them, and re-layouts: 0.75 us -> 5.32 us
    psum x1 -> x0, waiting for transfers between devices: 42.5 us -> none  [local(): lax.psum((slot_numer, slot_denom), ('tok', 'hid'))]
    reduce_scatter x2 -> x0, waiting for transfers between devices: 33.5 us -> none  [the longest x1 26.8 us: local(): lax.psum_scatter(token_numer, 'slot', scatter_dimension=0, tiled=True)]
    ppermute x0 -> x25, waiting for transfers between devices: none -> 26.2 us  [shift(): lax.ppermute(value, axis, [(i, (i + step) % count) for i in range(count)])]
    all_gather x1 -> x0, waiting for transfers between devices: 24.4 us -> none  [local(): fragment = lax.all_gather(tokens, 'slot', axis=0, tiled=True)]
    ppermute x0 -> x25, starting transfers between devices: none -> 21.7 us  [shift(): lax.ppermute(value, axis, [(i, (i + step) % count) for i in range(count)])]
    all_gather x2 -> x0, blocking collectives: 16.9 us -> none  [the longest x1 15 us: local(): lax.all_gather(owned_outputs, ('tok', 'hid'), axis=0, tiled=True)]
    psum x1 -> x0, blocking collectives: 16.4 us -> none  [local(): lax.psum((slot_numer, slot_denom), ('tok', 'hid'))]
    dot_general x4 -> x0, matrix products: 11 us -> none  [the longest x1 5.86 us: local(): jnp.dot(hidden, w_out[0, 0], preferred_element_type=jnp.float32)]
  transfers between devices with their start and end apart: 4 -> 25, of which waited for: 4 -> 12; matrix products, arithmetic and copies ran while one was open for 1% -> 0% of each run, Pallas kernels for 0% -> 2%
where the time goes in v1:
time: 58.6 us; the launch traced here: 58.3 us
  waiting for transfers between devices  26.2 us (45%)
  starting transfers between devices  21.7 us (37%)
  local copies, waits for them, and re-layouts  5.32 us (9%)
  Pallas kernels  4.99 us (9%)
    ppermute x25, waiting for transfers between devices, shift(): lax.ppermute(value, axis, [(i, (i + step) % count) for i in range(count)])  26.2 us
    ppermute x25, starting transfers between devices, shift(): lax.ppermute(value, axis, [(i, (i + step) % count) for i in range(count)])  21.7 us
    unnamed x10, local copies, waits for them, and re-layouts  5.32 us
    pallas_call x6, Pallas kernels, call(): pl.pallas_call(body, out_shape=[jax.ShapeDtypeStruct(s, d) for s, d in ou...  3.5 us
    pallas_call x1, Pallas kernels, local(): pl.pallas_call(functools.partial(combine_body, blocks, rows), out_shape=j...  1.49 us
  transfers between devices with their start and end apart: 25, of which 12 were waited for; matrix products, arithmetic and copies ran while one was open for 0% of the time, Pallas kernels for 2%

profile of v1, /device:TPU:0, one launch (start us, length us, event | category | flops | bytes accessed | tf_op | source)
XLA Modules:
  0.0 58.3 jit_solution(11478987220810362880)
XLA Ops:
  0.0 2.9 %collective-permute-start = (bf16[256,1024]{1,0:T(8,128)(2,1)}, bf16[256,1024]{1,0:T(8,128)(2,1)S(1)}, u32[]{:S(2)}, u32[]{:S(2)}) collective-permute-start(bf16[256,1024]{1,0:T(8,128)(2,1)} %refs_0_.1), channel_id=1, source_target_pairs={{0,2},{2,0},{1,3},{3,1},{4,6},{6,4},{5,7},{7,5},{8,10},{10,8},{9,1... | collective-permute-start | bytes 1572872 | tf_op jit(solution)/shard_map/ppermute | solution.py:29
  2.9 1.0 %copy-done.2 = bf16[1024,256]{1,0:T(8,128)(2,1)S(1)} copy-done((bf16[1024,256]{1,0:T(8,128)(2,1)S(1)}, bf16[1024,256]{1,0:T(8,128)(2,1)}, u32[]{:S(2)}) %copy-start.2) | copy-done | bytes 524312
  4.0 1.0 %copy-done.4 = bf16[256,1024]{1,0:T(8,128)(2,1)S(1)} copy-done((bf16[256,1024]{1,0:T(8,128)(2,1)S(1)}, bf16[256,1024]{1,0:T(8,128)(2,1)}, u32[]{:S(2)}) %copy-start.4) | copy-done | bytes 524312
  5.0 0.9 %dispatch_own.1 = (bf16[256,256]{1,0:T(8,128)(2,1)S(1)}, f32[264,512]{1,0:T(8,128)S(1)}, f32[264,512]{1,0:T(8,128)S(1)}) custom-call(bf16[256,1024]{1,0:T(8,128)(2,1)S(1)} %copy-done.4, bf16[1024,256]{1,0:T(8,128)(2,1)S(1)} %copy-done.2), custom_call_target="tpu_custom_call" | custom-call | flops 268435456 | bytes 524288 | tf_op jit(solution)/shard_map/dispatch_own/pallas_call | solution.py:16
  5.9 9.2 %collective-permute-done.refs_0_ = bf16[256,1024]{1,0:T(8,128)(2,1)S(1)} collective-permute-done((bf16[256,1024]{1,0:T(8,128)(2,1)}, bf16[256,1024]{1,0:T(8,128)(2,1)S(1)}, u32[]{:S(2)}, u32[]{:S(2)}) %collective-permute-start) | collective-permute-done | bytes 524320 | tf_op jit(solution)/shard_map/ppermute | solution.py:29
  15.1 1.0 %copy-done.3 = bf16[1024,256]{1,0:T(8,128)(2,1)S(1)} copy-done((bf16[1024,256]{1,0:T(8,128)(2,1)S(1)}, bf16[1024,256]{1,0:T(8,128)(2,1)}, u32[]{:S(2)}) %copy-start.3) | copy-done | bytes 524312
  16.1 0.9 %dispatch_other.1 = (bf16[256,256]{1,0:T(8,128)(2,1)S(1)}, f32[264,512]{1,0:T(8,128)S(1)}, f32[264,512]{1,0:T(8,128)S(1)}) custom-call(bf16[256,1024]{1,0:T(8,128)(2,1)S(1)} %collective-permute-done.refs_0_, bf16[1024,256]{1,0:T(8,128)(2,1)S(1)} %copy-done.3, f32[264,512]{1,0:T(8,128)S(1)} %get-tuple-element.19.refs_2_, f32[264,512]{1,0:T(8,128)S(1)} %get-tuple-element.20.refs_3_), custom_call_target="tpu_custom_call" | custom-call | flops 268435456 | bytes 524288 | tf_op jit(solution)/shard_map/dispatch_other/pallas_call | solution.py:16
  17.0 0.1 collective-permute-start.2
  17.1 1.9 %collective-permute-done.2.recv_ref = f32[264,512]{1,0:T(8,128)S(1)} collective-permute-done((f32[264,512]{1,0:T(8,128)S(1)}, f32[264,512]{1,0:T(8,128)S(1)}, u32[]{:S(2)}, u32[]{:S(2)}) %collective-permute-start.2) | collective-permute-done | bytes 540704 | tf_op jit(solution)/shard_map/ppermute | solution.py:29
  19.0 0.1 share.1
  19.0 1.9 %collective-permute-start.3 = (bf16[64,512]{1,0:T(8,128)(2,1)S(1)}, bf16[64,512]{1,0:T(8,128)(2,1)S(1)}, u32[]{:S(2)}, u32[]{:S(2)}) collective-permute-start(bf16[64,512]{1,0:T(8,128)(2,1)S(1)} %get-tuple-element.26), channel_id=1, source_target_pairs={{0,4},{4,8},{8,12},{12,0},{1,5},{5,9},{9,13},{13,1},{2,6},{6,10},{... | collective-permute-start | bytes 196616 | tf_op jit(solution)/shard_map/ppermute | solution.py:29
  20.9 2.6 %collective-permute-start.4 = (bf16[64,512]{1,0:T(8,128)(2,1)S(1)}, bf16[64,512]{1,0:T(8,128)(2,1)S(1)}, u32[]{:S(2)}, u32[]{:S(2)}) collective-permute-start(bf16[64,512]{1,0:T(8,128)(2,1)S(1)} %get-tuple-element.27), channel_id=1, source_target_pairs={{0,8},{4,12},{8,0},{12,4},{1,9},{5,13},{9,1},{13,5},{2,10},{6,14},... | collective-permute-start | bytes 196616 | tf_op jit(solution)/shard_map/ppermute | solution.py:29
  23.5 1.3 %collective-permute-start.5 = (bf16[64,512]{1,0:T(8,128)(2,1)S(1)}, bf16[64,512]{1,0:T(8,128)(2,1)S(1)}, u32[]{:S(2)}, u32[]{:S(2)}) collective-permute-start(bf16[64,512]{1,0:T(8,128)(2,1)S(1)} %get-tuple-element.28), channel_id=1, source_target_pairs={{0,12},{4,0},{8,4},{12,8},{1,13},{5,1},{9,5},{13,9},{2,14},{6,2},{... | collective-permute-start | bytes 196616 | tf_op jit(solution)/shard_map/ppermute | solution.py:29
  24.9 0.4 collective-permute-start.8
  25.3 1.7 %collective-permute-start.7 = (f32[8,256]{1,0:T(8,128)S(1)}, f32[8,256]{1,0:T(8,128)S(1)}, u32[]{:S(2)}, u32[]{:S(2)}) collective-permute-start(f32[8,256]{1,0:T(8,128)S(1)} %get-tuple-element.25.total_ref), channel_id=1, source_target_pairs={{0,8},{4,12},{8,0},{12,4},{1,9},{5,13},{9,1},{13,5},{2,10},{6,14},... | collective-permute-start | bytes 24584 | tf_op jit(solution)/shard_map/ppermute | solution.py:29
  27.0 1.6 %collective-permute-done.8.refs_5_ = f32[8,256]{1,0:T(8,128)S(1)} collective-permute-done((f32[8,256]{1,0:T(8,128)S(1)}, f32[8,256]{1,0:T(8,128)S(1)}, u32[]{:S(2)}, u32[]{:S(2)}) %collective-permute-start.8) | collective-permute-done | bytes 8224 | tf_op jit(solution)/shard_map/ppermute | solution.py:29
  28.6 1.9 %collective-permute-start.6 = (f32[8,256]{1,0:T(8,128)S(1)}, f32[8,256]{1,0:T(8,128)S(1)}, u32[]{:S(2)}, u32[]{:S(2)}) collective-permute-start(f32[8,256]{1,0:T(8,128)S(1)} %get-tuple-element.25.total_ref), channel_id=1, source_target_pairs={{0,4},{4,8},{8,12},{12,0},{1,5},{5,9},{9,13},{13,1},{2,6},{6,10},{... | collective-permute-start | bytes 24584 | tf_op jit(solution)/shard_map/ppermute | solution.py:29
  30.5 3.5 %collective-permute-done.6.refs_3_ = f32[8,256]{1,0:T(8,128)S(1)} collective-permute-done((f32[8,256]{1,0:T(8,128)S(1)}, f32[8,256]{1,0:T(8,128)S(1)}, u32[]{:S(2)}, u32[]{:S(2)}) %collective-permute-start.6) | collective-permute-done | bytes 8224 | tf_op jit(solution)/shard_map/ppermute | solution.py:29
  34.0 0.0 collective-permute-done.3.refs_0_
  34.0 0.0 collective-permute-done.4.refs_1_
  34.0 0.0 collective-permute-done.5.refs_2_
  34.0 0.1 slot_inputs.1.mine_ref
  34.1 0.1 collective-permute-start.9
  34.2 1.2 %collective-permute-done.9.other_ref = bf16[64,512]{1,0:T(8,128)(2,1)S(1)} collective-permute-done((bf16[64,512]{1,0:T(8,128)(2,1)S(1)}, bf16[64,512]{1,0:T(8,128)(2,1)S(1)}, u32[]{:S(2)}, u32[]{:S(2)}) %collective-permute-start.9) | collective-permute-done | bytes 65568 | tf_op jit(solution)/shard_map/ppermute | solution.py:29
  35.5 2.2 %copy-done.1 = bf16[1,1,2048,1024]{3,2,1,0:T(8,128)(2,1)S(1)} copy-done((bf16[1,1,2048,1024]{3,2,1,0:T(8,128)(2,1)S(1)}, bf16[1,1,2048,1024]{3,2,1,0:T(8,128)(2,1)}, u32[]{:S(2)}) %copy-start.1) | copy-done | bytes 4194328
  37.7 1.6 %expert.1.part_ref = f32[64,1024]{1,0:T(8,128)S(1)} custom-call(bf16[64,512]{1,0:T(8,128)(2,1)S(1)} %slot_inputs.1.mine_ref, bf16[64,512]{1,0:T(8,128)(2,1)S(1)} %collective-permute-done.9.other_ref, bf16[1024,2048]{1,0:T(8,128)(2,1)S(1)} %bitcast.2, bf16[2048,1024]{1,0:T(8,128)(2,1)S(1)} %bitcast.3), custom_call_target="tpu_custom_call" | custom-call | flops 536870912 | bytes 8388608 | tf_op jit(solution)/shard_map/expert/pallas_call | solution.py:16
  39.3 0.2 collective-permute-start.10
  39.5 1.5 %collective-permute-start.1 = (bf16[256,256]{1,0:T(8,128)(2,1)S(1)}, bf16[256,256]{1,0:T(8,128)(2,1)S(1)}, u32[]{:S(2)}, u32[]{:S(2)}) collective-permute-start(bf16[256,256]{1,0:T(8,128)(2,1)S(1)} %get-tuple-element.21), channel_id=1, source_target_pairs={{0,2},{2,0},{1,3},{3,1},{4,6},{6,4},{5,7},{7,5},{8,10},{10,8},{9,1... | collective-permute-start | bytes 393224 | tf_op jit(solution)/shard_map/ppermute | solution.py:29
  41.0 0.0 collective-permute-done.10.recv_ref
  41.0 1.4 %collective-permute-start.17 = (bf16[64,512]{1,0:T(8,128)(2,1)S(1)}, bf16[64,512]{1,0:T(8,128)(2,1)S(1)}, u32[]{:S(2)}, u32[]{:S(2)}) collective-permute-start(bf16[64,512]{1,0:T(8,128)(2,1)S(1)} %get-tuple-element.30), channel_id=1, source_target_pairs={{0,2},{2,0},{1,3},{3,1},{4,6},{6,4},{5,7},{7,5},{8,10},{10,8},{9,1... | collective-permute-start | bytes 196616 | tf_op jit(solution)/shard_map/ppermute | solution.py:29
  42.5 0.8 %collective-permute-start.15 = (bf16[64,512]{1,0:T(8,128)(2,1)S(1)}, bf16[64,512]{1,0:T(8,128)(2,1)S(1)}, u32[]{:S(2)}, u32[]{:S(2)}) collective-permute-start(bf16[64,512]{1,0:T(8,128)(2,1)S(1)} %get-tuple-element.30), channel_id=1, source_target_pairs={{0,12},{4,0},{8,4},{12,8},{1,13},{5,1},{9,5},{13,9},{2,14},{6,2},{... | collective-permute-start | bytes 196616 | tf_op jit(solution)/shard_map/ppermute | solution.py:29
  43.3 0.7 %collective-permute-start.13 = (bf16[64,512]{1,0:T(8,128)(2,1)S(1)}, bf16[64,512]{1,0:T(8,128)(2,1)S(1)}, u32[]{:S(2)}, u32[]{:S(2)}) collective-permute-start(bf16[64,512]{1,0:T(8,128)(2,1)S(1)} %get-tuple-element.30), channel_id=1, source_target_pairs={{0,8},{4,12},{8,0},{12,4},{1,9},{5,13},{9,1},{13,5},{2,10},{6,14},... | collective-permute-start | bytes 196616 | tf_op jit(solution)/shard_map/ppermute | solution.py:29
  44.0 0.5 collective-permute-start.11
  44.5 2.2 %collective-permute-done.17.refs_9_ = bf16[64,512]{1,0:T(8,128)(2,1)S(1)} collective-permute-done((bf16[64,512]{1,0:T(8,128)(2,1)S(1)}, bf16[64,512]{1,0:T(8,128)(2,1)S(1)}, u32[]{:S(2)}, u32[]{:S(2)}) %collective-permute-start.17) | collective-permute-done | bytes 65568 | tf_op jit(solution)/shard_map/ppermute | solution.py:29
  46.6 0.0 collective-permute-start.18
  46.6 0.8 %collective-permute-done.15.refs_7_ = bf16[64,512]{1,0:T(8,128)(2,1)S(1)} collective-permute-done((bf16[64,512]{1,0:T(8,128)(2,1)S(1)}, bf16[64,512]{1,0:T(8,128)(2,1)S(1)}, u32[]{:S(2)}, u32[]{:S(2)}) %collective-permute-start.15) | collective-permute-done | bytes 65568 | tf_op jit(solution)/shard_map/ppermute | solution.py:29
  47.4 0.7 %collective-permute-start.23 = (bf16[64,512]{1,0:T(8,128)(2,1)S(1)}, bf16[64,512]{1,0:T(8,128)(2,1)S(1)}, u32[]{:S(2)}, u32[]{:S(2)}) collective-permute-start(bf16[64,512]{1,0:T(8,128)(2,1)S(1)} %collective-permute-done.15.refs_7_), channel_id=1, source_target_pairs={{0,2},{2,0},{1,3},{3,1},{4,6},{6,4},{5,7},{7,5},{8,10},{10,8},{9,1... | collective-permute-start | bytes 196616 | tf_op jit(solution)/shard_map/ppermute | solution.py:29
  48.1 0.2 collective-permute-start.16
  48.4 2.2 %collective-permute-done.13.refs_5_ = bf16[64,512]{1,0:T(8,128)(2,1)S(1)} collective-permute-done((bf16[64,512]{1,0:T(8,128)(2,1)S(1)}, bf16[64,512]{1,0:T(8,128)(2,1)S(1)}, u32[]{:S(2)}, u32[]{:S(2)}) %collective-permute-start.13) | collective-permute-done | bytes 65568 | tf_op jit(solution)/shard_map/ppermute | solution.py:29
  50.6 0.6 collective-permute-start.21
  51.2 1.5 %collective-permute-start.19 = (bf16[64,512]{1,0:T(8,128)(2,1)S(1)}, bf16[64,512]{1,0:T(8,128)(2,1)S(1)}, u32[]{:S(2)}, u32[]{:S(2)}) collective-permute-start(bf16[64,512]{1,0:T(8,128)(2,1)S(1)} %collective-permute-done.11.refs_3_), channel_id=1, source_target_pairs={{0,2},{2,0},{1,3},{3,1},{4,6},{6,4},{5,7},{7,5},{8,10},{10,8},{9,1... | collective-permute-start | bytes 196616 | tf_op jit(solution)/shard_map/ppermute | solution.py:29
  52.6 0.5 collective-permute-start.12
  53.1 0.1 collective-permute-start.24
  53.2 1.6 %collective-permute-done.21.refs_13_ = bf16[64,512]{1,0:T(8,128)(2,1)S(1)} collective-permute-done((bf16[64,512]{1,0:T(8,128)(2,1)S(1)}, bf16[64,512]{1,0:T(8,128)(2,1)S(1)}, u32[]{:S(2)}, u32[]{:S(2)}) %collective-permute-start.21) | collective-permute-done | bytes 65568 | tf_op jit(solution)/shard_map/ppermute | solution.py:29
  54.9 0.7 %collective-permute-done.19.refs_11_ = bf16[64,512]{1,0:T(8,128)(2,1)S(1)} collective-permute-done((bf16[64,512]{1,0:T(8,128)(2,1)S(1)}, bf16[64,512]{1,0:T(8,128)(2,1)S(1)}, u32[]{:S(2)}, u32[]{:S(2)}) %collective-permute-start.19) | collective-permute-done | bytes 65568 | tf_op jit(solution)/shard_map/ppermute | solution.py:29
  55.6 0.5 collective-permute-done.22.refs_14_
  56.1 0.7 %collective-permute-done.20.refs_12_ = bf16[64,512]{1,0:T(8,128)(2,1)S(1)} collective-permute-done((bf16[64,512]{1,0:T(8,128)(2,1)S(1)}, bf16[64,512]{1,0:T(8,128)(2,1)S(1)}, u32[]{:S(2)}, u32[]{:S(2)}) %collective-permute-start.20) | collective-permute-done | bytes 65568 | tf_op jit(solution)/shard_map/ppermute | solution.py:29
  56.8 1.5 %combine.1 = f32[256,1024]{1,0:T(8,128)} custom-call(bf16[256,256]{1,0:T(8,128)(2,1)S(1)} %get-tuple-element.18.refs_0_, bf16[256,256]{1,0:T(8,128)(2,1)S(1)} %collective-permute-done.1.refs_1_, bf16[64,1024]{1,0:T(8,128)(2,1)S(1)} %get-tuple-element.29.refs_2_, bf16[64,512]{1,0:T(8,128)(2,1)S(1)} %collective-permute-done.11.refs_3_, ...), custom_call_target="tpu_custom_call" | custom-call | tf_op jit(solution)/shard_map/combine/pallas_call | solution.py:211
  (19 shorter events, 0.1 us)
Async XLA Ops:
  0.0 35.5 %copy-start = (bf16[1,1,1024,2048]{3,2,1,0:T(8,128)(2,1)S(1)}, bf16[1,1,1024,2048]{3,2,1,0:T(8,128)(2,1)}, u32[]{:S(2)}) copy-start(bf16[1,1,1024,2048]{3,2,1,0:T(8,128)(2,1)} %param.6) | copy-start | bytes 12582916
  0.0 15.1 %collective-permute-start = (bf16[256,1024]{1,0:T(8,128)(2,1)}, bf16[256,1024]{1,0:T(8,128)(2,1)S(1)}, u32[]{:S(2)}, u32[]{:S(2)}) collective-permute-start(bf16[256,1024]{1,0:T(8,128)(2,1)} %refs_0_.1), channel_id=1, source_target_pairs={{0,2},{2,0},{1,3},{3,1},{4,6},{6,4},{5,7},{7,5},{8,10},{10,8},{9,1... | collective-permute-start | bytes 1572872 | tf_op jit(solution)/shard_map/ppermute | solution.py:29
  2.9 1.0 %copy-start.2 = (bf16[1024,256]{1,0:T(8,128)(2,1)S(1)}, bf16[1024,256]{1,0:T(8,128)(2,1)}, u32[]{:S(2)}) copy-start(bf16[1024,256]{1,0:T(8,128)(2,1)} %refs_1_.3) | copy-start | bytes 1572868
  4.0 1.0 %copy-start.4 = (bf16[256,1024]{1,0:T(8,128)(2,1)S(1)}, bf16[256,1024]{1,0:T(8,128)(2,1)}, u32[]{:S(2)}) copy-start(bf16[256,1024]{1,0:T(8,128)(2,1)} %refs_0_.1) | copy-start | bytes 1572868
  15.1 1.0 %copy-start.3 = (bf16[1024,256]{1,0:T(8,128)(2,1)S(1)}, bf16[1024,256]{1,0:T(8,128)(2,1)}, u32[]{:S(2)}) copy-start(bf16[1024,256]{1,0:T(8,128)(2,1)} %refs_1_.3) | copy-start | bytes 1572868
  17.0 2.0 %collective-permute-start.2 = (f32[264,512]{1,0:T(8,128)S(1)}, f32[264,512]{1,0:T(8,128)S(1)}, u32[]{:S(2)}, u32[]{:S(2)}) collective-permute-start(f32[264,512]{1,0:T(8,128)S(1)} %get-tuple-element.23), channel_id=1, source_target_pairs={{0,1},{1,0},{2,3},{3,2},{4,5},{5,4},{6,7},{7,6},{8,9},{9,8},{10,11... | collective-permute-start | bytes 1622024 | tf_op jit(solution)/shard_map/ppermute | solution.py:29
  19.0 15.0 %collective-permute-start.3 = (bf16[64,512]{1,0:T(8,128)(2,1)S(1)}, bf16[64,512]{1,0:T(8,128)(2,1)S(1)}, u32[]{:S(2)}, u32[]{:S(2)}) collective-permute-start(bf16[64,512]{1,0:T(8,128)(2,1)S(1)} %get-tuple-element.26), channel_id=1, source_target_pairs={{0,4},{4,8},{8,12},{12,0},{1,5},{5,9},{9,13},{13,1},{2,6},{6,10},{... | collective-permute-start | bytes 196616 | tf_op jit(solution)/shard_map/ppermute | solution.py:29
  20.9 13.1 %collective-permute-start.4 = (bf16[64,512]{1,0:T(8,128)(2,1)S(1)}, bf16[64,512]{1,0:T(8,128)(2,1)S(1)}, u32[]{:S(2)}, u32[]{:S(2)}) collective-permute-start(bf16[64,512]{1,0:T(8,128)(2,1)S(1)} %get-tuple-element.27), channel_id=1, source_target_pairs={{0,8},{4,12},{8,0},{12,4},{1,9},{5,13},{9,1},{13,5},{2,10},{6,14},... | collective-permute-start | bytes 196616 | tf_op jit(solution)/shard_map/ppermute | solution.py:29
  23.5 10.5 %collective-permute-start.5 = (bf16[64,512]{1,0:T(8,128)(2,1)S(1)}, bf16[64,512]{1,0:T(8,128)(2,1)S(1)}, u32[]{:S(2)}, u32[]{:S(2)}) collective-permute-start(bf16[64,512]{1,0:T(8,128)(2,1)S(1)} %get-tuple-element.28), channel_id=1, source_target_pairs={{0,12},{4,0},{8,4},{12,8},{1,13},{5,1},{9,5},{13,9},{2,14},{6,2},{... | collective-permute-start | bytes 196616 | tf_op jit(solution)/shard_map/ppermute | solution.py:29
  24.9 3.7 %collective-permute-start.8 = (f32[8,256]{1,0:T(8,128)S(1)}, f32[8,256]{1,0:T(8,128)S(1)}, u32[]{:S(2)}, u32[]{:S(2)}) collective-permute-start(f32[8,256]{1,0:T(8,128)S(1)} %get-tuple-element.25.total_ref), channel_id=1, source_target_pairs={{0,12},{4,0},{8,4},{12,8},{1,13},{5,1},{9,5},{13,9},{2,14},{6,2},{... | collective-permute-start | bytes 24584 | tf_op jit(solution)/shard_map/ppermute | solution.py:29
  25.3 5.2 %collective-permute-start.7 = (f32[8,256]{1,0:T(8,128)S(1)}, f32[8,256]{1,0:T(8,128)S(1)}, u32[]{:S(2)}, u32[]{:S(2)}) collective-permute-start(f32[8,256]{1,0:T(8,128)S(1)} %get-tuple-element.25.total_ref), channel_id=1, source_target_pairs={{0,8},{4,12},{8,0},{12,4},{1,9},{5,13},{9,1},{13,5},{2,10},{6,14},... | collective-permute-start | bytes 24584 | tf_op jit(solution)/shard_map/ppermute | solution.py:29
  28.6 5.4 %collective-permute-start.6 = (f32[8,256]{1,0:T(8,128)S(1)}, f32[8,256]{1,0:T(8,128)S(1)}, u32[]{:S(2)}, u32[]{:S(2)}) collective-permute-start(f32[8,256]{1,0:T(8,128)S(1)} %get-tuple-element.25.total_ref), channel_id=1, source_target_pairs={{0,4},{4,8},{8,12},{12,0},{1,5},{5,9},{9,13},{13,1},{2,6},{6,10},{... | collective-permute-start | bytes 24584 | tf_op jit(solution)/shard_map/ppermute | solution.py:29
  34.1 1.3 %collective-permute-start.9 = (bf16[64,512]{1,0:T(8,128)(2,1)S(1)}, bf16[64,512]{1,0:T(8,128)(2,1)S(1)}, u32[]{:S(2)}, u32[]{:S(2)}) collective-permute-start(bf16[64,512]{1,0:T(8,128)(2,1)S(1)} %slot_inputs.1.mine_ref), channel_id=1, source_target_pairs={{0,1},{1,0},{2,3},{3,2},{4,5},{5,4},{6,7},{7,6},{8,9},{9,8},{10,11... | collective-permute-start | bytes 196616 | tf_op jit(solution)/shard_map/ppermute | solution.py:29
  35.5 2.2 %copy-start.1 = (bf16[1,1,2048,1024]{3,2,1,0:T(8,128)(2,1)S(1)}, bf16[1,1,2048,1024]{3,2,1,0:T(8,128)(2,1)}, u32[]{:S(2)}) copy-start(bf16[1,1,2048,1024]{3,2,1,0:T(8,128)(2,1)} %param.7) | copy-start | bytes 12582916
  39.3 1.7 %collective-permute-start.10 = (f32[64,1024]{1,0:T(8,128)S(1)}, f32[64,1024]{1,0:T(8,128)S(1)}, u32[]{:S(2)}, u32[]{:S(2)}) collective-permute-start(f32[64,1024]{1,0:T(8,128)S(1)} %expert.1.part_ref), channel_id=1, source_target_pairs={{0,1},{1,0},{2,3},{3,2},{4,5},{5,4},{6,7},{7,6},{8,9},{9,8},{10,11... | collective-permute-start | bytes 786440 | tf_op jit(solution)/shard_map/ppermute | solution.py:29
  39.5 8.7 %collective-permute-start.1 = (bf16[256,256]{1,0:T(8,128)(2,1)S(1)}, bf16[256,256]{1,0:T(8,128)(2,1)S(1)}, u32[]{:S(2)}, u32[]{:S(2)}) collective-permute-start(bf16[256,256]{1,0:T(8,128)(2,1)S(1)} %get-tuple-element.21), channel_id=1, source_target_pairs={{0,2},{2,0},{1,3},{3,1},{4,6},{6,4},{5,7},{7,5},{8,10},{10,8},{9,1... | collective-permute-start | bytes 393224 | tf_op jit(solution)/shard_map/ppermute | solution.py:29
  41.0 5.6 %collective-permute-start.17 = (bf16[64,512]{1,0:T(8,128)(2,1)S(1)}, bf16[64,512]{1,0:T(8,128)(2,1)S(1)}, u32[]{:S(2)}, u32[]{:S(2)}) collective-permute-start(bf16[64,512]{1,0:T(8,128)(2,1)S(1)} %get-tuple-element.30), channel_id=1, source_target_pairs={{0,2},{2,0},{1,3},{3,1},{4,6},{6,4},{5,7},{7,5},{8,10},{10,8},{9,1... | collective-permute-start | bytes 196616 | tf_op jit(solution)/shard_map/ppermute | solution.py:29
  42.5 5.0 %collective-permute-start.15 = (bf16[64,512]{1,0:T(8,128)(2,1)S(1)}, bf16[64,512]{1,0:T(8,128)(2,1)S(1)}, u32[]{:S(2)}, u32[]{:S(2)}) collective-permute-start(bf16[64,512]{1,0:T(8,128)(2,1)S(1)} %get-tuple-element.30), channel_id=1, source_target_pairs={{0,12},{4,0},{8,4},{12,8},{1,13},{5,1},{9,5},{13,9},{2,14},{6,2},{... | collective-permute-start | bytes 196616 | tf_op jit(solution)/shard_map/ppermute | solution.py:29
  43.3 7.3 %collective-permute-start.13 = (bf16[64,512]{1,0:T(8,128)(2,1)S(1)}, bf16[64,512]{1,0:T(8,128)(2,1)S(1)}, u32[]{:S(2)}, u32[]{:S(2)}) collective-permute-start(bf16[64,512]{1,0:T(8,128)(2,1)S(1)} %get-tuple-element.30), channel_id=1, source_target_pairs={{0,8},{4,12},{8,0},{12,4},{1,9},{5,13},{9,1},{13,5},{2,10},{6,14},... | collective-permute-start | bytes 196616 | tf_op jit(solution)/shard_map/ppermute | solution.py:29
  44.0 7.1 %collective-permute-start.11 = (bf16[64,512]{1,0:T(8,128)(2,1)S(1)}, bf16[64,512]{1,0:T(8,128)(2,1)S(1)}, u32[]{:S(2)}, u32[]{:S(2)}) collective-permute-start(bf16[64,512]{1,0:T(8,128)(2,1)S(1)} %get-tuple-element.30), channel_id=1, source_target_pairs={{0,4},{4,8},{8,12},{12,0},{1,5},{5,9},{9,13},{13,1},{2,6},{6,10},{... | collective-permute-start | bytes 196616 | tf_op jit(solution)/shard_map/ppermute | solution.py:29
  46.6 6.0 %collective-permute-start.18 = (bf16[64,512]{1,0:T(8,128)(2,1)S(1)}, bf16[64,512]{1,0:T(8,128)(2,1)S(1)}, u32[]{:S(2)}, u32[]{:S(2)}) collective-permute-start(bf16[64,512]{1,0:T(8,128)(2,1)S(1)} %collective-permute-done.17.refs_9_), channel_id=1, source_target_pairs={{0,1},{1,0},{2,3},{3,2},{4,5},{5,4},{6,7},{7,6},{8,9},{9,8},{10,11... | collective-permute-start | bytes 196616 | tf_op jit(solution)/shard_map/ppermute | solution.py:29
  47.4 5.2 %collective-permute-start.23 = (bf16[64,512]{1,0:T(8,128)(2,1)S(1)}, bf16[64,512]{1,0:T(8,128)(2,1)S(1)}, u32[]{:S(2)}, u32[]{:S(2)}) collective-permute-start(bf16[64,512]{1,0:T(8,128)(2,1)S(1)} %collective-permute-done.15.refs_7_), channel_id=1, source_target_pairs={{0,2},{2,0},{1,3},{3,1},{4,6},{6,4},{5,7},{7,5},{8,10},{10,8},{9,1... | collective-permute-start | bytes 196616 | tf_op jit(solution)/shard_map/ppermute | solution.py:29
  48.1 5.0 %collective-permute-start.16 = (bf16[64,512]{1,0:T(8,128)(2,1)S(1)}, bf16[64,512]{1,0:T(8,128)(2,1)S(1)}, u32[]{:S(2)}, u32[]{:S(2)}) collective-permute-start(bf16[64,512]{1,0:T(8,128)(2,1)S(1)} %collective-permute-done.15.refs_7_), channel_id=1, source_target_pairs={{0,1},{1,0},{2,3},{3,2},{4,5},{5,4},{6,7},{7,6},{8,9},{9,8},{10,11... | collective-permute-start | bytes 196616 | tf_op jit(solution)/shard_map/ppermute | solution.py:29
  50.6 4.3 %collective-permute-start.21 = (bf16[64,512]{1,0:T(8,128)(2,1)S(1)}, bf16[64,512]{1,0:T(8,128)(2,1)S(1)}, u32[]{:S(2)}, u32[]{:S(2)}) collective-permute-start(bf16[64,512]{1,0:T(8,128)(2,1)S(1)} %collective-permute-done.13.refs_5_), channel_id=1, source_target_pairs={{0,2},{2,0},{1,3},{3,1},{4,6},{6,4},{5,7},{7,5},{8,10},{10,8},{9,1... | collective-permute-start | bytes 196616 | tf_op jit(solution)/shard_map/ppermute | solution.py:29
  51.2 4.4 %collective-permute-start.19 = (bf16[64,512]{1,0:T(8,128)(2,1)S(1)}, bf16[64,512]{1,0:T(8,128)(2,1)S(1)}, u32[]{:S(2)}, u32[]{:S(2)}) collective-permute-start(bf16[64,512]{1,0:T(8,128)(2,1)S(1)} %collective-permute-done.11.refs_3_), channel_id=1, source_target_pairs={{0,2},{2,0},{1,3},{3,1},{4,6},{6,4},{5,7},{7,5},{8,10},{10,8},{9,1... | collective-permute-start | bytes 196616 | tf_op jit(solution)/shard_map/ppermute | solution.py:29
  52.6 2.9 %collective-permute-start.14 = (bf16[64,512]{1,0:T(8,128)(2,1)S(1)}, bf16[64,512]{1,0:T(8,128)(2,1)S(1)}, u32[]{:S(2)}, u32[]{:S(2)}) collective-permute-start(bf16[64,512]{1,0:T(8,128)(2,1)S(1)} %collective-permute-done.13.refs_5_), channel_id=1, source_target_pairs={{0,1},{1,0},{2,3},{3,2},{4,5},{5,4},{6,7},{7,6},{8,9},{9,8},{10,11... | collective-permute-start | bytes 196616 | tf_op jit(solution)/shard_map/ppermute | solution.py:29
  52.6 2.9 %collective-permute-start.12 = (bf16[64,512]{1,0:T(8,128)(2,1)S(1)}, bf16[64,512]{1,0:T(8,128)(2,1)S(1)}, u32[]{:S(2)}, u32[]{:S(2)}) collective-permute-start(bf16[64,512]{1,0:T(8,128)(2,1)S(1)} %collective-permute-done.11.refs_3_), channel_id=1, source_target_pairs={{0,1},{1,0},{2,3},{3,2},{4,5},{5,4},{6,7},{7,6},{8,9},{9,8},{10,11... | collective-permute-start | bytes 196616 | tf_op jit(solution)/shard_map/ppermute | solution.py:29
  53.1 2.4 %collective-permute-start.24 = (bf16[64,512]{1,0:T(8,128)(2,1)S(1)}, bf16[64,512]{1,0:T(8,128)(2,1)S(1)}, u32[]{:S(2)}, u32[]{:S(2)}) collective-permute-start(bf16[64,512]{1,0:T(8,128)(2,1)S(1)} %collective-permute-done.23.refs_15_), channel_id=1, source_target_pairs={{0,1},{1,0},{2,3},{3,2},{4,5},{5,4},{6,7},{7,6},{8,9},{9,8},{10,11... | collective-permute-start | bytes 196616 | tf_op jit(solution)/shard_map/ppermute | solution.py:29
  54.9 1.3 %collective-permute-start.22 = (bf16[64,512]{1,0:T(8,128)(2,1)S(1)}, bf16[64,512]{1,0:T(8,128)(2,1)S(1)}, u32[]{:S(2)}, u32[]{:S(2)}) collective-permute-start(bf16[64,512]{1,0:T(8,128)(2,1)S(1)} %collective-permute-done.21.refs_13_), channel_id=1, source_target_pairs={{0,1},{1,0},{2,3},{3,2},{4,5},{5,4},{6,7},{7,6},{8,9},{9,8},{10,11... | collective-permute-start | bytes 196616 | tf_op jit(solution)/shard_map/ppermute | solution.py:29
  55.6 1.3 %collective-permute-start.20 = (bf16[64,512]{1,0:T(8,128)(2,1)S(1)}, bf16[64,512]{1,0:T(8,128)(2,1)S(1)}, u32[]{:S(2)}, u32[]{:S(2)}) collective-permute-start(bf16[64,512]{1,0:T(8,128)(2,1)S(1)} %collective-permute-done.19.refs_11_), channel_id=1, source_target_pairs={{0,1},{1,0},{2,3},{3,2},{4,5},{5,4},{6,7},{7,6},{8,9},{9,8},{10,11... | collective-permute-start | bytes 196616 | tf_op jit(solution)/shard_map/ppermute | solution.py:29

commit v2 on v1

v2 whole, which is shorter than its diff:
```python
import functools

import jax
import jax.numpy as jnp
from jax import lax
from jax.experimental import pallas as pl
from jax.experimental.pallas import tpu as pltpu
from jax.sharding import PartitionSpec as P

epsilon = 1e-06
bf16, f32 = jnp.bfloat16, jnp.float32
VMEM = pl.BlockSpec(memory_space=pltpu.VMEM)
STAY = pl.BlockSpec(memory_space=pl.ANY)
AXES = ("tok", "slot", "hid")


def call(body, outs, *args, name, flops=0, nbytes=0, stay=0, scratch=()):
    return pl.pallas_call(
        body,
        out_shape=[jax.ShapeDtypeStruct(s, d) for s, d in outs],
        in_specs=[VMEM] * (len(args) - stay) + [STAY] * stay,
        out_specs=[VMEM] * len(outs),
        scratch_shapes=list(scratch),
        name=name,
        compiler_params=pltpu.CompilerParams(vmem_limit_bytes=24 * 2**20),
        cost_estimate=pl.CostEstimate(flops=flops, bytes_accessed=nbytes, transcendentals=0),
    )(*args)


def swap(value, axis, step):
    return lax.ppermute(value, axis, [(i, i ^ step) for i in range(lax.axis_size(axis))])


def swap_by_core(value, moves):
    rows, blocks = lax.axis_size("tok"), lax.axis_size("slot")
    pairs = []
    for row in range(rows):
        for block in range(blocks):
            for core, move in enumerate(moves):
                if move is None:
                    continue
                axis, step = move
                to_row = row ^ step if axis == "tok" else row
                to_block = block ^ step if axis == "slot" else block
                pairs.append(((row * blocks + block) * 2 + core, (to_row * blocks + to_block) * 2 + core))
    return lax.ppermute(value, AXES, pairs)


def halves(half):
    core = lax.axis_index("hid")
    mine = pl.ds(pl.multiple_of(core * half, half), half)
    other = pl.ds(pl.multiple_of((1 - core) * half, half), half)
    return mine, other


def total_at(slots, half, at):
    return slice(slots + 8 * (at // half), slots + 8 * (at // half) + 8)


def weigh(tok_ref, key_ref, key_scale):
    width = tok_ref.shape[1]
    tok = tok_ref[...].astype(f32)
    tok_scale = lax.rsqrt(jnp.sum(tok * tok, axis=1, keepdims=True) / width + epsilon)
    logits = jnp.dot(tok_ref[...], key_ref[...], preferred_element_type=f32)
    return jnp.exp(logits * (tok_scale * (4.0 / width)) * key_scale)


def collect(tok_ref, weights, half):
    low = weights.astype(bf16)
    mine, other = halves(half)
    dims = (((0,), (0,)), ((), ()))
    keep = lax.dot_general(low, tok_ref[:, mine], dims, preferred_element_type=f32)
    send = lax.dot_general(low, tok_ref[:, other], dims, preferred_element_type=f32)
    total = jnp.broadcast_to(jnp.sum(weights, axis=0, keepdims=True), (8, weights.shape[1]))
    return low, keep, send, total


def dispatch_own_body(half, tok_ref, key_ref, in_ref, out_ref, low_ref, keep_ref, send_ref, scale_ref, keys_ref, in_here, out_here, sems):
    copies = [pltpu.make_async_copy(in_ref, in_here, sems.at[0]), pltpu.make_async_copy(out_ref, out_here, sems.at[1])]
    for copy in copies:
        copy.start()
    width, slots = key_ref.shape
    key = key_ref[...].astype(f32)
    key_scale = lax.rsqrt(jnp.sum(key * key, axis=0, keepdims=True) / width + epsilon)
    scale_ref[...] = jnp.broadcast_to(key_scale, (8, slots))
    keys_ref[...] = key_ref[...]
    low, keep, send, total = collect(tok_ref, weigh(tok_ref, key_ref, key_scale), half)
    low_ref[...] = low
    keep_ref[0:slots, :] = keep
    send_ref[0:slots, :] = send
    for at in range(0, slots, half):
        wide = min(half, slots - at)
        for ref in (keep_ref, send_ref):
            ref[total_at(slots, half, at), 0:wide] = total[:, at : at + wide]
    for copy in copies:
        copy.wait()


def dispatch_other_body(half, tok_ref, key_ref, scale_ref, keep_in, send_in, low_ref, keep_ref, send_ref):
    slots = key_ref.shape[1]
    low, keep, send, total = collect(tok_ref, weigh(tok_ref, key_ref, scale_ref[0:1, :]), half)
    low_ref[...] = low
    keep_ref[0:slots, :] = keep + keep_in[0:slots, :]
    send_ref[0:slots, :] = send + send_in[0:slots, :]
    for at in range(0, slots, half):
        wide = min(half, slots - at)
        place = total_at(slots, half, at)
        for ref, old in ((keep_ref, keep_in), (send_ref, send_in)):
            ref[place, 0:wide] = total[:, at : at + wide] + old[place, 0:wide]


def total_rows(slots, half):
    return 8 * pl.cdiv(3 * pl.cdiv(slots, half), 8)


def share_body(owned, slots, keep_ref, recv_ref, mine_ref, total_ref, *send_refs):
    half = keep_ref.shape[1]
    row = lax.axis_index("tok")
    terms = []
    for at in range(0, slots, half):
        wide = min(half, slots - at)
        place = total_at(slots, half, at)
        total = keep_ref[place, 0:wide] + recv_ref[place, 0:wide]
        total_ref[:, at : at + wide] = total
        total = total[0:1, :]
        for _ in range(3):
            term = total.astype(bf16)
            terms.append((wide, term))
            total = total - term.astype(f32)
    for step in range(slots // owned):
        start = pl.ds(pl.multiple_of((row ^ step) * owned, owned), owned)
        piece = keep_ref[start, :] + recv_ref[start, :]
        if step == 0:
            mine_ref[...] = piece
            continue
        ref = send_refs[step - 1]
        ref[0:owned, :] = piece.astype(bf16)
        ref[owned:, :] = jnp.zeros((ref.shape[0] - owned, half), bf16)
        for index, (wide, term) in enumerate(terms):
            ref[owned + index : owned + index + 1, 0:wide] = term


def inputs_body(mine_ref, total_ref, *refs):
    piece_refs, out_ref = refs[:-1], refs[-1]
    owned, half = mine_ref.shape
    slots = total_ref.shape[1]
    numer = mine_ref[...]
    denom = jnp.zeros((owned, 1), f32)
    for ref in piece_refs:
        numer = numer + ref[0:owned, :].astype(f32)
    for at in range(0, slots, half):
        wide = min(half, slots - at)
        total = total_ref[0:1, at : at + wide]
        first = owned + 3 * (at // half)
        for ref in piece_refs:
            for index in range(first, first + 3):
                total = total + ref[index : index + 1, 0:wide].astype(f32)
        lane = lax.broadcasted_iota(jnp.int32, (owned, wide), 1) + at
        wanted = lax.broadcasted_iota(jnp.int32, (owned, wide), 0) + lax.axis_index("tok") * owned
        total = jnp.where(lane == wanted, jnp.broadcast_to(total, (owned, wide)), 0.0)
        denom = denom + jnp.sum(total, axis=1, keepdims=True)
    out_ref[...] = (numer / denom).astype(bf16)


def expert_body(mine_ref, other_ref, in_ref, out_w_ref, out_ref):
    mine, other = halves(mine_ref.shape[1])
    value = jnp.dot(mine_ref[...], in_ref[mine, :], preferred_element_type=f32)
    value = value + jnp.dot(other_ref[...], in_ref[other, :], preferred_element_type=f32)
    hidden = jax.nn.gelu(value, approximate=True).astype(bf16)
    out_ref[...] = jnp.dot(hidden, out_w_ref[...], preferred_element_type=f32)


def outputs_body(part_ref, recv_ref, full_ref):
    full_ref[...] = (part_ref[...] + recv_ref[...]).astype(bf16)


def combine_body(blocks, rows, slots, plan, *refs):
    low_refs, full_ref, pieces = refs[:blocks], refs[blocks], refs[blocks + 1 : -2]
    out_ref, all_ref = refs[-2], refs[-1]
    owned = full_ref.shape[0]
    core = lax.axis_index("hid")
    row = lax.axis_index("tok")

    def put(step, ref):
        block, expert = step
        start = block * slots + (row ^ expert) * owned
        all_ref[pl.ds(pl.multiple_of(start, owned), owned), :] = ref[...]

    put((0, 0), full_ref)
    for index, steps in enumerate(plan):
        for turn in range(2):
            ref = pieces[2 * index + turn]
            for holder in range(2):
                step = steps[holder ^ turn]
                if step is not None:
                    pl.when(core == holder)(functools.partial(put, step, ref))
    numer = None
    denom = None
    for block in range(blocks):
        low = low_refs[block][...]
        part = jnp.dot(low, all_ref[block * slots : (block + 1) * slots, :], preferred_element_type=f32)
        total = jnp.sum(low.astype(f32), axis=1, keepdims=True)
        numer = part if numer is None else numer + part
        denom = total if denom is None else denom + total
    out_ref[...] = numer / denom


def local(tokens, slot_keys, w_in, w_out):
    count, width = tokens.shape
    slots = slot_keys.shape[1]
    hidden = w_in.shape[3]
    rows, blocks = lax.axis_size("tok"), lax.axis_size("slot")
    owned = slots // rows
    half = width // 2
    extra = 8 * pl.cdiv(slots, half)
    part = ((slots + extra, half), f32)
    mac = 4 * count * width * slots

    arrived = [swap(tokens, "slot", step) for step in range(1, blocks)]
    low, keep, send, scale, keys, in_here, out_here = call(
        functools.partial(dispatch_own_body, half),
        [((count, slots), bf16), part, part, ((8, slots), f32), ((width, slots), bf16), ((width, hidden), bf16), ((hidden, width), bf16)],
        tokens, slot_keys, w_in[0, 0], w_out[0, 0],
        name="dispatch_own", flops=mac, nbytes=8 * hidden * width, stay=2, scratch=[pltpu.SemaphoreType.DMA((2,))],
    )
    lows = [low]
    for step in range(1, blocks):
        low, keep, send = call(
            functools.partial(dispatch_other_body, half),
            [((count, slots), bf16), part, part],
            arrived[step - 1], keys, scale, keep, send, name="dispatch_other", flops=mac, nbytes=2 * count * width,
        )
        lows.append(low)
    recv = swap(send, "hid", 1)
    mine, total, *sends = call(
        functools.partial(share_body, owned, slots),
        [((owned, half), f32), ((8, slots), f32)] + [((owned + total_rows(slots, half), half), bf16)] * (rows - 1),
        keep, recv, name="share", nbytes=12 * slots * half,
    )
    pieces = [swap(sends[step - 1], "tok", step) for step in range(1, rows)]
    lows = lows[:1] + [swap(lows[step], "slot", step) for step in range(1, blocks)]
    pieces, lows = lax.optimization_barrier((pieces, lows))
    (inputs,) = call(
        inputs_body, [((owned, half), bf16)],
        mine, total, *pieces, name="slot_inputs", nbytes=8 * owned * width,
    )
    inputs_other = swap(inputs, "hid", 1)
    (outputs_part,) = call(
        expert_body, [((owned, width), f32)],
        inputs, inputs_other, in_here, out_here,
        name="expert", flops=4 * owned * width * hidden, nbytes=4 * width * hidden,
    )
    outputs_recv = swap(outputs_part, "hid", 1)
    (full,) = call(outputs_body, [((owned, width), bf16)], outputs_part, outputs_recv, name="slot_outputs", nbytes=8 * owned * width)

    moves = [("tok", step) for step in range(1, rows)] + [("slot", step) for step in range(1, blocks)]
    moves += [None] * (len(moves) % 2)
    flights, plan = [], []
    turns = [moves[at : at + 2] for at in range(0, len(moves), 2)][::-1]
    for turn in turns:
        got = swap_by_core(full, turn)
        flights.append(got)
        plan.append([move and ((0, move[1]) if move[0] == "tok" else (move[1], 0)) for move in turn])
    for at, turn in list(enumerate(turns)):
        for step in range(1, blocks):
            along = [("slot", step) if move and move[0] == "tok" else None for move in turn]
            if any(along):
                flights.append(swap_by_core(flights[at], along))
                plan.append([move and (step, turn[core][1]) for core, move in enumerate(along)])
    pairs = []
    for got, steps in zip(flights, plan):
        pairs += [got, swap(got, "hid", 1)]
    return pl.pallas_call(
        functools.partial(combine_body, blocks, rows, slots, plan),
        out_shape=jax.ShapeDtypeStruct((count, width), f32),
        in_specs=[VMEM] * (blocks + 1 + len(pairs)),
        out_specs=VMEM,
        scratch_shapes=[pltpu.VMEM((blocks * slots, width), bf16)],
        name="combine",
        compiler_params=pltpu.CompilerParams(vmem_limit_bytes=40 * 2**20),
    )(*lows, full, *pairs)


def solution(mesh):
    in_specs = (
        P(("groups", "tok", "slot", "hid"), None),
        P("groups", "slot"),
        P(("groups", "slot"), "tok", None, "hid"),
        P(("groups", "slot"), "tok", "hid", None),
    )
    out_specs = P(("groups", "tok", "slot", "hid"), None)
    return jax.shard_map(local, mesh=mesh, in_specs=in_specs, out_specs=out_specs, check_vma=False)
```

time: 58.6 us -> 52.4 us (0.89)
  waiting for transfers between devices: 26.2 us -> 20.9 us
  starting transfers between devices: 21.7 us -> 19 us
  local copies, waits for them, and re-layouts: 5.32 us -> 6.46 us
  Pallas kernels: 4.99 us -> 5.67 us
    ppermute x25 -> x16, waiting for transfers between devices: 26.2 us -> 20.9 us  [the longest x12 14.5 us: swap(): lax.ppermute(value, axis, [(i, i ^ step) for i in range(lax.axis_size(axi...]
    ppermute x25 -> x16, starting transfers between devices: 21.7 us -> 19 us  [the longest x12 10.2 us: swap(): lax.ppermute(value, axis, [(i, i ^ step) for i in range(lax.axis_size(axi...]
    unnamed x10 -> x8, local copies, waits for them, and re-layouts: 5.32 us -> 6.46 us
    pallas_call x6, Pallas kernels: 3.5 us -> 4.14 us  [call(): pl.pallas_call(body, out_shape=[jax.ShapeDtypeStruct(s, d) for s, d in ou...]
  transfers between devices with their start and end apart: 25 -> 16, of which waited for: 12 -> 9; matrix products, arithmetic and copies ran while one was open for 0% -> 0% of each run, Pallas kernels for 2% -> 3%
where the time goes in v2:
time: 52.4 us; the launch traced here: 52.1 us
  waiting for transfers between devices  20.9 us (40%)
  starting transfers between devices  19 us (36%)
  local copies, waits for them, and re-layouts  6.46 us (12%)
  Pallas kernels  5.67 us (11%)
    ppermute x12, waiting for transfers between devices, swap(): lax.ppermute(value, axis, [(i, i ^ step) for i in range(lax.axis_size(axi...  14.5 us
    ppermute x12, starting transfers between devices, swap(): lax.ppermute(value, axis, [(i, i ^ step) for i in range(lax.axis_size(axi...  10.2 us
    ppermute x4, starting transfers between devices, swap_by_core(): return lax.ppermute(value, AXES, pairs)  8.78 us
    unnamed x8, local copies, waits for them, and re-layouts  6.46 us
    ppermute x4, waiting for transfers between devices, swap_by_core(): return lax.ppermute(value, AXES, pairs)  6.31 us
    pallas_call x6, Pallas kernels, call(): pl.pallas_call(body, out_shape=[jax.ShapeDtypeStruct(s, d) for s, d in ou...  4.14 us
    pallas_call x1, Pallas kernels, local(): pl.pallas_call(functools.partial(combine_body, blocks, rows, slots, plan)...  1.53 us
  transfers between devices with their start and end apart: 16, of which 9 were waited for; matrix products, arithmetic and copies ran while one was open for 0% of the time, Pallas kernels for 3%

profile of v2, /device:TPU:0, one launch (start us, length us, event | category | flops | bytes accessed | tf_op | source)
XLA Modules:
  0.0 52.1 jit_solution(13281335976569835470)
XLA Ops:
  0.0 2.9 %collective-permute-start = (bf16[256,1024]{1,0:T(8,128)(2,1)}, bf16[256,1024]{1,0:T(8,128)(2,1)S(1)}, u32[]{:S(2)}, u32[]{:S(2)}) collective-permute-start(bf16[256,1024]{1,0:T(8,128)(2,1)} %tok_ref.1), channel_id=1, source_target_pairs={{0,2},{2,0},{1,3},{3,1},{4,6},{6,4},{5,7},{7,5},{8,10},{10,8},{9,1... | collective-permute-start | bytes 1572872 | tf_op jit(solution)/shard_map/ppermute | solution.py:31
  2.9 0.0 copy-start
  2.9 2.2 %copy-done = bf16[1,1,1024,2048]{3,2,1,0:T(8,128)(2,1)S(1)} copy-done((bf16[1,1,1024,2048]{3,2,1,0:T(8,128)(2,1)S(1)}, bf16[1,1,1024,2048]{3,2,1,0:T(8,128)(2,1)}, u32[]{:S(2)}) %copy-start) | copy-done | bytes 4194328
  5.1 0.0 copy-start.1
  5.1 2.2 %copy-done.1 = bf16[1,1,2048,1024]{3,2,1,0:T(8,128)(2,1)S(1)} copy-done((bf16[1,1,2048,1024]{3,2,1,0:T(8,128)(2,1)S(1)}, bf16[1,1,2048,1024]{3,2,1,0:T(8,128)(2,1)}, u32[]{:S(2)}) %copy-start.1) | copy-done | bytes 4194328
  7.3 0.0 copy-start.2
  7.3 1.0 %copy-done.2 = bf16[1024,256]{1,0:T(8,128)(2,1)S(1)} copy-done((bf16[1024,256]{1,0:T(8,128)(2,1)S(1)}, bf16[1024,256]{1,0:T(8,128)(2,1)}, u32[]{:S(2)}) %copy-start.2) | copy-done | bytes 524312
  8.4 0.0 copy-start.3
  8.4 1.0 %copy-done.3 = bf16[256,1024]{1,0:T(8,128)(2,1)S(1)} copy-done((bf16[256,1024]{1,0:T(8,128)(2,1)S(1)}, bf16[256,1024]{1,0:T(8,128)(2,1)}, u32[]{:S(2)}) %copy-start.3) | copy-done | bytes 524312
  9.4 1.4 %dispatch_own.1 = (bf16[256,256]{1,0:T(8,128)(2,1)S(1)}, f32[264,512]{1,0:T(8,128)S(1)}, f32[264,512]{1,0:T(8,128)S(1)}, f32[8,256]{1,0:T(8,128)S(1)}, bf16[1024...) custom-call(bf16[256,1024]{1,0:T(8,128)(2,1)S(1)} %copy-done.3, ...), custom_call_target="tpu_custom_call" | custom-call | flops 268435456 | bytes 16777216 | tf_op jit(solution)/shard_map/dispatch_own/pallas_call | solution.py:18
  10.9 4.2 %collective-permute-done.tok_ref = bf16[256,1024]{1,0:T(8,128)(2,1)S(1)} collective-permute-done((bf16[256,1024]{1,0:T(8,128)(2,1)}, bf16[256,1024]{1,0:T(8,128)(2,1)S(1)}, u32[]{:S(2)}, u32[]{:S(2)}) %collective-permute-start) | collective-permute-done | bytes 524320 | tf_op jit(solution)/shard_map/ppermute | solution.py:31
  15.1 0.9 %dispatch_other.1 = (bf16[256,256]{1,0:T(8,128)(2,1)S(1)}, f32[264,512]{1,0:T(8,128)S(1)}, f32[264,512]{1,0:T(8,128)S(1)}) custom-call(bf16[256,1024]{1,0:T(8,128)(2,1)S(1)} %collective-permute-done.tok_ref, bf16[1024,256]{1,0:T(8,128)(2,1)S(1)} %get-tuple-element.25.key_ref, f32[8,256]{1,0:T(8,128)S(1)} %get-tuple-element.26.scale_ref, ...), custom_call_target="tpu_custom_call" | custom-call | flops 268435456 | bytes 524288 | tf_op jit(solution)/shard_map/dispatch_other/pallas_call | solution.py:18
  15.9 0.1 collective-permute-start.1
  16.0 1.8 %collective-permute-start.5 = (bf16[256,256]{1,0:T(8,128)(2,1)S(1)}, bf16[256,256]{1,0:T(8,128)(2,1)S(1)}, u32[]{:S(2)}, u32[]{:S(2)}) collective-permute-start(bf16[256,256]{1,0:T(8,128)(2,1)S(1)} %get-tuple-element.35), channel_id=1, source_target_pairs={{0,2},{2,0},{1,3},{3,1},{4,6},{6,4},{5,7},{7,5},{8,10},{10,8},{9,1... | collective-permute-start | bytes 393224 | tf_op jit(solution)/shard_map/ppermute | solution.py:31
  17.8 0.1 collective-permute-done.1.recv_ref
  17.9 0.1 share.1
  18.0 1.9 %collective-permute-start.2 = (bf16[72,512]{1,0:T(8,128)(2,1)S(1)}, bf16[72,512]{1,0:T(8,128)(2,1)S(1)}, u32[]{:S(2)}, u32[]{:S(2)}) collective-permute-start(bf16[72,512]{1,0:T(8,128)(2,1)S(1)} %get-tuple-element.31), channel_id=1, source_target_pairs={{0,4},{4,0},{8,12},{12,8},{1,5},{5,1},{9,13},{13,9},{2,6},{6,2},{1... | collective-permute-start | bytes 221192 | tf_op jit(solution)/shard_map/ppermute | solution.py:31
  19.9 2.6 %collective-permute-start.3 = (bf16[72,512]{1,0:T(8,128)(2,1)S(1)}, bf16[72,512]{1,0:T(8,128)(2,1)S(1)}, u32[]{:S(2)}, u32[]{:S(2)}) collective-permute-start(bf16[72,512]{1,0:T(8,128)(2,1)S(1)} %get-tuple-element.32), channel_id=1, source_target_pairs={{0,8},{4,12},{8,0},{12,4},{1,9},{5,13},{9,1},{13,5},{2,10},{6,14},... | collective-permute-start | bytes 221192 | tf_op jit(solution)/shard_map/ppermute | solution.py:31
  22.5 0.0 collective-permute-start.4
  22.5 0.0 collective-permute-done.5.refs_1_
  22.5 0.0 collective-permute-done.2.refs_0_
  22.5 6.3 %collective-permute-done.3.refs_1_ = bf16[72,512]{1,0:T(8,128)(2,1)S(1)} collective-permute-done((bf16[72,512]{1,0:T(8,128)(2,1)S(1)}, bf16[72,512]{1,0:T(8,128)(2,1)S(1)}, u32[]{:S(2)}, u32[]{:S(2)}) %collective-permute-start.3) | collective-permute-done | bytes 73760 | tf_op jit(solution)/shard_map/ppermute | solution.py:31
  28.8 0.0 collective-permute-done.4.refs_2_
  28.8 0.1 slot_inputs.1.mine_ref
  28.9 0.1 collective-permute-start.6
  29.0 1.2 %collective-permute-done.6.other_ref = bf16[64,512]{1,0:T(8,128)(2,1)S(1)} collective-permute-done((bf16[64,512]{1,0:T(8,128)(2,1)S(1)}, bf16[64,512]{1,0:T(8,128)(2,1)S(1)}, u32[]{:S(2)}, u32[]{:S(2)}) %collective-permute-start.6) | collective-permute-done | bytes 65568 | tf_op jit(solution)/shard_map/ppermute | solution.py:31
  30.2 1.6 %expert.1.part_ref = f32[64,1024]{1,0:T(8,128)S(1)} custom-call(bf16[64,512]{1,0:T(8,128)(2,1)S(1)} %slot_inputs.1.mine_ref, bf16[64,512]{1,0:T(8,128)(2,1)S(1)} %collective-permute-done.6.other_ref, bf16[1024,2048]{1,0:T(8,128)(2,1)S(1)} %get-tuple-element.43.in_ref, bf16[2048,1024]{1,0:T(8,128)(2,1)S(1)} %get-tuple-element.44.out_w_ref), custom_call_target="tpu_custom_call" | custom-call | flops 536870912 | bytes 8388608 | tf_op jit(solution)/shard_map/expert/pallas_call | solution.py:18
  31.8 0.2 collective-permute-start.7
  32.1 1.4 %collective-permute-done.7.recv_ref = f32[64,1024]{1,0:T(8,128)S(1)} collective-permute-done((f32[64,1024]{1,0:T(8,128)S(1)}, f32[64,1024]{1,0:T(8,128)S(1)}, u32[]{:S(2)}, u32[]{:S(2)}) %collective-permute-start.7) | collective-permute-done | bytes 262176 | tf_op jit(solution)/shard_map/ppermute | solution.py:31
  33.5 1.5 %collective-permute-start.10 = (bf16[64,1024]{1,0:T(8,128)(2,1)S(1)}, bf16[64,1024]{1,0:T(8,128)(2,1)S(1)}, u32[]{:S(2)}, u32[]{:S(2)}) collective-permute-start(bf16[64,1024]{1,0:T(8,128)(2,1)S(1)} %slot_outputs.1.refs_2_), channel_id=1, source_target_pairs={{0,4},{1,9},{2,6},{3,11},{4,0},{5,13},{6,2},{7,15},{8,12},{9,1},{1... | collective-permute-start | bytes 393224 | tf_op jit(solution)/shard_map/ppermute | solution.py:46
  35.0 2.4 %collective-permute-start.8 = (bf16[64,1024]{1,0:T(8,128)(2,1)S(1)}, bf16[64,1024]{1,0:T(8,128)(2,1)S(1)}, u32[]{:S(2)}, u32[]{:S(2)}) collective-permute-start(bf16[64,1024]{1,0:T(8,128)(2,1)S(1)} %slot_outputs.1.refs_2_), channel_id=1, source_target_pairs={{0,12},{1,3},{2,14},{3,1},{4,8},{5,7},{6,10},{7,5},{8,4},{9,11},{1... | collective-permute-start | bytes 393224 | tf_op jit(solution)/shard_map/ppermute | solution.py:46
  37.4 2.3 %collective-permute-done.10.refs_5_ = bf16[64,1024]{1,0:T(8,128)(2,1)S(1)} collective-permute-done((bf16[64,1024]{1,0:T(8,128)(2,1)S(1)}, bf16[64,1024]{1,0:T(8,128)(2,1)S(1)}, u32[]{:S(2)}, u32[]{:S(2)}) %collective-permute-start.10) | collective-permute-done | bytes 131104 | tf_op jit(solution)/shard_map/ppermute | solution.py:46
  39.6 1.5 %collective-permute-start.14 = (bf16[64,1024]{1,0:T(8,128)(2,1)S(1)}, bf16[64,1024]{1,0:T(8,128)(2,1)S(1)}, u32[]{:S(2)}, u32[]{:S(2)}) collective-permute-start(bf16[64,1024]{1,0:T(8,128)(2,1)S(1)} %collective-permute-done.10.refs_5_), channel_id=1, source_target_pairs={{0,2},{1,3},{2,0},{3,1},{4,6},{5,7},{6,4},{7,5},{8,10},{9,11},{10,... | collective-permute-start | bytes 393224 | tf_op jit(solution)/shard_map/ppermute | solution.py:46
  41.1 1.3 %collective-permute-done.8.refs_3_ = bf16[64,1024]{1,0:T(8,128)(2,1)S(1)} collective-permute-done((bf16[64,1024]{1,0:T(8,128)(2,1)S(1)}, bf16[64,1024]{1,0:T(8,128)(2,1)S(1)}, u32[]{:S(2)}, u32[]{:S(2)}) %collective-permute-start.8) | collective-permute-done | bytes 131104 | tf_op jit(solution)/shard_map/ppermute | solution.py:46
  42.4 3.4 %collective-permute-start.12 = (bf16[64,1024]{1,0:T(8,128)(2,1)S(1)}, bf16[64,1024]{1,0:T(8,128)(2,1)S(1)}, u32[]{:S(2)}, u32[]{:S(2)}) collective-permute-start(bf16[64,1024]{1,0:T(8,128)(2,1)S(1)} %collective-permute-done.8.refs_3_), channel_id=1, source_target_pairs={{0,2},{2,0},{4,6},{6,4},{8,10},{10,8},{12,14},{14,12},{16,18},{18,... | collective-permute-start | bytes 393224 | tf_op jit(solution)/shard_map/ppermute | solution.py:46
  45.8 0.1 collective-permute-start.11
  45.9 0.5 collective-permute-start.9
  46.3 0.0 collective-permute-done.14.refs_9_
  46.4 0.1 collective-permute-start.15
  46.4 2.8 %collective-permute-done.12.refs_7_ = bf16[64,1024]{1,0:T(8,128)(2,1)S(1)} collective-permute-done((bf16[64,1024]{1,0:T(8,128)(2,1)S(1)}, bf16[64,1024]{1,0:T(8,128)(2,1)S(1)}, u32[]{:S(2)}, u32[]{:S(2)}) %collective-permute-start.12) | collective-permute-done | bytes 131104 | tf_op jit(solution)/shard_map/ppermute | solution.py:46
  49.2 0.0 collective-permute-start.13
  49.2 0.0 collective-permute-done.11.refs_6_
  49.2 0.0 collective-permute-done.9.refs_4_
  49.2 0.0 collective-permute-done.15.refs_10_
  49.2 1.3 %collective-permute-done.13.refs_8_ = bf16[64,1024]{1,0:T(8,128)(2,1)S(1)} collective-permute-done((bf16[64,1024]{1,0:T(8,128)(2,1)S(1)}, bf16[64,1024]{1,0:T(8,128)(2,1)S(1)}, u32[]{:S(2)}, u32[]{:S(2)}) %collective-permute-start.13) | collective-permute-done | bytes 131104 | tf_op jit(solution)/shard_map/ppermute | solution.py:31
  50.6 1.5 %combine.1 = f32[256,1024]{1,0:T(8,128)} custom-call(bf16[256,256]{1,0:T(8,128)(2,1)S(1)} %get-tuple-element.36.refs_0_, bf16[256,256]{1,0:T(8,128)(2,1)S(1)} %collective-permute-done.5.refs_1_, bf16[64,1024]{1,0:T(8,128)(2,1)S(1)} %slot_outputs.1.refs_2_, bf16[64,1024]{1,0:T(8,128)(2,1)S(1)} %collective-permute-done.8.refs_3_, ...), custom_call_target="tpu_custom_call" | custom-call | tf_op jit(solution)/shard_map/combine/pallas_call | solution.py:273
  (1 shorter events, 0.0 us)
Async XLA Ops:
  0.0 15.1 %collective-permute-start = (bf16[256,1024]{1,0:T(8,128)(2,1)}, bf16[256,1024]{1,0:T(8,128)(2,1)S(1)}, u32[]{:S(2)}, u32[]{:S(2)}) collective-permute-start(bf16[256,1024]{1,0:T(8,128)(2,1)} %tok_ref.1), channel_id=1, source_target_pairs={{0,2},{2,0},{1,3},{3,1},{4,6},{6,4},{5,7},{7,5},{8,10},{10,8},{9,1... | collective-permute-start | bytes 1572872 | tf_op jit(solution)/shard_map/ppermute | solution.py:31
  2.9 2.2 %copy-start = (bf16[1,1,1024,2048]{3,2,1,0:T(8,128)(2,1)S(1)}, bf16[1,1,1024,2048]{3,2,1,0:T(8,128)(2,1)}, u32[]{:S(2)}) copy-start(bf16[1,1,1024,2048]{3,2,1,0:T(8,128)(2,1)} %param.6) | copy-start | bytes 12582916
  5.1 2.2 %copy-start.1 = (bf16[1,1,2048,1024]{3,2,1,0:T(8,128)(2,1)S(1)}, bf16[1,1,2048,1024]{3,2,1,0:T(8,128)(2,1)}, u32[]{:S(2)}) copy-start(bf16[1,1,2048,1024]{3,2,1,0:T(8,128)(2,1)} %param.7) | copy-start | bytes 12582916
  7.3 1.0 %copy-start.2 = (bf16[1024,256]{1,0:T(8,128)(2,1)S(1)}, bf16[1024,256]{1,0:T(8,128)(2,1)}, u32[]{:S(2)}) copy-start(bf16[1024,256]{1,0:T(8,128)(2,1)} %key_ref.1) | copy-start | bytes 1572868
  8.4 1.0 %copy-start.3 = (bf16[256,1024]{1,0:T(8,128)(2,1)S(1)}, bf16[256,1024]{1,0:T(8,128)(2,1)}, u32[]{:S(2)}) copy-start(bf16[256,1024]{1,0:T(8,128)(2,1)} %tok_ref.1) | copy-start | bytes 1572868
  15.9 2.0 %collective-permute-start.1 = (f32[264,512]{1,0:T(8,128)S(1)}, f32[264,512]{1,0:T(8,128)S(1)}, u32[]{:S(2)}, u32[]{:S(2)}) collective-permute-start(f32[264,512]{1,0:T(8,128)S(1)} %get-tuple-element.30), channel_id=1, source_target_pairs={{0,1},{1,0},{2,3},{3,2},{4,5},{5,4},{6,7},{7,6},{8,9},{9,8},{10,11... | collective-permute-start | bytes 1622024 | tf_op jit(solution)/shard_map/ppermute | solution.py:31
  16.0 6.5 %collective-permute-start.5 = (bf16[256,256]{1,0:T(8,128)(2,1)S(1)}, bf16[256,256]{1,0:T(8,128)(2,1)S(1)}, u32[]{:S(2)}, u32[]{:S(2)}) collective-permute-start(bf16[256,256]{1,0:T(8,128)(2,1)S(1)} %get-tuple-element.35), channel_id=1, source_target_pairs={{0,2},{2,0},{1,3},{3,1},{4,6},{6,4},{5,7},{7,5},{8,10},{10,8},{9,1... | collective-permute-start | bytes 393224 | tf_op jit(solution)/shard_map/ppermute | solution.py:31
  18.0 4.5 %collective-permute-start.2 = (bf16[72,512]{1,0:T(8,128)(2,1)S(1)}, bf16[72,512]{1,0:T(8,128)(2,1)S(1)}, u32[]{:S(2)}, u32[]{:S(2)}) collective-permute-start(bf16[72,512]{1,0:T(8,128)(2,1)S(1)} %get-tuple-element.31), channel_id=1, source_target_pairs={{0,4},{4,0},{8,12},{12,8},{1,5},{5,1},{9,13},{13,9},{2,6},{6,2},{1... | collective-permute-start | bytes 221192 | tf_op jit(solution)/shard_map/ppermute | solution.py:31
  19.9 8.9 %collective-permute-start.3 = (bf16[72,512]{1,0:T(8,128)(2,1)S(1)}, bf16[72,512]{1,0:T(8,128)(2,1)S(1)}, u32[]{:S(2)}, u32[]{:S(2)}) collective-permute-start(bf16[72,512]{1,0:T(8,128)(2,1)S(1)} %get-tuple-element.32), channel_id=1, source_target_pairs={{0,8},{4,12},{8,0},{12,4},{1,9},{5,13},{9,1},{13,5},{2,10},{6,14},... | collective-permute-start | bytes 221192 | tf_op jit(solution)/shard_map/ppermute | solution.py:31
  22.5 6.3 %collective-permute-start.4 = (bf16[72,512]{1,0:T(8,128)(2,1)S(1)}, bf16[72,512]{1,0:T(8,128)(2,1)S(1)}, u32[]{:S(2)}, u32[]{:S(2)}) collective-permute-start(bf16[72,512]{1,0:T(8,128)(2,1)S(1)} %get-tuple-element.33), channel_id=1, source_target_pairs={{0,12},{4,8},{8,4},{12,0},{1,13},{5,9},{9,5},{13,1},{2,14},{6,10},... | collective-permute-start | bytes 221192 | tf_op jit(solution)/shard_map/ppermute | solution.py:31
  28.9 1.3 %collective-permute-start.6 = (bf16[64,512]{1,0:T(8,128)(2,1)S(1)}, bf16[64,512]{1,0:T(8,128)(2,1)S(1)}, u32[]{:S(2)}, u32[]{:S(2)}) collective-permute-start(bf16[64,512]{1,0:T(8,128)(2,1)S(1)} %slot_inputs.1.mine_ref), channel_id=1, source_target_pairs={{0,1},{1,0},{2,3},{3,2},{4,5},{5,4},{6,7},{7,6},{8,9},{9,8},{10,11... | collective-permute-start | bytes 196616 | tf_op jit(solution)/shard_map/ppermute | solution.py:31
  31.8 1.6 %collective-permute-start.7 = (f32[64,1024]{1,0:T(8,128)S(1)}, f32[64,1024]{1,0:T(8,128)S(1)}, u32[]{:S(2)}, u32[]{:S(2)}) collective-permute-start(f32[64,1024]{1,0:T(8,128)S(1)} %expert.1.part_ref), channel_id=1, source_target_pairs={{0,1},{1,0},{2,3},{3,2},{4,5},{5,4},{6,7},{7,6},{8,9},{9,8},{10,11... | collective-permute-start | bytes 786440 | tf_op jit(solution)/shard_map/ppermute | solution.py:31
  33.5 6.2 %collective-permute-start.10 = (bf16[64,1024]{1,0:T(8,128)(2,1)S(1)}, bf16[64,1024]{1,0:T(8,128)(2,1)S(1)}, u32[]{:S(2)}, u32[]{:S(2)}) collective-permute-start(bf16[64,1024]{1,0:T(8,128)(2,1)S(1)} %slot_outputs.1.refs_2_), channel_id=1, source_target_pairs={{0,4},{1,9},{2,6},{3,11},{4,0},{5,13},{6,2},{7,15},{8,12},{9,1},{1... | collective-permute-start | bytes 393224 | tf_op jit(solution)/shard_map/ppermute | solution.py:46
  35.0 7.4 %collective-permute-start.8 = (bf16[64,1024]{1,0:T(8,128)(2,1)S(1)}, bf16[64,1024]{1,0:T(8,128)(2,1)S(1)}, u32[]{:S(2)}, u32[]{:S(2)}) collective-permute-start(bf16[64,1024]{1,0:T(8,128)(2,1)S(1)} %slot_outputs.1.refs_2_), channel_id=1, source_target_pairs={{0,12},{1,3},{2,14},{3,1},{4,8},{5,7},{6,10},{7,5},{8,4},{9,11},{1... | collective-permute-start | bytes 393224 | tf_op jit(solution)/shard_map/ppermute | solution.py:46
  39.6 6.7 %collective-permute-start.14 = (bf16[64,1024]{1,0:T(8,128)(2,1)S(1)}, bf16[64,1024]{1,0:T(8,128)(2,1)S(1)}, u32[]{:S(2)}, u32[]{:S(2)}) collective-permute-start(bf16[64,1024]{1,0:T(8,128)(2,1)S(1)} %collective-permute-done.10.refs_5_), channel_id=1, source_target_pairs={{0,2},{1,3},{2,0},{3,1},{4,6},{5,7},{6,4},{7,5},{8,10},{9,11},{10,... | collective-permute-start | bytes 393224 | tf_op jit(solution)/shard_map/ppermute | solution.py:46
  42.4 6.8 %collective-permute-start.12 = (bf16[64,1024]{1,0:T(8,128)(2,1)S(1)}, bf16[64,1024]{1,0:T(8,128)(2,1)S(1)}, u32[]{:S(2)}, u32[]{:S(2)}) collective-permute-start(bf16[64,1024]{1,0:T(8,128)(2,1)S(1)} %collective-permute-done.8.refs_3_), channel_id=1, source_target_pairs={{0,2},{2,0},{4,6},{6,4},{8,10},{10,8},{12,14},{14,12},{16,18},{18,... | collective-permute-start | bytes 393224 | tf_op jit(solution)/shard_map/ppermute | solution.py:46
  45.8 3.5 %collective-permute-start.11 = (bf16[64,1024]{1,0:T(8,128)(2,1)S(1)}, bf16[64,1024]{1,0:T(8,128)(2,1)S(1)}, u32[]{:S(2)}, u32[]{:S(2)}) collective-permute-start(bf16[64,1024]{1,0:T(8,128)(2,1)S(1)} %collective-permute-done.10.refs_5_), channel_id=1, source_target_pairs={{0,1},{1,0},{2,3},{3,2},{4,5},{5,4},{6,7},{7,6},{8,9},{9,8},{10,11... | collective-permute-start | bytes 393224 | tf_op jit(solution)/shard_map/ppermute | solution.py:31
  45.9 3.4 %collective-permute-start.9 = (bf16[64,1024]{1,0:T(8,128)(2,1)S(1)}, bf16[64,1024]{1,0:T(8,128)(2,1)S(1)}, u32[]{:S(2)}, u32[]{:S(2)}) collective-permute-start(bf16[64,1024]{1,0:T(8,128)(2,1)S(1)} %collective-permute-done.8.refs_3_), channel_id=1, source_target_pairs={{0,1},{1,0},{2,3},{3,2},{4,5},{5,4},{6,7},{7,6},{8,9},{9,8},{10,11... | collective-permute-start | bytes 393224 | tf_op jit(solution)/shard_map/ppermute | solution.py:31
  46.4 2.9 %collective-permute-start.15 = (bf16[64,1024]{1,0:T(8,128)(2,1)S(1)}, bf16[64,1024]{1,0:T(8,128)(2,1)S(1)}, u32[]{:S(2)}, u32[]{:S(2)}) collective-permute-start(bf16[64,1024]{1,0:T(8,128)(2,1)S(1)} %collective-permute-done.14.refs_9_), channel_id=1, source_target_pairs={{0,1},{1,0},{2,3},{3,2},{4,5},{5,4},{6,7},{7,6},{8,9},{9,8},{10,11... | collective-permute-start | bytes 393224 | tf_op jit(solution)/shard_map/ppermute | solution.py:31
  49.2 1.3 %collective-permute-start.13 = (bf16[64,1024]{1,0:T(8,128)(2,1)S(1)}, bf16[64,1024]{1,0:T(8,128)(2,1)S(1)}, u32[]{:S(2)}, u32[]{:S(2)}) collective-permute-start(bf16[64,1024]{1,0:T(8,128)(2,1)S(1)} %collective-permute-done.12.refs_7_), channel_id=1, source_target_pairs={{0,1},{1,0},{2,3},{3,2},{4,5},{5,4},{6,7},{7,6},{8,9},{9,8},{10,11... | collective-permute-start | bytes 393224 | tf_op jit(solution)/shard_map/ppermute | solution.py:31

commit v3 on v2

--- a/solution.py
+++ b/solution.py
@@ -36,13 +36,9 @@
     pairs = []
     for row in range(rows):
         for block in range(blocks):
-            for core, move in enumerate(moves):
-                if move is None:
-                    continue
-                axis, step = move
-                to_row = row ^ step if axis == "tok" else row
-                to_block = block ^ step if axis == "slot" else block
-                pairs.append(((row * blocks + block) * 2 + core, (to_row * blocks + to_block) * 2 + core))
+            for core, (over, across) in enumerate(moves):
+                to = (row ^ over) * blocks + (block ^ across)
+                pairs.append(((row * blocks + block) * 2 + core, to * 2 + core))
     return lax.ppermute(value, AXES, pairs)
 
 
@@ -162,10 +158,14 @@
     out_ref[...] = (numer / denom).astype(bf16)
 
 
-def expert_body(mine_ref, other_ref, in_ref, out_w_ref, out_ref):
-    mine, other = halves(mine_ref.shape[1])
-    value = jnp.dot(mine_ref[...], in_ref[mine, :], preferred_element_type=f32)
-    value = value + jnp.dot(other_ref[...], in_ref[other, :], preferred_element_type=f32)
+def expert_first_body(mine_ref, in_ref, value_ref):
+    mine, _ = halves(mine_ref.shape[1])
+    value_ref[...] = jnp.dot(mine_ref[...], in_ref[mine, :], preferred_element_type=f32)
+
+
+def expert_body(value_ref, other_ref, in_ref, out_w_ref, out_ref):
+    _, other = halves(other_ref.shape[1])
+    value = value_ref[...] + jnp.dot(other_ref[...], in_ref[other, :], preferred_element_type=f32)
     hidden = jax.nn.gelu(value, approximate=True).astype(bf16)
     out_ref[...] = jnp.dot(hidden, out_w_ref[...], preferred_element_type=f32)
 
@@ -174,26 +174,28 @@
     full_ref[...] = (part_ref[...] + recv_ref[...]).astype(bf16)
 
 
-def combine_body(blocks, rows, slots, plan, *refs):
-    low_refs, full_ref, pieces = refs[:blocks], refs[blocks], refs[blocks + 1 : -2]
-    out_ref, all_ref = refs[-2], refs[-1]
-    owned = full_ref.shape[0]
+def gather_pieces(all_ref, pieces, plan, slots, owned, first):
     core = lax.axis_index("hid")
     row = lax.axis_index("tok")
-
-    def put(step, ref):
-        block, expert = step
-        start = block * slots + (row ^ expert) * owned
+    pieces = list(pieces)
+
+    def put(ref, starts, turn):
+        start = jnp.where(core == turn, starts[0], starts[1])
         all_ref[pl.ds(pl.multiple_of(start, owned), owned), :] = ref[...]
 
-    put((0, 0), full_ref)
-    for index, steps in enumerate(plan):
-        for turn in range(2):
-            ref = pieces[2 * index + turn]
-            for holder in range(2):
-                step = steps[holder ^ turn]
-                if step is not None:
-                    pl.when(core == holder)(functools.partial(put, step, ref))
+    for moves in plan:
+        starts = [(across - first) * slots + (row ^ over) * owned for over, across in moves]
+        put(pieces.pop(0), starts, 0)
+        if moves[0] != moves[1]:
+            put(pieces.pop(0), starts, 1)
+
+
+def combine_first_body(blocks, slots, plan, *refs):
+    low_refs, full_ref, pieces = refs[:blocks], refs[blocks], refs[blocks + 1 : -3]
+    numer_ref, denom_ref, all_ref = refs[-3:]
+    owned = full_ref.shape[0]
+    all_ref[...] = jnp.zeros_like(all_ref)
+    gather_pieces(all_ref, (full_ref,) + pieces, [((0, 0), (0, 0))] + plan, slots, owned, 0)
     numer = None
     denom = None
     for block in range(blocks):
@@ -202,7 +204,23 @@
         total = jnp.sum(low.astype(f32), axis=1, keepdims=True)
         numer = part if numer is None else numer + part
         denom = total if denom is None else denom + total
-    out_ref[...] = numer / denom
+    numer_ref[...] = numer
+    denom_ref[...] = jnp.broadcast_to(denom, denom_ref.shape)
+
+
+def combine_last_body(blocks, slots, owned, plan, *refs):
+    low_refs, numer_ref, denom_ref, pieces = refs[: blocks - 1], refs[blocks - 1], refs[blocks], refs[blocks + 1 : -2]
+    out_ref, all_ref = refs[-2:]
+
+    @pl.when(pl.program_id(0) == 0)
+    def _():
+        all_ref[...] = jnp.zeros_like(all_ref)
+        gather_pieces(all_ref, pieces, plan, slots, owned, 1)
+
+    numer = numer_ref[...]
+    for block in range(blocks - 1):
+        numer = numer + jnp.dot(low_refs[block][...], all_ref[block * slots : (block + 1) * slots, :], preferred_element_type=f32)
+    out_ref[...] = numer / denom_ref[:, 0:1]
 
 
 def local(tokens, slot_keys, w_in, w_out):
@@ -245,40 +263,73 @@
         mine, total, *pieces, name="slot_inputs", nbytes=8 * owned * width,
     )
     inputs_other = swap(inputs, "hid", 1)
+    (value,) = call(
+        expert_first_body, [((owned, hidden), f32)], inputs, in_here,
+        name="expert_first", flops=owned * width * hidden, nbytes=width * hidden,
+    )
     (outputs_part,) = call(
         expert_body, [((owned, width), f32)],
-        inputs, inputs_other, in_here, out_here,
+        value, inputs_other, in_here, out_here,
         name="expert", flops=4 * owned * width * hidden, nbytes=4 * width * hidden,
     )
     outputs_recv = swap(outputs_part, "hid", 1)
-    (full,) = call(outputs_body, [((owned, width), bf16)], outputs_part, outputs_recv, name="slot_outputs", nbytes=8 * owned * width)
-
-    moves = [("tok", step) for step in range(1, rows)] + [("slot", step) for step in range(1, blocks)]
-    moves += [None] * (len(moves) % 2)
-    flights, plan = [], []
-    turns = [moves[at : at + 2] for at in range(0, len(moves), 2)][::-1]
-    for turn in turns:
-        got = swap_by_core(full, turn)
-        flights.append(got)
-        plan.append([move and ((0, move[1]) if move[0] == "tok" else (move[1], 0)) for move in turn])
-    for at, turn in list(enumerate(turns)):
-        for step in range(1, blocks):
-            along = [("slot", step) if move and move[0] == "tok" else None for move in turn]
-            if any(along):
-                flights.append(swap_by_core(flights[at], along))
-                plan.append([move and (step, turn[core][1]) for core, move in enumerate(along)])
-    pairs = []
-    for got, steps in zip(flights, plan):
-        pairs += [got, swap(got, "hid", 1)]
+    (full,) = call(
+        outputs_body, [((owned, width), bf16)],
+        outputs_part, outputs_recv, name="slot_outputs", nbytes=8 * owned * width,
+    )
+
+    far = [(over, 0) for over in range(2, rows)]
+    near = [(1, 0)] + [(0, across) for across in range(1, blocks)]
+    flights = []
+
+    def fly(value, moves, came=None):
+        came = came or moves
+        flights.append((swap_by_core(value, moves), came))
+        return flights[-1][0]
+
+    passed = []
+    for at in range(0, len(far), 2):
+        moves = far[at : at + 2]
+        got = fly(full, moves)
+        passed += [(got, moves)]
+    for at in range(0, len(near), 2):
+        fly(full, near[at : at + 2])
+    for across in range(1, blocks):
+        fly(full, [(1, across)] * 2)
+    direct = len(flights)
+    held = lax.optimization_barrier([got for got, _ in passed] + [got for got, came in flights if came[0] == came[1]])
+    passed = [(got, moves) for got, (_, moves) in zip(held, passed)]
+    for got, moves in passed:
+        for across in range(1, blocks):
+            fly(got, [(0, across)] * 2, [(over, across) for over, _ in moves])
+    def both(flights):
+        pieces = []
+        for got, came in flights:
+            pieces += [got] if came[0] == came[1] else [got, swap(got, "hid", 1)]
+        return pieces, [came for _, came in flights]
+
+    pieces, plan = both(flights[:direct])
+    numer, denom = call(
+        functools.partial(combine_first_body, blocks, slots, plan),
+        [((count, width), f32), ((count, 128), f32)],
+        *lows, full, *pieces,
+        name="combine_first", flops=2 * count * width * slots * blocks, nbytes=8 * count * width,
+        scratch=[pltpu.VMEM((blocks * slots, width), bf16)],
+    )
+    pieces, plan = both(flights[direct:])
+    tile = count // 2
     return pl.pallas_call(
-        functools.partial(combine_body, blocks, rows, slots, plan),
+        functools.partial(combine_last_body, blocks, slots, owned, plan),
         out_shape=jax.ShapeDtypeStruct((count, width), f32),
-        in_specs=[VMEM] * (blocks + 1 + len(pairs)),
-        out_specs=VMEM,
-        scratch_shapes=[pltpu.VMEM((blocks * slots, width), bf16)],
-        name="combine",
-        compiler_params=pltpu.CompilerParams(vmem_limit_bytes=40 * 2**20),
-    )(*lows, full, *pairs)
+        grid=(count // tile,),
+        in_specs=[pl.BlockSpec((tile, slots), lambda i: (i, 0))] * (blocks - 1)
+        + [pl.BlockSpec((tile, width), lambda i: (i, 0)), pl.BlockSpec((tile, 128), lambda i: (i, 0))]
+        + [VMEM] * len(pieces),
+        out_specs=pl.BlockSpec((tile, width), lambda i: (i, 0)),
+        scratch_shapes=[pltpu.VMEM(((blocks - 1) * slots, width), bf16)],
+        name="combine_last",
+        compiler_params=pltpu.CompilerParams(vmem_limit_bytes=24 * 2**20),
+    )(*lows[1:], numer, denom, *pieces)
 
 
 def solution(mesh):

time: 52.4 us -> 51.3 us (0.979)
  starting transfers between devices: 19 us -> 16.2 us
  waiting for transfers between devices: 20.9 us -> 22.1 us
    ppermute x4, starting transfers between devices: 8.78 us -> 5.98 us  [swap_by_core(): return lax.ppermute(value, AXES, pairs)]
    ppermute x4, waiting for transfers between devices: 6.31 us -> 8.71 us  [swap_by_core(): return lax.ppermute(value, AXES, pairs)]
    ppermute x12 -> x11, waiting for transfers between devices: 14.5 us -> 13.4 us  [swap(): lax.ppermute(value, axis, [(i, i ^ step) for i in range(lax.axis_size(axi...]
    pallas_call x6 -> x8, Pallas kernels: 4.14 us -> 4.84 us  [call(): pl.pallas_call(body, out_shape=[jax.ShapeDtypeStruct(s, d) for s, d in ou...]
    ppermute x12 -> x11, starting transfers between devices: 10.2 us -> 10.2 us  [swap(): lax.ppermute(value, axis, [(i, i ^ step) for i in range(lax.axis_size(axi...]
  transfers between devices with their start and end apart: 16 -> 15, of which waited for: 9 -> 10; matrix products, arithmetic and copies ran while one was open for 0% -> 0% of each run, Pallas kernels for 3% -> 5%
where the time goes in v3:
time: 51.3 us; the launch traced here: 51 us
  waiting for transfers between devices  22.1 us (43%)
  starting transfers between devices  16.2 us (32%)
  local copies, waits for them, and re-layouts  6.46 us (13%)
  Pallas kernels  6.18 us (12%)
    ppermute x11, waiting for transfers between devices, swap(): lax.ppermute(value, axis, [(i, i ^ step) for i in range(lax.axis_size(axi...  13.4 us
    ppermute x11, starting transfers between devices, swap(): lax.ppermute(value, axis, [(i, i ^ step) for i in range(lax.axis_size(axi...  10.2 us
    ppermute x4, waiting for transfers between devices, swap_by_core(): return lax.ppermute(value, AXES, pairs)  8.71 us
    unnamed x8, local copies, waits for them, and re-layouts  6.46 us
    ppermute x4, starting transfers between devices, swap_by_core(): return lax.ppermute(value, AXES, pairs)  5.98 us
    pallas_call x8, Pallas kernels, call(): pl.pallas_call(body, out_shape=[jax.ShapeDtypeStruct(s, d) for s, d in ou...  4.84 us
    pallas_call x1, Pallas kernels, local(): pl.pallas_call(functools.partial(combine_last_body, blocks, slots, owned,...  1.34 us
  transfers between devices with their start and end apart: 15, of which 10 were waited for; matrix products, arithmetic and copies ran while one was open for 0% of the time, Pallas kernels for 5%

profile of v3, /device:TPU:0, one launch (start us, length us, event | category | flops | bytes accessed | tf_op | source)
XLA Modules:
  0.0 51.0 jit_solution(6572647103472969581)
XLA Ops:
  0.0 2.9 %collective-permute-start = (bf16[256,1024]{1,0:T(8,128)(2,1)}, bf16[256,1024]{1,0:T(8,128)(2,1)S(1)}, u32[]{:S(2)}, u32[]{:S(2)}) collective-permute-start(bf16[256,1024]{1,0:T(8,128)(2,1)} %tok_ref.1), channel_id=1, source_target_pairs={{0,2},{2,0},{1,3},{3,1},{4,6},{6,4},{5,7},{7,5},{8,10},{10,8},{9,1... | collective-permute-start | bytes 1572872 | tf_op jit(solution)/shard_map/ppermute | solution.py:31
  2.9 0.0 copy-start
  2.9 2.2 %copy-done = bf16[1,1,1024,2048]{3,2,1,0:T(8,128)(2,1)S(1)} copy-done((bf16[1,1,1024,2048]{3,2,1,0:T(8,128)(2,1)S(1)}, bf16[1,1,1024,2048]{3,2,1,0:T(8,128)(2,1)}, u32[]{:S(2)}) %copy-start) | copy-done | bytes 4194328
  5.1 0.0 copy-start.1
  5.1 2.2 %copy-done.1 = bf16[1,1,2048,1024]{3,2,1,0:T(8,128)(2,1)S(1)} copy-done((bf16[1,1,2048,1024]{3,2,1,0:T(8,128)(2,1)S(1)}, bf16[1,1,2048,1024]{3,2,1,0:T(8,128)(2,1)}, u32[]{:S(2)}) %copy-start.1) | copy-done | bytes 4194328
  7.3 0.0 copy-start.2
  7.3 1.0 %copy-done.2 = bf16[1024,256]{1,0:T(8,128)(2,1)S(1)} copy-done((bf16[1024,256]{1,0:T(8,128)(2,1)S(1)}, bf16[1024,256]{1,0:T(8,128)(2,1)}, u32[]{:S(2)}) %copy-start.2) | copy-done | bytes 524312
  8.4 0.0 copy-start.3
  8.4 1.0 %copy-done.3 = bf16[256,1024]{1,0:T(8,128)(2,1)S(1)} copy-done((bf16[256,1024]{1,0:T(8,128)(2,1)S(1)}, bf16[256,1024]{1,0:T(8,128)(2,1)}, u32[]{:S(2)}) %copy-start.3) | copy-done | bytes 524312
  9.4 1.4 %dispatch_own.1 = (bf16[256,256]{1,0:T(8,128)(2,1)S(1)}, f32[264,512]{1,0:T(8,128)S(1)}, f32[264,512]{1,0:T(8,128)S(1)}, f32[8,256]{1,0:T(8,128)S(1)}, bf16[1024...) custom-call(bf16[256,1024]{1,0:T(8,128)(2,1)S(1)} %copy-done.3, ...), custom_call_target="tpu_custom_call" | custom-call | flops 268435456 | bytes 16777216 | tf_op jit(solution)/shard_map/dispatch_own/pallas_call | solution.py:18
  10.9 4.2 %collective-permute-done.tok_ref = bf16[256,1024]{1,0:T(8,128)(2,1)S(1)} collective-permute-done((bf16[256,1024]{1,0:T(8,128)(2,1)}, bf16[256,1024]{1,0:T(8,128)(2,1)S(1)}, u32[]{:S(2)}, u32[]{:S(2)}) %collective-permute-start) | collective-permute-done | bytes 524320 | tf_op jit(solution)/shard_map/ppermute | solution.py:31
  15.1 0.9 %dispatch_other.1 = (bf16[256,256]{1,0:T(8,128)(2,1)S(1)}, f32[264,512]{1,0:T(8,128)S(1)}, f32[264,512]{1,0:T(8,128)S(1)}) custom-call(bf16[256,1024]{1,0:T(8,128)(2,1)S(1)} %collective-permute-done.tok_ref, bf16[1024,256]{1,0:T(8,128)(2,1)S(1)} %get-tuple-element.28.key_ref, f32[8,256]{1,0:T(8,128)S(1)} %get-tuple-element.29.scale_ref, ...), custom_call_target="tpu_custom_call" | custom-call | flops 268435456 | bytes 524288 | tf_op jit(solution)/shard_map/dispatch_other/pallas_call | solution.py:18
  15.9 0.1 collective-permute-start.1
  16.0 1.8 %collective-permute-start.5 = (bf16[256,256]{1,0:T(8,128)(2,1)S(1)}, bf16[256,256]{1,0:T(8,128)(2,1)S(1)}, u32[]{:S(2)}, u32[]{:S(2)}) collective-permute-start(bf16[256,256]{1,0:T(8,128)(2,1)S(1)} %get-tuple-element.38), channel_id=1, source_target_pairs={{0,2},{2,0},{1,3},{3,1},{4,6},{6,4},{5,7},{7,5},{8,10},{10,8},{9,1... | collective-permute-start | bytes 393224 | tf_op jit(solution)/shard_map/ppermute | solution.py:31
  17.8 0.1 collective-permute-done.1.recv_ref
  17.9 0.1 share.1
  18.0 1.9 %collective-permute-start.2 = (bf16[72,512]{1,0:T(8,128)(2,1)S(1)}, bf16[72,512]{1,0:T(8,128)(2,1)S(1)}, u32[]{:S(2)}, u32[]{:S(2)}) collective-permute-start(bf16[72,512]{1,0:T(8,128)(2,1)S(1)} %get-tuple-element.34), channel_id=1, source_target_pairs={{0,4},{4,0},{8,12},{12,8},{1,5},{5,1},{9,13},{13,9},{2,6},{6,2},{1... | collective-permute-start | bytes 221192 | tf_op jit(solution)/shard_map/ppermute | solution.py:31
  19.9 2.6 %collective-permute-start.3 = (bf16[72,512]{1,0:T(8,128)(2,1)S(1)}, bf16[72,512]{1,0:T(8,128)(2,1)S(1)}, u32[]{:S(2)}, u32[]{:S(2)}) collective-permute-start(bf16[72,512]{1,0:T(8,128)(2,1)S(1)} %get-tuple-element.35), channel_id=1, source_target_pairs={{0,8},{4,12},{8,0},{12,4},{1,9},{5,13},{9,1},{13,5},{2,10},{6,14},... | collective-permute-start | bytes 221192 | tf_op jit(solution)/shard_map/ppermute | solution.py:31
  22.5 0.0 collective-permute-start.4
  22.5 0.0 collective-permute-done.5.refs_1_.refs_0_
  22.5 0.0 collective-permute-done.2.refs_0_
  22.5 6.3 %collective-permute-done.3.refs_1_ = bf16[72,512]{1,0:T(8,128)(2,1)S(1)} collective-permute-done((bf16[72,512]{1,0:T(8,128)(2,1)S(1)}, bf16[72,512]{1,0:T(8,128)(2,1)S(1)}, u32[]{:S(2)}, u32[]{:S(2)}) %collective-permute-start.3) | collective-permute-done | bytes 73760 | tf_op jit(solution)/shard_map/ppermute | solution.py:31
  28.8 0.0 collective-permute-done.4.refs_2_
  28.8 0.1 slot_inputs.1.mine_ref
  28.9 0.1 collective-permute-start.6
  29.0 0.5 expert_first.1.value_ref
  29.5 0.8 %collective-permute-done.6.other_ref = bf16[64,512]{1,0:T(8,128)(2,1)S(1)} collective-permute-done((bf16[64,512]{1,0:T(8,128)(2,1)S(1)}, bf16[64,512]{1,0:T(8,128)(2,1)S(1)}, u32[]{:S(2)}, u32[]{:S(2)}) %collective-permute-start.6) | collective-permute-done | bytes 65568 | tf_op jit(solution)/shard_map/ppermute | solution.py:31
  30.2 1.3 %expert.1.part_ref = f32[64,1024]{1,0:T(8,128)S(1)} custom-call(f32[64,2048]{1,0:T(8,128)S(1)} %expert_first.1.value_ref, bf16[64,512]{1,0:T(8,128)(2,1)S(1)} %collective-permute-done.6.other_ref, bf16[1024,2048]{1,0:T(8,128)(2,1)S(1)} %get-tuple-element.46.in_ref, bf16[2048,1024]{1,0:T(8,128)(2,1)S(1)} %get-tuple-element.47.out_w_ref), custom_call_target="tpu_custom_call" | custom-call | flops 536870912 | bytes 8388608 | tf_op jit(solution)/shard_map/expert/pallas_call | solution.py:18
  31.5 0.2 collective-permute-start.7
  31.7 1.4 %collective-permute-done.7.recv_ref = f32[64,1024]{1,0:T(8,128)S(1)} collective-permute-done((f32[64,1024]{1,0:T(8,128)S(1)}, f32[64,1024]{1,0:T(8,128)S(1)}, u32[]{:S(2)}, u32[]{:S(2)}) %collective-permute-start.7) | collective-permute-done | bytes 262176 | tf_op jit(solution)/shard_map/ppermute | solution.py:31
  33.1 2.4 %collective-permute-start.12 = (bf16[64,1024]{1,0:T(8,128)(2,1)S(1)}, bf16[64,1024]{1,0:T(8,128)(2,1)S(1)}, u32[]{:S(2)}, u32[]{:S(2)}) collective-permute-start(bf16[64,1024]{1,0:T(8,128)(2,1)S(1)} %slot_outputs.1.refs_2_), channel_id=1, source_target_pairs={{0,6},{1,7},{2,4},{3,5},{4,2},{5,3},{6,0},{7,1},{8,14},{9,15},{10,... | collective-permute-start | bytes 393224 | tf_op jit(solution)/shard_map/ppermute | solution.py:42
  35.6 1.6 %collective-permute-start.8 = (bf16[64,1024]{1,0:T(8,128)(2,1)S(1)}, bf16[64,1024]{1,0:T(8,128)(2,1)S(1)}, u32[]{:S(2)}, u32[]{:S(2)}) collective-permute-start(bf16[64,1024]{1,0:T(8,128)(2,1)S(1)} %slot_outputs.1.refs_2_), channel_id=1, source_target_pairs={{0,8},{1,13},{2,10},{3,15},{4,12},{5,9},{6,14},{7,11},{8,0},{9,5},... | collective-permute-start | bytes 393224 | tf_op jit(solution)/shard_map/ppermute | solution.py:42
  37.2 1.3 %collective-permute-start.10 = (bf16[64,1024]{1,0:T(8,128)(2,1)S(1)}, bf16[64,1024]{1,0:T(8,128)(2,1)S(1)}, u32[]{:S(2)}, u32[]{:S(2)}) collective-permute-start(bf16[64,1024]{1,0:T(8,128)(2,1)S(1)} %slot_outputs.1.refs_2_), channel_id=1, source_target_pairs={{0,4},{1,3},{2,6},{3,1},{4,0},{5,7},{6,2},{7,5},{8,12},{9,11},{10,... | collective-permute-start | bytes 393224 | tf_op jit(solution)/shard_map/ppermute | solution.py:42
  38.5 1.1 %collective-permute-done.12.refs_7_ = bf16[64,1024]{1,0:T(8,128)(2,1)S(1)} collective-permute-done((bf16[64,1024]{1,0:T(8,128)(2,1)S(1)}, bf16[64,1024]{1,0:T(8,128)(2,1)S(1)}, u32[]{:S(2)}, u32[]{:S(2)}) %collective-permute-start.12) | collective-permute-done | bytes 131104 | tf_op jit(solution)/shard_map/ppermute | solution.py:42
  39.6 2.5 %collective-permute-done.8.refs_3_ = bf16[64,1024]{1,0:T(8,128)(2,1)S(1)} collective-permute-done((bf16[64,1024]{1,0:T(8,128)(2,1)S(1)}, bf16[64,1024]{1,0:T(8,128)(2,1)S(1)}, u32[]{:S(2)}, u32[]{:S(2)}) %collective-permute-start.8) | collective-permute-done | bytes 131104 | tf_op jit(solution)/shard_map/ppermute | solution.py:42
  42.2 0.6 %collective-permute-start.13 = (bf16[64,1024]{1,0:T(8,128)(2,1)S(1)}, bf16[64,1024]{1,0:T(8,128)(2,1)S(1)}, u32[]{:S(2)}, u32[]{:S(2)}) collective-permute-start(bf16[64,1024]{1,0:T(8,128)(2,1)S(1)} %collective-permute-done.8.refs_3_), channel_id=1, source_target_pairs={{0,2},{1,3},{2,0},{3,1},{4,6},{5,7},{6,4},{7,5},{8,10},{9,11},{10,... | collective-permute-start | bytes 393224 | tf_op jit(solution)/shard_map/ppermute | solution.py:42
  42.8 1.5 %collective-permute-done.10.refs_5_ = bf16[64,1024]{1,0:T(8,128)(2,1)S(1)} collective-permute-done((bf16[64,1024]{1,0:T(8,128)(2,1)S(1)}, bf16[64,1024]{1,0:T(8,128)(2,1)S(1)}, u32[]{:S(2)}, u32[]{:S(2)}) %collective-permute-start.10) | collective-permute-done | bytes 131104 | tf_op jit(solution)/shard_map/ppermute | solution.py:42
  44.2 0.0 collective-permute-start.11
  44.2 0.5 collective-permute-start.9
  44.7 3.6 %collective-permute-done.13.refs_3_ = bf16[64,1024]{1,0:T(8,128)(2,1)S(1)} collective-permute-done((bf16[64,1024]{1,0:T(8,128)(2,1)S(1)}, bf16[64,1024]{1,0:T(8,128)(2,1)S(1)}, u32[]{:S(2)}, u32[]{:S(2)}) %collective-permute-start.13) | collective-permute-done | bytes 131104 | tf_op jit(solution)/shard_map/ppermute | solution.py:42
  48.3 0.1 collective-permute-start.14
  48.4 0.0 collective-permute-done.11.refs_6_
  48.4 0.0 collective-permute-done.9.refs_4_
  48.4 0.6 %combine_first.1 = (f32[256,1024]{1,0:T(8,128)S(1)}, f32[256,128]{1,0:T(8,128)S(1)}) custom-call(bf16[256,256]{1,0:T(8,128)(2,1)S(1)} %get-tuple-element.40.refs_0_, bf16[256,256]{1,0:T(8,128)(2,1)S(1)} %collective-permute-done.5.refs_1_.refs_0_, bf16[64,1024]{1,0:T(8,128)(2,1)S(1)} %slot_outputs.1.refs_2_, ...), custom_call_target="tpu_custom_call" | custom-call | flops 268435456 | bytes 2097152 | tf_op jit(solution)/shard_map/combine_first/pallas_call | solution.py:18
  49.0 0.7 %collective-permute-done.14.refs_4_ = bf16[64,1024]{1,0:T(8,128)(2,1)S(1)} collective-permute-done((bf16[64,1024]{1,0:T(8,128)(2,1)S(1)}, bf16[64,1024]{1,0:T(8,128)(2,1)S(1)}, u32[]{:S(2)}, u32[]{:S(2)}) %collective-permute-start.14) | collective-permute-done | bytes 131104 | tf_op jit(solution)/shard_map/ppermute | solution.py:31
  49.7 1.3 %combine_last.1 = f32[256,1024]{1,0:T(8,128)} custom-call(bf16[256,256]{1,0:T(8,128)(2,1)S(1)} %collective-permute-done.5.refs_1_.refs_0_, f32[256,1024]{1,0:T(8,128)S(1)} %get-tuple-element.48.refs_1_, f32[256,128]{1,0:T(8,128)S(1)} %get-tuple-element.49.refs_2_, bf16[64,1024]{1,0:T(8,128)(2,1)S(1)} %collective-permute-done.13.refs_3_, ...), custom_call_target="tpu_custom_call" | custom-call | tf_op jit(solution)/shard_map/combine_last/pallas_call | solution.py:321
  (1 shorter events, 0.0 us)
Async XLA Ops:
  0.0 15.1 %collective-permute-start = (bf16[256,1024]{1,0:T(8,128)(2,1)}, bf16[256,1024]{1,0:T(8,128)(2,1)S(1)}, u32[]{:S(2)}, u32[]{:S(2)}) collective-permute-start(bf16[256,1024]{1,0:T(8,128)(2,1)} %tok_ref.1), channel_id=1, source_target_pairs={{0,2},{2,0},{1,3},{3,1},{4,6},{6,4},{5,7},{7,5},{8,10},{10,8},{9,1... | collective-permute-start | bytes 1572872 | tf_op jit(solution)/shard_map/ppermute | solution.py:31
  2.9 2.2 %copy-start = (bf16[1,1,1024,2048]{3,2,1,0:T(8,128)(2,1)S(1)}, bf16[1,1,1024,2048]{3,2,1,0:T(8,128)(2,1)}, u32[]{:S(2)}) copy-start(bf16[1,1,1024,2048]{3,2,1,0:T(8,128)(2,1)} %param.6) | copy-start | bytes 12582916
  5.1 2.2 %copy-start.1 = (bf16[1,1,2048,1024]{3,2,1,0:T(8,128)(2,1)S(1)}, bf16[1,1,2048,1024]{3,2,1,0:T(8,128)(2,1)}, u32[]{:S(2)}) copy-start(bf16[1,1,2048,1024]{3,2,1,0:T(8,128)(2,1)} %param.7) | copy-start | bytes 12582916
  7.3 1.0 %copy-start.2 = (bf16[1024,256]{1,0:T(8,128)(2,1)S(1)}, bf16[1024,256]{1,0:T(8,128)(2,1)}, u32[]{:S(2)}) copy-start(bf16[1024,256]{1,0:T(8,128)(2,1)} %key_ref.1) | copy-start | bytes 1572868
  8.4 1.0 %copy-start.3 = (bf16[256,1024]{1,0:T(8,128)(2,1)S(1)}, bf16[256,1024]{1,0:T(8,128)(2,1)}, u32[]{:S(2)}) copy-start(bf16[256,1024]{1,0:T(8,128)(2,1)} %tok_ref.1) | copy-start | bytes 1572868
  15.9 2.0 %collective-permute-start.1 = (f32[264,512]{1,0:T(8,128)S(1)}, f32[264,512]{1,0:T(8,128)S(1)}, u32[]{:S(2)}, u32[]{:S(2)}) collective-permute-start(f32[264,512]{1,0:T(8,128)S(1)} %get-tuple-element.33), channel_id=1, source_target_pairs={{0,1},{1,0},{2,3},{3,2},{4,5},{5,4},{6,7},{7,6},{8,9},{9,8},{10,11... | collective-permute-start | bytes 1622024 | tf_op jit(solution)/shard_map/ppermute | solution.py:31
  16.0 6.5 %collective-permute-start.5 = (bf16[256,256]{1,0:T(8,128)(2,1)S(1)}, bf16[256,256]{1,0:T(8,128)(2,1)S(1)}, u32[]{:S(2)}, u32[]{:S(2)}) collective-permute-start(bf16[256,256]{1,0:T(8,128)(2,1)S(1)} %get-tuple-element.38), channel_id=1, source_target_pairs={{0,2},{2,0},{1,3},{3,1},{4,6},{6,4},{5,7},{7,5},{8,10},{10,8},{9,1... | collective-permute-start | bytes 393224 | tf_op jit(solution)/shard_map/ppermute | solution.py:31
  18.0 4.5 %collective-permute-start.2 = (bf16[72,512]{1,0:T(8,128)(2,1)S(1)}, bf16[72,512]{1,0:T(8,128)(2,1)S(1)}, u32[]{:S(2)}, u32[]{:S(2)}) collective-permute-start(bf16[72,512]{1,0:T(8,128)(2,1)S(1)} %get-tuple-element.34), channel_id=1, source_target_pairs={{0,4},{4,0},{8,12},{12,8},{1,5},{5,1},{9,13},{13,9},{2,6},{6,2},{1... | collective-permute-start | bytes 221192 | tf_op jit(solution)/shard_map/ppermute | solution.py:31
  19.9 8.9 %collective-permute-start.3 = (bf16[72,512]{1,0:T(8,128)(2,1)S(1)}, bf16[72,512]{1,0:T(8,128)(2,1)S(1)}, u32[]{:S(2)}, u32[]{:S(2)}) collective-permute-start(bf16[72,512]{1,0:T(8,128)(2,1)S(1)} %get-tuple-element.35), channel_id=1, source_target_pairs={{0,8},{4,12},{8,0},{12,4},{1,9},{5,13},{9,1},{13,5},{2,10},{6,14},... | collective-permute-start | bytes 221192 | tf_op jit(solution)/shard_map/ppermute | solution.py:31
  22.5 6.3 %collective-permute-start.4 = (bf16[72,512]{1,0:T(8,128)(2,1)S(1)}, bf16[72,512]{1,0:T(8,128)(2,1)S(1)}, u32[]{:S(2)}, u32[]{:S(2)}) collective-permute-start(bf16[72,512]{1,0:T(8,128)(2,1)S(1)} %get-tuple-element.36), channel_id=1, source_target_pairs={{0,12},{4,8},{8,4},{12,0},{1,13},{5,9},{9,5},{13,1},{2,14},{6,10},... | collective-permute-start | bytes 221192 | tf_op jit(solution)/shard_map/ppermute | solution.py:31
  28.9 1.3 %collective-permute-start.6 = (bf16[64,512]{1,0:T(8,128)(2,1)S(1)}, bf16[64,512]{1,0:T(8,128)(2,1)S(1)}, u32[]{:S(2)}, u32[]{:S(2)}) collective-permute-start(bf16[64,512]{1,0:T(8,128)(2,1)S(1)} %slot_inputs.1.mine_ref), channel_id=1, source_target_pairs={{0,1},{1,0},{2,3},{3,2},{4,5},{5,4},{6,7},{7,6},{8,9},{9,8},{10,11... | collective-permute-start | bytes 196616 | tf_op jit(solution)/shard_map/ppermute | solution.py:31
  31.5 1.6 %collective-permute-start.7 = (f32[64,1024]{1,0:T(8,128)S(1)}, f32[64,1024]{1,0:T(8,128)S(1)}, u32[]{:S(2)}, u32[]{:S(2)}) collective-permute-start(f32[64,1024]{1,0:T(8,128)S(1)} %expert.1.part_ref), channel_id=1, source_target_pairs={{0,1},{1,0},{2,3},{3,2},{4,5},{5,4},{6,7},{7,6},{8,9},{9,8},{10,11... | collective-permute-start | bytes 786440 | tf_op jit(solution)/shard_map/ppermute | solution.py:31
  33.1 6.5 %collective-permute-start.12 = (bf16[64,1024]{1,0:T(8,128)(2,1)S(1)}, bf16[64,1024]{1,0:T(8,128)(2,1)S(1)}, u32[]{:S(2)}, u32[]{:S(2)}) collective-permute-start(bf16[64,1024]{1,0:T(8,128)(2,1)S(1)} %slot_outputs.1.refs_2_), channel_id=1, source_target_pairs={{0,6},{1,7},{2,4},{3,5},{4,2},{5,3},{6,0},{7,1},{8,14},{9,15},{10,... | collective-permute-start | bytes 393224 | tf_op jit(solution)/shard_map/ppermute | solution.py:42
  35.6 6.6 %collective-permute-start.8 = (bf16[64,1024]{1,0:T(8,128)(2,1)S(1)}, bf16[64,1024]{1,0:T(8,128)(2,1)S(1)}, u32[]{:S(2)}, u32[]{:S(2)}) collective-permute-start(bf16[64,1024]{1,0:T(8,128)(2,1)S(1)} %slot_outputs.1.refs_2_), channel_id=1, source_target_pairs={{0,8},{1,13},{2,10},{3,15},{4,12},{5,9},{6,14},{7,11},{8,0},{9,5},... | collective-permute-start | bytes 393224 | tf_op jit(solution)/shard_map/ppermute | solution.py:42
  37.2 7.1 %collective-permute-start.10 = (bf16[64,1024]{1,0:T(8,128)(2,1)S(1)}, bf16[64,1024]{1,0:T(8,128)(2,1)S(1)}, u32[]{:S(2)}, u32[]{:S(2)}) collective-permute-start(bf16[64,1024]{1,0:T(8,128)(2,1)S(1)} %slot_outputs.1.refs_2_), channel_id=1, source_target_pairs={{0,4},{1,3},{2,6},{3,1},{4,0},{5,7},{6,2},{7,5},{8,12},{9,11},{10,... | collective-permute-start | bytes 393224 | tf_op jit(solution)/shard_map/ppermute | solution.py:42
  42.2 6.1 %collective-permute-start.13 = (bf16[64,1024]{1,0:T(8,128)(2,1)S(1)}, bf16[64,1024]{1,0:T(8,128)(2,1)S(1)}, u32[]{:S(2)}, u32[]{:S(2)}) collective-permute-start(bf16[64,1024]{1,0:T(8,128)(2,1)S(1)} %collective-permute-done.8.refs_3_), channel_id=1, source_target_pairs={{0,2},{1,3},{2,0},{3,1},{4,6},{5,7},{6,4},{7,5},{8,10},{9,11},{10,... | collective-permute-start | bytes 393224 | tf_op jit(solution)/shard_map/ppermute | solution.py:42
  44.2 4.2 %collective-permute-start.11 = (bf16[64,1024]{1,0:T(8,128)(2,1)S(1)}, bf16[64,1024]{1,0:T(8,128)(2,1)S(1)}, u32[]{:S(2)}, u32[]{:S(2)}) collective-permute-start(bf16[64,1024]{1,0:T(8,128)(2,1)S(1)} %collective-permute-done.10.refs_5_), channel_id=1, source_target_pairs={{0,1},{1,0},{2,3},{3,2},{4,5},{5,4},{6,7},{7,6},{8,9},{9,8},{10,11... | collective-permute-start | bytes 393224 | tf_op jit(solution)/shard_map/ppermute | solution.py:31
  44.2 4.2 %collective-permute-start.9 = (bf16[64,1024]{1,0:T(8,128)(2,1)S(1)}, bf16[64,1024]{1,0:T(8,128)(2,1)S(1)}, u32[]{:S(2)}, u32[]{:S(2)}) collective-permute-start(bf16[64,1024]{1,0:T(8,128)(2,1)S(1)} %collective-permute-done.8.refs_3_), channel_id=1, source_target_pairs={{0,1},{1,0},{2,3},{3,2},{4,5},{5,4},{6,7},{7,6},{8,9},{9,8},{10,11... | collective-permute-start | bytes 393224 | tf_op jit(solution)/shard_map/ppermute | solution.py:31
  48.3 1.3 %collective-permute-start.14 = (bf16[64,1024]{1,0:T(8,128)(2,1)S(1)}, bf16[64,1024]{1,0:T(8,128)(2,1)S(1)}, u32[]{:S(2)}, u32[]{:S(2)}) collective-permute-start(bf16[64,1024]{1,0:T(8,128)(2,1)S(1)} %collective-permute-done.13.refs_3_), channel_id=1, source_target_pairs={{0,1},{1,0},{2,3},{3,2},{4,5},{5,4},{6,7},{7,6},{8,9},{9,8},{10,11... | collective-permute-start | bytes 393224 | tf_op jit(solution)/shard_map/ppermute | solution.py:31

commit v4 on v3

v4 whole, which is shorter than its diff:
```python
import functools

import jax
import jax.numpy as jnp
from jax import lax
from jax.experimental import pallas as pl
from jax.experimental.pallas import tpu as pltpu
from jax.sharding import PartitionSpec as P

epsilon = 1e-06
bf16, f32 = jnp.bfloat16, jnp.float32
VMEM = pl.BlockSpec(memory_space=pltpu.VMEM)
STAY = pl.BlockSpec(memory_space=pltpu.HBM)
AXES = ("tok", "slot", "hid")


def call(body, outs, *args, name, flops=0, nbytes=0, stay=0, scratch=()):
    return pl.pallas_call(
        body,
        out_shape=[jax.ShapeDtypeStruct(s, d) for s, d in outs],
        in_specs=[VMEM] * (len(args) - stay) + [STAY] * stay,
        out_specs=[VMEM] * len(outs),
        scratch_shapes=list(scratch),
        name=name,
        compiler_params=pltpu.CompilerParams(vmem_limit_bytes=24 * 2**20),
        cost_estimate=pl.CostEstimate(flops=flops, bytes_accessed=nbytes, transcendentals=0),
    )(*args)


def swap(value, axis, step):
    return lax.ppermute(value, axis, [(i, i ^ step) for i in range(lax.axis_size(axis))])


def swap_by_core(value, moves):
    rows, blocks = lax.axis_size("tok"), lax.axis_size("slot")
    pairs = []
    for row in range(rows):
        for block in range(blocks):
            for core, (over, across) in enumerate(moves):
                to = (row ^ over) * blocks + (block ^ across)
                pairs.append(((row * blocks + block) * 2 + core, to * 2 + core))
    return lax.ppermute(value, AXES, pairs)


def spread(value, step, across):
    rows, blocks = lax.axis_size("tok"), lax.axis_size("slot")
    per = rows // 2
    pairs = []
    for row in range(rows):
        for block in range(blocks):
            for core in range(2):
                to = (core * per + (row % per ^ step)) * blocks + (block ^ across)
                pairs.append(((row * blocks + block) * 2 + core, to * 2 + (row // per ^ core)))
    return lax.ppermute(value, AXES, pairs)


def keys_body(key_ref, out_ref, sem):
    part = out_ref.shape[1]
    core = lax.axis_index("hid")
    copy = pltpu.make_async_copy(key_ref.at[:, pl.ds(pl.multiple_of(core * part, part), part)], out_ref, sem)
    copy.start()
    copy.wait()


def stage_body(after_ref, from_ref, here_ref, sem):
    copy = pltpu.make_async_copy(from_ref, here_ref, sem)
    copy.start()
    copy.wait()


def stage(after, value):
    return call(stage_body, [(value.shape, value.dtype)], after, value, name="stage", nbytes=4 * value.size, stay=1, scratch=[pltpu.SemaphoreType.DMA])[0]


def dispatch_body(first, owned, *refs):
    if first:
        tok_refs, key_ref, low_refs, scale_refs, piece_refs, numer_ref = refs[0:2], refs[2], refs[3:5], refs[5:7], refs[8:-1], refs[-1]
        refs[7][...] = tok_refs[0][...]
    else:
        tok_refs, key_ref, scale_refs, low_refs, piece_refs, numer_ref = refs[0:2], refs[2], refs[3:5], refs[5:7], refs[7:-1], refs[-1]
    width, part = key_ref.shape
    key = key_ref[...].astype(f32)
    key_scale = lax.rsqrt(jnp.sum(key * key, axis=0, keepdims=True) / width + epsilon)
    numer = None
    total = None
    for tok_ref, low_ref, scale_ref in zip(tok_refs, low_refs, scale_refs):
        if first:
            tok = tok_ref[...].astype(f32)
            scale = lax.rsqrt(jnp.sum(tok * tok, axis=1, keepdims=True) / width + epsilon) * (4.0 / width)
            scale_ref[...] = jnp.broadcast_to(scale, scale_ref.shape)
        else:
            scale = scale_ref[:, 0:1]
        logits = jnp.dot(tok_ref[...], key_ref[...], preferred_element_type=f32)
        weights = jnp.exp(logits * scale * key_scale)
        low = weights.astype(bf16)
        low_ref[...] = low
        mine = lax.dot_general(low, tok_ref[...], (((0,), (0,)), ((), ())), preferred_element_type=f32)
        numer = mine if numer is None else numer + mine
        mine = jnp.sum(weights, axis=0, keepdims=True)
        total = mine if total is None else total + mine
    numer_ref[...] = numer
    terms = []
    for _ in range(3):
        term = total.astype(bf16)
        terms.append(term)
        total = total - term.astype(f32)
    per = part // owned
    low_row = lax.rem(lax.axis_index("tok"), per)
    for step, ref in enumerate(piece_refs):
        start = pl.multiple_of((low_row ^ step) * owned, owned)
        ref[0:owned, :] = numer_ref[pl.ds(start, owned), :].astype(bf16)
        ref[owned:, :] = jnp.zeros((8, width), bf16)
        for index, term in enumerate(terms):
            ref[owned + index : owned + index + 1, 0:part] = term


def sum_body(*refs):
    piece_refs, out_ref = refs[:-1], refs[-1]
    out = None
    for ref in piece_refs:
        piece = ref[...].astype(f32)
        out = piece if out is None else out + piece
    out_ref[...] = out


def expert_body(part, mine_ref, other_ref, in_ref, out_w_ref, out_ref):
    owned = out_ref.shape[0]
    numer = mine_ref[0:owned, :] + other_ref[0:owned, :]
    total = mine_ref[owned:, 0:part] + other_ref[owned:, 0:part]
    total = total[0:1, :] + total[1:2, :] + total[2:3, :]
    per = part // owned
    lane = lax.broadcasted_iota(jnp.int32, (owned, part), 1)
    wanted = lax.broadcasted_iota(jnp.int32, (owned, part), 0) + lax.rem(lax.axis_index("tok"), per) * owned
    denom = jnp.sum(jnp.where(lane == wanted, jnp.broadcast_to(total, (owned, part)), 0.0), axis=1, keepdims=True)
    inputs = (numer / denom).astype(bf16)
    value = jnp.dot(inputs, in_ref[...], preferred_element_type=f32)
    hidden = jax.nn.gelu(value, approximate=True).astype(bf16)
    out_ref[...] = jnp.dot(hidden, out_w_ref[...], preferred_element_type=f32)


def outputs_body(part_ref, recv_ref, full_ref):
    full_ref[...] = (part_ref[...] + recv_ref[...]).astype(bf16)


def gather_pieces(all_ref, pieces, plan, slots, owned, first):
    core = lax.axis_index("hid")
    row = lax.axis_index("tok")
    pieces = list(pieces)

    def put(ref, starts, turn):
        start = jnp.where(core == turn, starts[0], starts[1])
        all_ref[pl.ds(pl.multiple_of(start, owned), owned), :] = ref[...]

    for moves in plan:
        starts = [(across - first) * slots + (row ^ over) * owned for over, across in moves]
        put(pieces.pop(0), starts, 0)
        if moves[0] != moves[1]:
            put(pieces.pop(0), starts, 1)


def mix(low_refs, all_ref, blocks, slots):
    part = slots // 2
    core = lax.axis_index("hid")
    numer = None
    for index, ref in enumerate(low_refs):
        start = (index // 2) * slots + (core if index % 2 == 0 else 1 - core) * part
        mine = jnp.dot(ref[...], all_ref[pl.ds(pl.multiple_of(start, part), part), :], preferred_element_type=f32)
        numer = mine if numer is None else numer + mine
    return numer


def combine_first_body(blocks, slots, plan, *refs):
    low_refs, full_ref, pieces = refs[: 2 * blocks], refs[2 * blocks], refs[2 * blocks + 1 : -3]
    numer_ref, denom_ref, all_ref = refs[-3:]
    all_ref[...] = jnp.zeros_like(all_ref)
    gather_pieces(all_ref, (full_ref,) + pieces, [((0, 0), (0, 0))] + plan, slots, full_ref.shape[0], 0)
    numer_ref[...] = mix(low_refs, all_ref, blocks, slots)
    denom = None
    for ref in low_refs:
        total = jnp.sum(ref[...].astype(f32), axis=1, keepdims=True)
        denom = total if denom is None else denom + total
    denom_ref[...] = jnp.broadcast_to(denom, denom_ref.shape)


def combine_last_body(blocks, slots, owned, plan, *refs):
    lows = 2 * (blocks - 1)
    low_refs, numer_ref, denom_ref, pieces = refs[:lows], refs[lows], refs[lows + 1], refs[lows + 2 : -2]
    out_ref, all_ref = refs[-2:]

    @pl.when(pl.program_id(0) == 0)
    def _():
        all_ref[...] = jnp.zeros_like(all_ref)
        gather_pieces(all_ref, pieces, plan, slots, owned, 1)

    out_ref[...] = (numer_ref[...] + mix(low_refs, all_ref, blocks - 1, slots)) / denom_ref[:, 0:1]


def local(tokens, slot_keys, w_in, w_out):
    count, width = tokens.shape
    slots = slot_keys.shape[1]
    hidden = w_in.shape[3]
    rows, blocks = lax.axis_size("tok"), lax.axis_size("slot")
    owned = slots // rows
    part = slots // 2
    mac = 8 * count * width * part
    piece = ((owned + 8, width), bf16)
    lows_shape = [((count, part), bf16)] * 2
    scratch = [pltpu.VMEM((part, width), f32)]

    (keys,) = call(keys_body, [((width, part), bf16)], slot_keys, name="keys", nbytes=4 * width * part, stay=1, scratch=[pltpu.SemaphoreType.DMA])
    arrived = [swap(keys, "slot", across) for across in range(1, blocks)]
    beside = swap(tokens, "hid", 1)
    low_mine, low_send, scale, scale_beside, here, *pieces = call(
        functools.partial(dispatch_body, True, owned),
        lows_shape + [((count, 128), f32)] * 2 + [((count, width), bf16)] + [piece] * (rows // 2),
        tokens, beside, keys, name="dispatch_own", flops=mac, nbytes=4 * count * width, scratch=scratch,
    )
    sent = [spread(value, step, 0) for step, value in enumerate(pieces)]
    lows = [low_mine, swap(low_send, "hid", 1)]
    for across in range(1, blocks):
        low_mine, low_send, *pieces = call(
            functools.partial(dispatch_body, False, owned),
            lows_shape + [piece] * (rows // 2),
            here, beside, arrived[across - 1], scale, scale_beside,
            name="dispatch_other", flops=mac, nbytes=4 * count * width, scratch=scratch,
        )
        sent += [spread(value, step, across) for step, value in enumerate(pieces)]
        lows += [low_mine, swap(low_send, "hid", 1)]
    out_here = stage(low_send, w_out[0, 0])
    sent, lows, out_here = lax.optimization_barrier((sent, lows, out_here))
    (mine,) = call(sum_body, [((owned + 8, width), f32)], *sent, name="sum_pieces", nbytes=4 * owned * width * len(sent))
    other = swap(mine, "hid", 1)
    (outputs_part,) = call(
        functools.partial(expert_body, part), [((owned, width), f32)],
        mine, other, w_in[0, 0], out_here,
        name="expert", flops=4 * owned * width * hidden, nbytes=4 * width * hidden,
    )
    outputs_recv = swap(outputs_part, "hid", 1)
    (full,) = call(
        outputs_body, [((owned, width), bf16)],
        outputs_part, outputs_recv, name="slot_outputs", nbytes=8 * owned * width,
    )

    far = [(over, 0) for over in range(2, rows)]
    near = [(1, 0)] + [(0, across) for across in range(1, blocks)]
    flights = []

    def fly(value, moves, came=None):
        came = came or moves
        flights.append((swap_by_core(value, moves), came))
        return flights[-1][0]

    passed = []
    for at in range(0, len(far), 2):
        moves = far[at : at + 2]
        got = fly(full, moves)
        passed += [(got, moves)]
    for at in range(0, len(near), 2):
        fly(full, near[at : at + 2])
    for across in range(1, blocks):
        fly(full, [(1, across)] * 2)
    direct = len(flights)
    held = lax.optimization_barrier([got for got, _ in passed] + [got for got, came in flights if came[0] == came[1]])
    passed = [(got, moves) for got, (_, moves) in zip(held, passed)]
    for got, moves in passed:
        for across in range(1, blocks):
            fly(got, [(0, across)] * 2, [(over, across) for over, _ in moves])
    def both(flights):
        pieces = []
        for got, came in flights:
            pieces += [got] if came[0] == came[1] else [got, swap(got, "hid", 1)]
        return pieces, [came for _, came in flights]

    pieces, plan = both(flights[:direct])
    numer, denom = call(
        functools.partial(combine_first_body, blocks, slots, plan),
        [((count, width), f32), ((count, 128), f32)],
        *lows, full, *pieces,
        name="combine_first", flops=2 * count * width * slots * blocks, nbytes=8 * count * width,
        scratch=[pltpu.VMEM((blocks * slots, width), bf16)],
    )
    pieces, plan = both(flights[direct:])
    tile = count // 2
    return pl.pallas_call(
        functools.partial(combine_last_body, blocks, slots, owned, plan),
        out_shape=jax.ShapeDtypeStruct((count, width), f32),
        grid=(count // tile,),
        in_specs=[pl.BlockSpec((tile, part), lambda i: (i, 0))] * (2 * blocks - 2)
        + [pl.BlockSpec((tile, width), lambda i: (i, 0)), pl.BlockSpec((tile, 128), lambda i: (i, 0))]
        + [VMEM] * len(pieces),
        out_specs=pl.BlockSpec((tile, width), lambda i: (i, 0)),
        scratch_shapes=[pltpu.VMEM(((blocks - 1) * slots, width), bf16)],
        name="combine_last",
        compiler_params=pltpu.CompilerParams(vmem_limit_bytes=24 * 2**20),
    )(*lows[2:], numer, denom, *pieces)


def solution(mesh):
    in_specs = (
        P(("groups", "tok", "slot", "hid"), None),
        P("groups", "slot"),
        P(("groups", "slot"), "tok", None, "hid"),
        P(("groups", "slot"), "tok", "hid", None),
    )
    out_specs = P(("groups", "tok", "slot", "hid"), None)
    return jax.shard_map(local, mesh=mesh, in_specs=in_specs, out_specs=out_specs, check_vma=False)
```

time: 51.3 us -> 46.5 us (0.906)
  waiting for transfers between devices: 22.1 us -> 12.2 us
  starting transfers between devices: 16.2 us -> 23.3 us
  local copies, waits for them, and re-layouts: 6.46 us -> 4.27 us
    ppermute x11 -> x9, waiting for transfers between devices: 13.4 us -> 6.01 us  [swap(): lax.ppermute(value, axis, [(i, i ^ step) for i in range(lax.axis_size(axi...]
    ppermute x0 -> x4, starting transfers between devices: none -> 5.65 us  [spread(): return lax.ppermute(value, AXES, pairs)]
    ppermute x4, waiting for transfers between devices: 8.71 us -> 6.18 us  [swap_by_core(): return lax.ppermute(value, AXES, pairs)]
    unnamed x8, local copies, waits for them, and re-layouts: 6.46 us -> 4.27 us
    ppermute x4, starting transfers between devices: 5.98 us -> 7.04 us  [swap_by_core(): return lax.ppermute(value, AXES, pairs)]
    ppermute x11 -> x9, starting transfers between devices: 10.2 us -> 10.6 us  [swap(): lax.ppermute(value, axis, [(i, i ^ step) for i in range(lax.axis_size(axi...]
  transfers between devices with their start and end apart: 15 -> 17, of which waited for: 10 -> 9; matrix products, arithmetic and copies ran while one was open for 0% -> 0% of each run, Pallas kernels for 5% -> 7%
where the time goes in v4:
time: 46.5 us; the launch traced here: 46.2 us
  starting transfers between devices  23.3 us (50%)
  waiting for transfers between devices  12.2 us (26%)
  Pallas kernels  6.27 us (13%)
  local copies, waits for them, and re-layouts  4.27 us (9%)
    ppermute x9, starting transfers between devices, swap(): lax.ppermute(value, axis, [(i, i ^ step) for i in range(lax.axis_size(axi...  10.6 us
    ppermute x4, starting transfers between devices, swap_by_core(): return lax.ppermute(value, AXES, pairs)  7.04 us
    ppermute x4, waiting for transfers between devices, swap_by_core(): return lax.ppermute(value, AXES, pairs)  6.18 us
    ppermute x9, waiting for transfers between devices, swap(): lax.ppermute(value, axis, [(i, i ^ step) for i in range(lax.axis_size(axi...  6.01 us
    ppermute x4, starting transfers between devices, spread(): return lax.ppermute(value, AXES, pairs)  5.65 us
    pallas_call x8, Pallas kernels, call(): pl.pallas_call(body, out_shape=[jax.ShapeDtypeStruct(s, d) for s, d in ou...  4.82 us
    unnamed x8, local copies, waits for them, and re-layouts  4.27 us
    pallas_call x1, Pallas kernels, local(): pl.pallas_call(functools.partial(combine_last_body, blocks, slots, owned,...  1.45 us
  transfers between devices with their start and end apart: 17, of which 9 were waited for; matrix products, arithmetic and copies ran while one was open for 0% of the time, Pallas kernels for 7%

profile of v4, /device:TPU:0, one launch (start us, length us, event | category | flops | bytes accessed | tf_op | source)
XLA Modules:
  0.0 46.2 jit_solution(739415648955767794)
XLA Ops:
  0.0 0.5 collective-permute-start
  0.5 0.0 copy-start.2
  0.5 1.0 %copy-done.2 = bf16[1024,256]{1,0:T(8,128)(2,1)S(1)} copy-done((bf16[1024,256]{1,0:T(8,128)(2,1)S(1)}, bf16[1024,256]{1,0:T(8,128)(2,1)}, u32[]{:S(2)}) %copy-start.2) | copy-done | bytes 524312
  1.5 0.1 keys.1.refs_2_
  1.6 2.6 %collective-permute-start.3 = (bf16[1024,128]{1,0:T(8,128)(2,1)S(1)}, bf16[1024,128]{1,0:T(8,128)(2,1)S(1)}, u32[]{:S(2)}, u32[]{:S(2)}) collective-permute-start(bf16[1024,128]{1,0:T(8,128)(2,1)S(1)} %keys.1.refs_2_), channel_id=1, source_target_pairs={{0,2},{2,0},{1,3},{3,1},{4,6},{6,4},{5,7},{7,5},{8,10},{10,8},{9,1... | collective-permute-start | bytes 786440 | tf_op jit(solution)/shard_map/ppermute | solution.py:31
  4.1 0.0 collective-permute-done.refs_1_
  4.1 0.0 copy-start.3
  4.1 1.0 %copy-done.3 = bf16[256,1024]{1,0:T(8,128)(2,1)S(1)} copy-done((bf16[256,1024]{1,0:T(8,128)(2,1)S(1)}, bf16[256,1024]{1,0:T(8,128)(2,1)}, u32[]{:S(2)}) %copy-start.3) | copy-done | bytes 524312
  5.2 1.1 %dispatch_own.1 = (bf16[256,128]{1,0:T(8,128)(2,1)S(1)}, bf16[256,128]{1,0:T(8,128)(2,1)S(1)}, f32[256,128]{1,0:T(8,128)S(1)}, f32[256,128]{1,0:T(8,128)S(1)}, b...) custom-call(bf16[256,1024]{1,0:T(8,128)(2,1)S(1)} %copy-done.3, ...), custom_call_target="tpu_custom_call" | custom-call | flops 268435456 | bytes 1048576 | tf_op jit(solution)/shard_map/dispatch_own/pallas_call | solution.py:18
  6.2 0.7 %collective-permute-start.1 = (bf16[72,1024]{1,0:T(8,128)(2,1)S(1)}, bf16[72,1024]{1,0:T(8,128)(2,1)S(1)}, u32[]{:S(2)}, u32[]{:S(2)}) collective-permute-start(bf16[72,1024]{1,0:T(8,128)(2,1)S(1)} %get-tuple-element.28), channel_id=1, source_target_pairs={{0,0},{1,9},{2,2},{3,11},{4,4},{5,13},{6,6},{7,15},{8,1},{9,8},{10... | collective-permute-start | bytes 442376 | tf_op jit(solution)/shard_map/ppermute | solution.py:54
  6.9 1.6 %collective-permute-start.2 = (bf16[72,1024]{1,0:T(8,128)(2,1)S(1)}, bf16[72,1024]{1,0:T(8,128)(2,1)S(1)}, u32[]{:S(2)}, u32[]{:S(2)}) collective-permute-start(bf16[72,1024]{1,0:T(8,128)(2,1)S(1)} %get-tuple-element.29), channel_id=1, source_target_pairs={{0,4},{1,13},{2,6},{3,15},{4,0},{5,9},{6,2},{7,11},{8,5},{9,12},{1... | collective-permute-start | bytes 442376 | tf_op jit(solution)/shard_map/ppermute | solution.py:54
  8.5 2.6 %collective-permute-done.3.refs_2_ = bf16[1024,128]{1,0:T(8,128)(2,1)S(1)} collective-permute-done((bf16[1024,128]{1,0:T(8,128)(2,1)S(1)}, bf16[1024,128]{1,0:T(8,128)(2,1)S(1)}, u32[]{:S(2)}, u32[]{:S(2)}) %collective-permute-start.3) | collective-permute-done | bytes 262176 | tf_op jit(solution)/shard_map/ppermute | solution.py:31
  11.1 0.8 %dispatch_other.1 = (bf16[256,128]{1,0:T(8,128)(2,1)S(1)}, bf16[256,128]{1,0:T(8,128)(2,1)S(1)}, bf16[72,1024]{1,0:T(8,128)(2,1)S(1)}, bf16[72,1024]{1,0:T(8,128)(2,1)S(1)}) custom-call(bf16[256,1024]{1,0:T(8,128)(2,1)S(1)} %get-tuple-element.30.refs_0_, bf16[256,1024]{1,0:T(8,128)(2,1)S(1)} %collective-permute-done.refs_1_, ...), custom_call_target="tpu_custom_call" | custom-call | flops 268435456 | bytes 1048576 | tf_op jit(solution)/shard_map/dispatch_other/pallas_call | solution.py:18
  11.9 1.8 %collective-permute-start.4 = (bf16[72,1024]{1,0:T(8,128)(2,1)S(1)}, bf16[72,1024]{1,0:T(8,128)(2,1)S(1)}, u32[]{:S(2)}, u32[]{:S(2)}) collective-permute-start(bf16[72,1024]{1,0:T(8,128)(2,1)S(1)} %get-tuple-element.33), channel_id=1, source_target_pairs={{0,2},{1,11},{2,0},{3,9},{4,6},{5,15},{6,4},{7,13},{8,3},{9,10},{1... | collective-permute-start | bytes 442376 | tf_op jit(solution)/shard_map/ppermute | solution.py:54
  13.7 1.6 %collective-permute-start.5 = (bf16[72,1024]{1,0:T(8,128)(2,1)S(1)}, bf16[72,1024]{1,0:T(8,128)(2,1)S(1)}, u32[]{:S(2)}, u32[]{:S(2)}) collective-permute-start(bf16[72,1024]{1,0:T(8,128)(2,1)S(1)} %get-tuple-element.34), channel_id=1, source_target_pairs={{0,6},{1,15},{2,4},{3,13},{4,2},{5,11},{6,0},{7,9},{8,7},{9,14},{1... | collective-permute-start | bytes 442376 | tf_op jit(solution)/shard_map/ppermute | solution.py:54
  15.3 1.9 %collective-permute-start.7 = (bf16[256,128]{1,0:T(8,128)(2,1)S(1)}, bf16[256,128]{1,0:T(8,128)(2,1)S(1)}, u32[]{:S(2)}, u32[]{:S(2)}) collective-permute-start(bf16[256,128]{1,0:T(8,128)(2,1)S(1)} %get-tuple-element.38.after_ref), channel_id=1, source_target_pairs={{0,1},{1,0},{2,3},{3,2},{4,5},{5,4},{6,7},{7,6},{8,9},{9,8},{10,11... | collective-permute-start | bytes 196616 | tf_op jit(solution)/shard_map/ppermute | solution.py:31
  17.2 0.9 %collective-permute-done.7.refs_3_.refs_1_ = bf16[256,128]{1,0:T(8,128)(2,1)S(1)} collective-permute-done((bf16[256,128]{1,0:T(8,128)(2,1)S(1)}, bf16[256,128]{1,0:T(8,128)(2,1)S(1)}, u32[]{:S(2)}, u32[]{:S(2)}) %collective-permute-start.7) | collective-permute-done | bytes 65568 | tf_op jit(solution)/shard_map/ppermute | solution.py:31
  18.1 0.4 collective-permute-start.6
  18.4 2.2 %copy-done = bf16[1,1,2048,1024]{3,2,1,0:T(8,128)(2,1)S(1)} copy-done((bf16[1,1,2048,1024]{3,2,1,0:T(8,128)(2,1)S(1)}, bf16[1,1,2048,1024]{3,2,1,0:T(8,128)(2,1)}, u32[]{:S(2)}) %copy-start) | copy-done | bytes 4194328
  20.6 0.3 stage.1.out_w_ref
  20.9 0.0 collective-permute-done.6.refs_1_
  20.9 0.0 collective-permute-done.1.refs_0_
  20.9 0.0 collective-permute-done.2.refs_1_
  20.9 0.0 collective-permute-done.4.refs_2_
  21.0 0.0 collective-permute-done.5.refs_3_
  21.0 0.1 sum_pieces.1.mine_ref
  21.0 2.9 %collective-permute-start.8 = (f32[72,1024]{1,0:T(8,128)S(1)}, f32[72,1024]{1,0:T(8,128)S(1)}, u32[]{:S(2)}, u32[]{:S(2)}) collective-permute-start(f32[72,1024]{1,0:T(8,128)S(1)} %sum_pieces.1.mine_ref), channel_id=1, source_target_pairs={{0,1},{1,0},{2,3},{3,2},{4,5},{5,4},{6,7},{7,6},{8,9},{9,8},{10,11... | collective-permute-start | bytes 884744 | tf_op jit(solution)/shard_map/ppermute | solution.py:31
  23.9 1.2 %collective-permute-done.8.other_ref = f32[72,1024]{1,0:T(8,128)S(1)} collective-permute-done((f32[72,1024]{1,0:T(8,128)S(1)}, f32[72,1024]{1,0:T(8,128)S(1)}, u32[]{:S(2)}, u32[]{:S(2)}) %collective-permute-start.8) | collective-permute-done | bytes 294944 | tf_op jit(solution)/shard_map/ppermute | solution.py:31
  25.1 0.0 copy-done.1
  25.1 1.7 %expert.1.part_ref = f32[64,1024]{1,0:T(8,128)S(1)} custom-call(f32[72,1024]{1,0:T(8,128)S(1)} %sum_pieces.1.mine_ref, f32[72,1024]{1,0:T(8,128)S(1)} %collective-permute-done.8.other_ref, bf16[1024,2048]{1,0:T(8,128)(2,1)S(1)} %bitcast.3, bf16[2048,1024]{1,0:T(8,128)(2,1)S(1)} %stage.1.out_w_ref), custom_call_target="tpu_custom_call" | custom-call | flops 536870912 | bytes 8388608 | tf_op jit(solution)/shard_map/expert/pallas_call | solution.py:18
  26.8 0.4 collective-permute-start.9
  27.2 1.2 %collective-permute-done.9.recv_ref = f32[64,1024]{1,0:T(8,128)S(1)} collective-permute-done((f32[64,1024]{1,0:T(8,128)S(1)}, f32[64,1024]{1,0:T(8,128)S(1)}, u32[]{:S(2)}, u32[]{:S(2)}) %collective-permute-start.9) | collective-permute-done | bytes 262176 | tf_op jit(solution)/shard_map/ppermute | solution.py:31
  28.4 2.8 %collective-permute-start.14 = (bf16[64,1024]{1,0:T(8,128)(2,1)S(1)}, bf16[64,1024]{1,0:T(8,128)(2,1)S(1)}, u32[]{:S(2)}, u32[]{:S(2)}) collective-permute-start(bf16[64,1024]{1,0:T(8,128)(2,1)S(1)} %slot_outputs.1.refs_4_), channel_id=1, source_target_pairs={{0,6},{1,7},{2,4},{3,5},{4,2},{5,3},{6,0},{7,1},{8,14},{9,15},{10,... | collective-permute-start | bytes 393224 | tf_op jit(solution)/shard_map/ppermute | solution.py:42
  31.3 1.2 %collective-permute-start.10 = (bf16[64,1024]{1,0:T(8,128)(2,1)S(1)}, bf16[64,1024]{1,0:T(8,128)(2,1)S(1)}, u32[]{:S(2)}, u32[]{:S(2)}) collective-permute-start(bf16[64,1024]{1,0:T(8,128)(2,1)S(1)} %slot_outputs.1.refs_4_), channel_id=1, source_target_pairs={{0,8},{1,13},{2,10},{3,15},{4,12},{5,9},{6,14},{7,11},{8,0},{9,5},... | collective-permute-start | bytes 393224 | tf_op jit(solution)/shard_map/ppermute | solution.py:42
  32.5 2.1 %collective-permute-start.12 = (bf16[64,1024]{1,0:T(8,128)(2,1)S(1)}, bf16[64,1024]{1,0:T(8,128)(2,1)S(1)}, u32[]{:S(2)}, u32[]{:S(2)}) collective-permute-start(bf16[64,1024]{1,0:T(8,128)(2,1)S(1)} %slot_outputs.1.refs_4_), channel_id=1, source_target_pairs={{0,4},{1,3},{2,6},{3,1},{4,0},{5,7},{6,2},{7,5},{8,12},{9,11},{10,... | collective-permute-start | bytes 393224 | tf_op jit(solution)/shard_map/ppermute | solution.py:42
  34.6 0.6 %collective-permute-done.14.refs_9_ = bf16[64,1024]{1,0:T(8,128)(2,1)S(1)} collective-permute-done((bf16[64,1024]{1,0:T(8,128)(2,1)S(1)}, bf16[64,1024]{1,0:T(8,128)(2,1)S(1)}, u32[]{:S(2)}, u32[]{:S(2)}) %collective-permute-start.14) | collective-permute-done | bytes 131104 | tf_op jit(solution)/shard_map/ppermute | solution.py:42
  35.3 2.1 %collective-permute-done.10.refs_5_ = bf16[64,1024]{1,0:T(8,128)(2,1)S(1)} collective-permute-done((bf16[64,1024]{1,0:T(8,128)(2,1)S(1)}, bf16[64,1024]{1,0:T(8,128)(2,1)S(1)}, u32[]{:S(2)}, u32[]{:S(2)}) %collective-permute-start.10) | collective-permute-done | bytes 131104 | tf_op jit(solution)/shard_map/ppermute | solution.py:42
  37.4 0.8 %collective-permute-start.15 = (bf16[64,1024]{1,0:T(8,128)(2,1)S(1)}, bf16[64,1024]{1,0:T(8,128)(2,1)S(1)}, u32[]{:S(2)}, u32[]{:S(2)}) collective-permute-start(bf16[64,1024]{1,0:T(8,128)(2,1)S(1)} %collective-permute-done.10.refs_5_), channel_id=1, source_target_pairs={{0,2},{1,3},{2,0},{3,1},{4,6},{5,7},{6,4},{7,5},{8,10},{9,11},{10,... | collective-permute-start | bytes 393224 | tf_op jit(solution)/shard_map/ppermute | solution.py:42
  38.3 1.5 %collective-permute-done.12.refs_7_ = bf16[64,1024]{1,0:T(8,128)(2,1)S(1)} collective-permute-done((bf16[64,1024]{1,0:T(8,128)(2,1)S(1)}, bf16[64,1024]{1,0:T(8,128)(2,1)S(1)}, u32[]{:S(2)}, u32[]{:S(2)}) %collective-permute-start.12) | collective-permute-done | bytes 131104 | tf_op jit(solution)/shard_map/ppermute | solution.py:42
  39.8 0.7 %collective-permute-start.13 = (bf16[64,1024]{1,0:T(8,128)(2,1)S(1)}, bf16[64,1024]{1,0:T(8,128)(2,1)S(1)}, u32[]{:S(2)}, u32[]{:S(2)}) collective-permute-start(bf16[64,1024]{1,0:T(8,128)(2,1)S(1)} %collective-permute-done.12.refs_7_), channel_id=1, source_target_pairs={{0,1},{1,0},{2,3},{3,2},{4,5},{5,4},{6,7},{7,6},{8,9},{9,8},{10,11... | collective-permute-start | bytes 393224 | tf_op jit(solution)/shard_map/ppermute | solution.py:31
  40.5 0.0 collective-permute-start.11
  40.5 1.9 %collective-permute-done.15.refs_4_ = bf16[64,1024]{1,0:T(8,128)(2,1)S(1)} collective-permute-done((bf16[64,1024]{1,0:T(8,128)(2,1)S(1)}, bf16[64,1024]{1,0:T(8,128)(2,1)S(1)}, u32[]{:S(2)}, u32[]{:S(2)}) %collective-permute-start.15) | collective-permute-done | bytes 131104 | tf_op jit(solution)/shard_map/ppermute | solution.py:42
  42.4 1.3 %collective-permute-start.16 = (bf16[64,1024]{1,0:T(8,128)(2,1)S(1)}, bf16[64,1024]{1,0:T(8,128)(2,1)S(1)}, u32[]{:S(2)}, u32[]{:S(2)}) collective-permute-start(bf16[64,1024]{1,0:T(8,128)(2,1)S(1)} %collective-permute-done.15.refs_4_), channel_id=1, source_target_pairs={{0,1},{1,0},{2,3},{3,2},{4,5},{5,4},{6,7},{7,6},{8,9},{9,8},{10,11... | collective-permute-start | bytes 393224 | tf_op jit(solution)/shard_map/ppermute | solution.py:31
  43.7 0.0 collective-permute-done.13.refs_8_
  43.7 0.0 collective-permute-done.11.refs_6_
  43.7 0.8 %combine_first.1 = (f32[256,1024]{1,0:T(8,128)S(1)}, f32[256,128]{1,0:T(8,128)S(1)}) custom-call(bf16[256,128]{1,0:T(8,128)(2,1)S(1)} %get-tuple-element.41.refs_0_, bf16[256,128]{1,0:T(8,128)(2,1)S(1)} %collective-permute-done.6.refs_1_, bf16[256,128]{1,0:T(8,128)(2,1)S(1)} %get-tuple-element.39.refs_2_.refs_0_, ...), custom_call_target="tpu_custom_call" | custom-call | flops 268435456 | bytes 2097152 | tf_op jit(solution)/shard_map/combine_first/pallas_call | solution.py:18
  44.5 0.2 collective-permute-done.16.refs_5_
  44.7 1.5 %combine_last.1 = f32[256,1024]{1,0:T(8,128)} custom-call(bf16[256,128]{1,0:T(8,128)(2,1)S(1)} %get-tuple-element.39.refs_2_.refs_0_, bf16[256,128]{1,0:T(8,128)(2,1)S(1)} %collective-permute-done.7.refs_3_.refs_1_, f32[256,1024]{1,0:T(8,128)S(1)} %get-tuple-element.48.refs_2_, f32[256,128]{1,0:T(8,128)S(1)} %get-tuple-element.49.refs_3_, ...), custom_call_target="tpu_custom_call" | custom-call | tf_op jit(solution)/shard_map/combine_last/pallas_call | solution.py:284
  (3 shorter events, 0.0 us)
Async XLA Ops:
  0.0 4.1 %collective-permute-start = (bf16[256,1024]{1,0:T(8,128)(2,1)}, bf16[256,1024]{1,0:T(8,128)(2,1)S(1)}, u32[]{:S(2)}, u32[]{:S(2)}) collective-permute-start(bf16[256,1024]{1,0:T(8,128)(2,1)} %refs_0_.1), channel_id=1, source_target_pairs={{0,1},{1,0},{2,3},{3,2},{4,5},{5,4},{6,7},{7,6},{8,9},{9,8},{10,11... | collective-permute-start | bytes 1572872 | tf_op jit(solution)/shard_map/ppermute | solution.py:31
  0.5 1.0 %copy-start.2 = (bf16[1024,256]{1,0:T(8,128)(2,1)S(1)}, bf16[1024,256]{1,0:T(8,128)(2,1)}, u32[]{:S(2)}) copy-start(bf16[1024,256]{1,0:T(8,128)(2,1)} %key_ref.1) | copy-start | bytes 1572868
  1.6 9.5 %collective-permute-start.3 = (bf16[1024,128]{1,0:T(8,128)(2,1)S(1)}, bf16[1024,128]{1,0:T(8,128)(2,1)S(1)}, u32[]{:S(2)}, u32[]{:S(2)}) collective-permute-start(bf16[1024,128]{1,0:T(8,128)(2,1)S(1)} %keys.1.refs_2_), channel_id=1, source_target_pairs={{0,2},{2,0},{1,3},{3,1},{4,6},{6,4},{5,7},{7,5},{8,10},{10,8},{9,1... | collective-permute-start | bytes 786440 | tf_op jit(solution)/shard_map/ppermute | solution.py:31
  4.1 1.0 %copy-start.3 = (bf16[256,1024]{1,0:T(8,128)(2,1)S(1)}, bf16[256,1024]{1,0:T(8,128)(2,1)}, u32[]{:S(2)}) copy-start(bf16[256,1024]{1,0:T(8,128)(2,1)} %refs_0_.1) | copy-start | bytes 1572868
  6.2 14.7 %collective-permute-start.1 = (bf16[72,1024]{1,0:T(8,128)(2,1)S(1)}, bf16[72,1024]{1,0:T(8,128)(2,1)S(1)}, u32[]{:S(2)}, u32[]{:S(2)}) collective-permute-start(bf16[72,1024]{1,0:T(8,128)(2,1)S(1)} %get-tuple-element.28), channel_id=1, source_target_pairs={{0,0},{1,9},{2,2},{3,11},{4,4},{5,13},{6,6},{7,15},{8,1},{9,8},{10... | collective-permute-start | bytes 442376 | tf_op jit(solution)/shard_map/ppermute | solution.py:54
  6.9 14.0 %collective-permute-start.2 = (bf16[72,1024]{1,0:T(8,128)(2,1)S(1)}, bf16[72,1024]{1,0:T(8,128)(2,1)S(1)}, u32[]{:S(2)}, u32[]{:S(2)}) collective-permute-start(bf16[72,1024]{1,0:T(8,128)(2,1)S(1)} %get-tuple-element.29), channel_id=1, source_target_pairs={{0,4},{1,13},{2,6},{3,15},{4,0},{5,9},{6,2},{7,11},{8,5},{9,12},{1... | collective-permute-start | bytes 442376 | tf_op jit(solution)/shard_map/ppermute | solution.py:54
  11.9 9.0 %collective-permute-start.4 = (bf16[72,1024]{1,0:T(8,128)(2,1)S(1)}, bf16[72,1024]{1,0:T(8,128)(2,1)S(1)}, u32[]{:S(2)}, u32[]{:S(2)}) collective-permute-start(bf16[72,1024]{1,0:T(8,128)(2,1)S(1)} %get-tuple-element.33), channel_id=1, source_target_pairs={{0,2},{1,11},{2,0},{3,9},{4,6},{5,15},{6,4},{7,13},{8,3},{9,10},{1... | collective-permute-start | bytes 442376 | tf_op jit(solution)/shard_map/ppermute | solution.py:54
  13.7 7.2 %collective-permute-start.5 = (bf16[72,1024]{1,0:T(8,128)(2,1)S(1)}, bf16[72,1024]{1,0:T(8,128)(2,1)S(1)}, u32[]{:S(2)}, u32[]{:S(2)}) collective-permute-start(bf16[72,1024]{1,0:T(8,128)(2,1)S(1)} %get-tuple-element.34), channel_id=1, source_target_pairs={{0,6},{1,15},{2,4},{3,13},{4,2},{5,11},{6,0},{7,9},{8,7},{9,14},{1... | collective-permute-start | bytes 442376 | tf_op jit(solution)/shard_map/ppermute | solution.py:54
  15.3 2.8 %collective-permute-start.7 = (bf16[256,128]{1,0:T(8,128)(2,1)S(1)}, bf16[256,128]{1,0:T(8,128)(2,1)S(1)}, u32[]{:S(2)}, u32[]{:S(2)}) collective-permute-start(bf16[256,128]{1,0:T(8,128)(2,1)S(1)} %get-tuple-element.38.after_ref), channel_id=1, source_target_pairs={{0,1},{1,0},{2,3},{3,2},{4,5},{5,4},{6,7},{7,6},{8,9},{9,8},{10,11... | collective-permute-start | bytes 196616 | tf_op jit(solution)/shard_map/ppermute | solution.py:31
  18.1 2.8 %collective-permute-start.6 = (bf16[256,128]{1,0:T(8,128)(2,1)S(1)}, bf16[256,128]{1,0:T(8,128)(2,1)S(1)}, u32[]{:S(2)}, u32[]{:S(2)}) collective-permute-start(bf16[256,128]{1,0:T(8,128)(2,1)S(1)} %get-tuple-element.36), channel_id=1, source_target_pairs={{0,1},{1,0},{2,3},{3,2},{4,5},{5,4},{6,7},{7,6},{8,9},{9,8},{10,11... | collective-permute-start | bytes 196616 | tf_op jit(solution)/shard_map/ppermute | solution.py:31
  18.4 2.2 %copy-start = (bf16[1,1,2048,1024]{3,2,1,0:T(8,128)(2,1)S(1)}, bf16[1,1,2048,1024]{3,2,1,0:T(8,128)(2,1)}, u32[]{:S(2)}) copy-start(bf16[1,1,2048,1024]{3,2,1,0:T(8,128)(2,1)} %param.7) | copy-start | bytes 12582916
  20.6 4.5 %copy-start.1 = (bf16[1,1,1024,2048]{3,2,1,0:T(8,128)(2,1)S(1)}, bf16[1,1,1024,2048]{3,2,1,0:T(8,128)(2,1)}, u32[]{:S(2)}) copy-start(bf16[1,1,1024,2048]{3,2,1,0:T(8,128)(2,1)} %param.6) | copy-start | bytes 12582916
  21.0 4.1 %collective-permute-start.8 = (f32[72,1024]{1,0:T(8,128)S(1)}, f32[72,1024]{1,0:T(8,128)S(1)}, u32[]{:S(2)}, u32[]{:S(2)}) collective-permute-start(f32[72,1024]{1,0:T(8,128)S(1)} %sum_pieces.1.mine_ref), channel_id=1, source_target_pairs={{0,1},{1,0},{2,3},{3,2},{4,5},{5,4},{6,7},{7,6},{8,9},{9,8},{10,11... | collective-permute-start | bytes 884744 | tf_op jit(solution)/shard_map/ppermute | solution.py:31
  26.8 1.6 %collective-permute-start.9 = (f32[64,1024]{1,0:T(8,128)S(1)}, f32[64,1024]{1,0:T(8,128)S(1)}, u32[]{:S(2)}, u32[]{:S(2)}) collective-permute-start(f32[64,1024]{1,0:T(8,128)S(1)} %expert.1.part_ref), channel_id=1, source_target_pairs={{0,1},{1,0},{2,3},{3,2},{4,5},{5,4},{6,7},{7,6},{8,9},{9,8},{10,11... | collective-permute-start | bytes 786440 | tf_op jit(solution)/shard_map/ppermute | solution.py:31
  28.4 6.8 %collective-permute-start.14 = (bf16[64,1024]{1,0:T(8,128)(2,1)S(1)}, bf16[64,1024]{1,0:T(8,128)(2,1)S(1)}, u32[]{:S(2)}, u32[]{:S(2)}) collective-permute-start(bf16[64,1024]{1,0:T(8,128)(2,1)S(1)} %slot_outputs.1.refs_4_), channel_id=1, source_target_pairs={{0,6},{1,7},{2,4},{3,5},{4,2},{5,3},{6,0},{7,1},{8,14},{9,15},{10,... | collective-permute-start | bytes 393224 | tf_op jit(solution)/shard_map/ppermute | solution.py:42
  31.3 6.2 %collective-permute-start.10 = (bf16[64,1024]{1,0:T(8,128)(2,1)S(1)}, bf16[64,1024]{1,0:T(8,128)(2,1)S(1)}, u32[]{:S(2)}, u32[]{:S(2)}) collective-permute-start(bf16[64,1024]{1,0:T(8,128)(2,1)S(1)} %slot_outputs.1.refs_4_), channel_id=1, source_target_pairs={{0,8},{1,13},{2,10},{3,15},{4,12},{5,9},{6,14},{7,11},{8,0},{9,5},... | collective-permute-start | bytes 393224 | tf_op jit(solution)/shard_map/ppermute | solution.py:42
  32.5 7.3 %collective-permute-start.12 = (bf16[64,1024]{1,0:T(8,128)(2,1)S(1)}, bf16[64,1024]{1,0:T(8,128)(2,1)S(1)}, u32[]{:S(2)}, u32[]{:S(2)}) collective-permute-start(bf16[64,1024]{1,0:T(8,128)(2,1)S(1)} %slot_outputs.1.refs_4_), channel_id=1, source_target_pairs={{0,4},{1,3},{2,6},{3,1},{4,0},{5,7},{6,2},{7,5},{8,12},{9,11},{10,... | collective-permute-start | bytes 393224 | tf_op jit(solution)/shard_map/ppermute | solution.py:42
  37.4 5.0 %collective-permute-start.15 = (bf16[64,1024]{1,0:T(8,128)(2,1)S(1)}, bf16[64,1024]{1,0:T(8,128)(2,1)S(1)}, u32[]{:S(2)}, u32[]{:S(2)}) collective-permute-start(bf16[64,1024]{1,0:T(8,128)(2,1)S(1)} %collective-permute-done.10.refs_5_), channel_id=1, source_target_pairs={{0,2},{1,3},{2,0},{3,1},{4,6},{5,7},{6,4},{7,5},{8,10},{9,11},{10,... | collective-permute-start | bytes 393224 | tf_op jit(solution)/shard_map/ppermute | solution.py:42
  39.8 4.0 %collective-permute-start.13 = (bf16[64,1024]{1,0:T(8,128)(2,1)S(1)}, bf16[64,1024]{1,0:T(8,128)(2,1)S(1)}, u32[]{:S(2)}, u32[]{:S(2)}) collective-permute-start(bf16[64,1024]{1,0:T(8,128)(2,1)S(1)} %collective-permute-done.12.refs_7_), channel_id=1, source_target_pairs={{0,1},{1,0},{2,3},{3,2},{4,5},{5,4},{6,7},{7,6},{8,9},{9,8},{10,11... | collective-permute-start | bytes 393224 | tf_op jit(solution)/shard_map/ppermute | solution.py:31
  40.5 3.2 %collective-permute-start.11 = (bf16[64,1024]{1,0:T(8,128)(2,1)S(1)}, bf16[64,1024]{1,0:T(8,128)(2,1)S(1)}, u32[]{:S(2)}, u32[]{:S(2)}) collective-permute-start(bf16[64,1024]{1,0:T(8,128)(2,1)S(1)} %collective-permute-done.10.refs_5_), channel_id=1, source_target_pairs={{0,1},{1,0},{2,3},{3,2},{4,5},{5,4},{6,7},{7,6},{8,9},{9,8},{10,11... | collective-permute-start | bytes 393224 | tf_op jit(solution)/shard_map/ppermute | solution.py:31
  42.4 2.3 %collective-permute-start.16 = (bf16[64,1024]{1,0:T(8,128)(2,1)S(1)}, bf16[64,1024]{1,0:T(8,128)(2,1)S(1)}, u32[]{:S(2)}, u32[]{:S(2)}) collective-permute-start(bf16[64,1024]{1,0:T(8,128)(2,1)S(1)} %collective-permute-done.15.refs_4_), channel_id=1, source_target_pairs={{0,1},{1,0},{2,3},{3,2},{4,5},{5,4},{6,7},{7,6},{8,9},{9,8},{10,11... | collective-permute-start | bytes 393224 | tf_op jit(solution)/shard_map/ppermute | solution.py:31

commit v5 on v4

--- a/solution.py
+++ b/solution.py
@@ -182,17 +182,33 @@
     denom_ref[...] = jnp.broadcast_to(denom, denom_ref.shape)
 
 
-def combine_last_body(blocks, slots, owned, plan, *refs):
+def combine_last_body(blocks, slots, owned, tiles, plan, *refs):
     lows = 2 * (blocks - 1)
-    low_refs, numer_ref, denom_ref, pieces = refs[:lows], refs[lows], refs[lows + 1], refs[lows + 2 : -2]
-    out_ref, all_ref = refs[-2:]
-
-    @pl.when(pl.program_id(0) == 0)
-    def _():
+    low_refs, numer_ref, denom_ref, pieces = refs[:lows], refs[lows], refs[lows + 1], refs[lows + 2 : -4]
+    out_hbm, all_ref, out_ref, sems = refs[-4:]
+    part = slots // 2
+    per = part // owned
+    core = lax.axis_index("hid")
+    far = 1 - lax.axis_index("tok") // per
+    if per > 2:
         all_ref[...] = jnp.zeros_like(all_ref)
-        gather_pieces(all_ref, pieces, plan, slots, owned, 1)
-
-    out_ref[...] = (numer_ref[...] + mix(low_refs, all_ref, blocks - 1, slots)) / denom_ref[:, 0:1]
+    gather_pieces(all_ref, pieces, plan, slots, owned, 1)
+    tile = out_ref.shape[0] // tiles
+    copies = []
+    for index in range(tiles):
+        rows = pl.ds(index * tile, tile)
+        numer = numer_ref[rows, :]
+        for block in range(blocks - 1):
+            mine, other = low_refs[2 * block][rows, :], low_refs[2 * block + 1][rows, :]
+            for side in [far] if per == 2 else [0, 1]:
+                low = jnp.where(core == side, mine, other)
+                start = pl.multiple_of(block * slots + side * part, part)
+                numer = numer + jnp.dot(low, all_ref[pl.ds(start, part), :], preferred_element_type=f32)
+        out_ref[rows, :] = numer / denom_ref[rows, 0:1]
+        copies.append(pltpu.make_async_copy(out_ref.at[rows, :], out_hbm.at[rows, :], sems.at[index]))
+        copies[-1].start()
+    for copy in copies:
+        copy.wait()
 
 
 def local(tokens, slot_keys, w_in, w_out):
@@ -280,16 +296,17 @@
         scratch=[pltpu.VMEM((blocks * slots, width), bf16)],
     )
     pieces, plan = both(flights[direct:])
-    tile = count // 2
+    tiles = 4
     return pl.pallas_call(
-        functools.partial(combine_last_body, blocks, slots, owned, plan),
+        functools.partial(combine_last_body, blocks, slots, owned, tiles, plan),
         out_shape=jax.ShapeDtypeStruct((count, width), f32),
-        grid=(count // tile,),
-        in_specs=[pl.BlockSpec((tile, part), lambda i: (i, 0))] * (2 * blocks - 2)
-        + [pl.BlockSpec((tile, width), lambda i: (i, 0)), pl.BlockSpec((tile, 128), lambda i: (i, 0))]
-        + [VMEM] * len(pieces),
-        out_specs=pl.BlockSpec((tile, width), lambda i: (i, 0)),
-        scratch_shapes=[pltpu.VMEM(((blocks - 1) * slots, width), bf16)],
+        in_specs=[VMEM] * (2 * blocks + len(pieces)),
+        out_specs=pl.BlockSpec(memory_space=pl.ANY),
+        scratch_shapes=[
+            pltpu.VMEM(((blocks - 1) * slots, width), bf16),
+            pltpu.VMEM((count, width), f32),
+            pltpu.SemaphoreType.DMA((tiles,)),
+        ],
         name="combine_last",
         compiler_params=pltpu.CompilerParams(vmem_limit_bytes=24 * 2**20),
     )(*lows[2:], numer, denom, *pieces)

time: 46.5 us -> 46.3 us (level)
  no operation moved by 1% of the time
where the time goes in v5:
time: 46.3 us; the launch traced here: 46 us
  starting transfers between devices  23.3 us (50%)
  waiting for transfers between devices  12.2 us (26%)
  Pallas kernels  6.05 us (13%)
  local copies, waits for them, and re-layouts  4.27 us (9%)
    ppermute x9, starting transfers between devices, swap(): lax.ppermute(value, axis, [(i, i ^ step) for i in range(lax.axis_size(axi...  10.6 us
    ppermute x4, starting transfers between devices, swap_by_core(): return lax.ppermute(value, AXES, pairs)  7.04 us
    ppermute x4, waiting for transfers between devices, swap_by_core(): return lax.ppermute(value, AXES, pairs)  6.18 us
    ppermute x9, waiting for transfers between devices, swap(): lax.ppermute(value, axis, [(i, i ^ step) for i in range(lax.axis_size(axi...  6.01 us
    ppermute x4, starting transfers between devices, spread(): return lax.ppermute(value, AXES, pairs)  5.65 us
    pallas_call x8, Pallas kernels, call(): pl.pallas_call(body, out_shape=[jax.ShapeDtypeStruct(s, d) for s, d in ou...  4.82 us
    unnamed x8, local copies, waits for them, and re-layouts  4.27 us
    pallas_call x1, Pallas kernels, local(): pl.pallas_call(functools.partial(combine_last_body, blocks, slots, owned,...  1.23 us
  transfers between devices with their start and end apart: 17, of which 9 were waited for; matrix products, arithmetic and copies ran while one was open for 0% of the time, Pallas kernels for 7%

profile of v5, /device:TPU:0, one launch (start us, length us, event | category | flops | bytes accessed | tf_op | source)
XLA Modules:
  0.0 46.0 jit_solution(8293771118875541982)
XLA Ops:
  0.0 0.5 collective-permute-start
  0.5 0.0 copy-start.2
  0.5 1.0 %copy-done.2 = bf16[1024,256]{1,0:T(8,128)(2,1)S(1)} copy-done((bf16[1024,256]{1,0:T(8,128)(2,1)S(1)}, bf16[1024,256]{1,0:T(8,128)(2,1)}, u32[]{:S(2)}) %copy-start.2) | copy-done | bytes 524312
  1.5 0.1 keys.1.refs_2_
  1.6 2.6 %collective-permute-start.3 = (bf16[1024,128]{1,0:T(8,128)(2,1)S(1)}, bf16[1024,128]{1,0:T(8,128)(2,1)S(1)}, u32[]{:S(2)}, u32[]{:S(2)}) collective-permute-start(bf16[1024,128]{1,0:T(8,128)(2,1)S(1)} %keys.1.refs_2_), channel_id=1, source_target_pairs={{0,2},{2,0},{1,3},{3,1},{4,6},{6,4},{5,7},{7,5},{8,10},{10,8},{9,1... | collective-permute-start | bytes 786440 | tf_op jit(solution)/shard_map/ppermute | solution.py:31
  4.1 0.0 collective-permute-done.refs_1_
  4.1 0.0 copy-start.3
  4.1 1.0 %copy-done.3 = bf16[256,1024]{1,0:T(8,128)(2,1)S(1)} copy-done((bf16[256,1024]{1,0:T(8,128)(2,1)S(1)}, bf16[256,1024]{1,0:T(8,128)(2,1)}, u32[]{:S(2)}) %copy-start.3) | copy-done | bytes 524312
  5.2 1.1 %dispatch_own.1 = (bf16[256,128]{1,0:T(8,128)(2,1)S(1)}, bf16[256,128]{1,0:T(8,128)(2,1)S(1)}, f32[256,128]{1,0:T(8,128)S(1)}, f32[256,128]{1,0:T(8,128)S(1)}, b...) custom-call(bf16[256,1024]{1,0:T(8,128)(2,1)S(1)} %copy-done.3, ...), custom_call_target="tpu_custom_call" | custom-call | flops 268435456 | bytes 1048576 | tf_op jit(solution)/shard_map/dispatch_own/pallas_call | solution.py:18
  6.2 0.7 %collective-permute-start.1 = (bf16[72,1024]{1,0:T(8,128)(2,1)S(1)}, bf16[72,1024]{1,0:T(8,128)(2,1)S(1)}, u32[]{:S(2)}, u32[]{:S(2)}) collective-permute-start(bf16[72,1024]{1,0:T(8,128)(2,1)S(1)} %get-tuple-element.28), channel_id=1, source_target_pairs={{0,0},{1,9},{2,2},{3,11},{4,4},{5,13},{6,6},{7,15},{8,1},{9,8},{10... | collective-permute-start | bytes 442376 | tf_op jit(solution)/shard_map/ppermute | solution.py:54
  6.9 1.6 %collective-permute-start.2 = (bf16[72,1024]{1,0:T(8,128)(2,1)S(1)}, bf16[72,1024]{1,0:T(8,128)(2,1)S(1)}, u32[]{:S(2)}, u32[]{:S(2)}) collective-permute-start(bf16[72,1024]{1,0:T(8,128)(2,1)S(1)} %get-tuple-element.29), channel_id=1, source_target_pairs={{0,4},{1,13},{2,6},{3,15},{4,0},{5,9},{6,2},{7,11},{8,5},{9,12},{1... | collective-permute-start | bytes 442376 | tf_op jit(solution)/shard_map/ppermute | solution.py:54
  8.5 2.6 %collective-permute-done.3.refs_2_ = bf16[1024,128]{1,0:T(8,128)(2,1)S(1)} collective-permute-done((bf16[1024,128]{1,0:T(8,128)(2,1)S(1)}, bf16[1024,128]{1,0:T(8,128)(2,1)S(1)}, u32[]{:S(2)}, u32[]{:S(2)}) %collective-permute-start.3) | collective-permute-done | bytes 262176 | tf_op jit(solution)/shard_map/ppermute | solution.py:31
  11.1 0.8 %dispatch_other.1 = (bf16[256,128]{1,0:T(8,128)(2,1)S(1)}, bf16[256,128]{1,0:T(8,128)(2,1)S(1)}, bf16[72,1024]{1,0:T(8,128)(2,1)S(1)}, bf16[72,1024]{1,0:T(8,128)(2,1)S(1)}) custom-call(bf16[256,1024]{1,0:T(8,128)(2,1)S(1)} %get-tuple-element.30.refs_0_, bf16[256,1024]{1,0:T(8,128)(2,1)S(1)} %collective-permute-done.refs_1_, ...), custom_call_target="tpu_custom_call" | custom-call | flops 268435456 | bytes 1048576 | tf_op jit(solution)/shard_map/dispatch_other/pallas_call | solution.py:18
  11.9 1.8 %collective-permute-start.4 = (bf16[72,1024]{1,0:T(8,128)(2,1)S(1)}, bf16[72,1024]{1,0:T(8,128)(2,1)S(1)}, u32[]{:S(2)}, u32[]{:S(2)}) collective-permute-start(bf16[72,1024]{1,0:T(8,128)(2,1)S(1)} %get-tuple-element.33), channel_id=1, source_target_pairs={{0,2},{1,11},{2,0},{3,9},{4,6},{5,15},{6,4},{7,13},{8,3},{9,10},{1... | collective-permute-start | bytes 442376 | tf_op jit(solution)/shard_map/ppermute | solution.py:54
  13.7 1.6 %collective-permute-start.5 = (bf16[72,1024]{1,0:T(8,128)(2,1)S(1)}, bf16[72,1024]{1,0:T(8,128)(2,1)S(1)}, u32[]{:S(2)}, u32[]{:S(2)}) collective-permute-start(bf16[72,1024]{1,0:T(8,128)(2,1)S(1)} %get-tuple-element.34), channel_id=1, source_target_pairs={{0,6},{1,15},{2,4},{3,13},{4,2},{5,11},{6,0},{7,9},{8,7},{9,14},{1... | collective-permute-start | bytes 442376 | tf_op jit(solution)/shard_map/ppermute | solution.py:54
  15.3 1.9 %collective-permute-start.7 = (bf16[256,128]{1,0:T(8,128)(2,1)S(1)}, bf16[256,128]{1,0:T(8,128)(2,1)S(1)}, u32[]{:S(2)}, u32[]{:S(2)}) collective-permute-start(bf16[256,128]{1,0:T(8,128)(2,1)S(1)} %get-tuple-element.38.after_ref), channel_id=1, source_target_pairs={{0,1},{1,0},{2,3},{3,2},{4,5},{5,4},{6,7},{7,6},{8,9},{9,8},{10,11... | collective-permute-start | bytes 196616 | tf_op jit(solution)/shard_map/ppermute | solution.py:31
  17.2 0.9 %collective-permute-done.7.refs_3_.refs_1_ = bf16[256,128]{1,0:T(8,128)(2,1)S(1)} collective-permute-done((bf16[256,128]{1,0:T(8,128)(2,1)S(1)}, bf16[256,128]{1,0:T(8,128)(2,1)S(1)}, u32[]{:S(2)}, u32[]{:S(2)}) %collective-permute-start.7) | collective-permute-done | bytes 65568 | tf_op jit(solution)/shard_map/ppermute | solution.py:31
  18.1 0.4 collective-permute-start.6
  18.4 2.2 %copy-done = bf16[1,1,2048,1024]{3,2,1,0:T(8,128)(2,1)S(1)} copy-done((bf16[1,1,2048,1024]{3,2,1,0:T(8,128)(2,1)S(1)}, bf16[1,1,2048,1024]{3,2,1,0:T(8,128)(2,1)}, u32[]{:S(2)}) %copy-start) | copy-done | bytes 4194328
  20.6 0.3 stage.1.out_w_ref
  20.9 0.0 collective-permute-done.6.refs_1_
  20.9 0.0 collective-permute-done.1.refs_0_
  20.9 0.0 collective-permute-done.2.refs_1_
  20.9 0.0 collective-permute-done.4.refs_2_
  21.0 0.0 collective-permute-done.5.refs_3_
  21.0 0.1 sum_pieces.1.mine_ref
  21.0 2.9 %collective-permute-start.8 = (f32[72,1024]{1,0:T(8,128)S(1)}, f32[72,1024]{1,0:T(8,128)S(1)}, u32[]{:S(2)}, u32[]{:S(2)}) collective-permute-start(f32[72,1024]{1,0:T(8,128)S(1)} %sum_pieces.1.mine_ref), channel_id=1, source_target_pairs={{0,1},{1,0},{2,3},{3,2},{4,5},{5,4},{6,7},{7,6},{8,9},{9,8},{10,11... | collective-permute-start | bytes 884744 | tf_op jit(solution)/shard_map/ppermute | solution.py:31
  23.9 1.2 %collective-permute-done.8.other_ref = f32[72,1024]{1,0:T(8,128)S(1)} collective-permute-done((f32[72,1024]{1,0:T(8,128)S(1)}, f32[72,1024]{1,0:T(8,128)S(1)}, u32[]{:S(2)}, u32[]{:S(2)}) %collective-permute-start.8) | collective-permute-done | bytes 294944 | tf_op jit(solution)/shard_map/ppermute | solution.py:31
  25.1 0.0 copy-done.1
  25.1 1.7 %expert.1.part_ref = f32[64,1024]{1,0:T(8,128)S(1)} custom-call(f32[72,1024]{1,0:T(8,128)S(1)} %sum_pieces.1.mine_ref, f32[72,1024]{1,0:T(8,128)S(1)} %collective-permute-done.8.other_ref, bf16[1024,2048]{1,0:T(8,128)(2,1)S(1)} %bitcast.3, bf16[2048,1024]{1,0:T(8,128)(2,1)S(1)} %stage.1.out_w_ref), custom_call_target="tpu_custom_call" | custom-call | flops 536870912 | bytes 8388608 | tf_op jit(solution)/shard_map/expert/pallas_call | solution.py:18
  26.8 0.4 collective-permute-start.9
  27.2 1.2 %collective-permute-done.9.recv_ref = f32[64,1024]{1,0:T(8,128)S(1)} collective-permute-done((f32[64,1024]{1,0:T(8,128)S(1)}, f32[64,1024]{1,0:T(8,128)S(1)}, u32[]{:S(2)}, u32[]{:S(2)}) %collective-permute-start.9) | collective-permute-done | bytes 262176 | tf_op jit(solution)/shard_map/ppermute | solution.py:31
  28.4 2.8 %collective-permute-start.14 = (bf16[64,1024]{1,0:T(8,128)(2,1)S(1)}, bf16[64,1024]{1,0:T(8,128)(2,1)S(1)}, u32[]{:S(2)}, u32[]{:S(2)}) collective-permute-start(bf16[64,1024]{1,0:T(8,128)(2,1)S(1)} %slot_outputs.1.refs_4_), channel_id=1, source_target_pairs={{0,6},{1,7},{2,4},{3,5},{4,2},{5,3},{6,0},{7,1},{8,14},{9,15},{10,... | collective-permute-start | bytes 393224 | tf_op jit(solution)/shard_map/ppermute | solution.py:42
  31.3 1.2 %collective-permute-start.10 = (bf16[64,1024]{1,0:T(8,128)(2,1)S(1)}, bf16[64,1024]{1,0:T(8,128)(2,1)S(1)}, u32[]{:S(2)}, u32[]{:S(2)}) collective-permute-start(bf16[64,1024]{1,0:T(8,128)(2,1)S(1)} %slot_outputs.1.refs_4_), channel_id=1, source_target_pairs={{0,8},{1,13},{2,10},{3,15},{4,12},{5,9},{6,14},{7,11},{8,0},{9,5},... | collective-permute-start | bytes 393224 | tf_op jit(solution)/shard_map/ppermute | solution.py:42
  32.5 2.1 %collective-permute-start.12 = (bf16[64,1024]{1,0:T(8,128)(2,1)S(1)}, bf16[64,1024]{1,0:T(8,128)(2,1)S(1)}, u32[]{:S(2)}, u32[]{:S(2)}) collective-permute-start(bf16[64,1024]{1,0:T(8,128)(2,1)S(1)} %slot_outputs.1.refs_4_), channel_id=1, source_target_pairs={{0,4},{1,3},{2,6},{3,1},{4,0},{5,7},{6,2},{7,5},{8,12},{9,11},{10,... | collective-permute-start | bytes 393224 | tf_op jit(solution)/shard_map/ppermute | solution.py:42
  34.6 0.6 %collective-permute-done.14.refs_9_ = bf16[64,1024]{1,0:T(8,128)(2,1)S(1)} collective-permute-done((bf16[64,1024]{1,0:T(8,128)(2,1)S(1)}, bf16[64,1024]{1,0:T(8,128)(2,1)S(1)}, u32[]{:S(2)}, u32[]{:S(2)}) %collective-permute-start.14) | collective-permute-done | bytes 131104 | tf_op jit(solution)/shard_map/ppermute | solution.py:42
  35.3 2.1 %collective-permute-done.10.refs_5_ = bf16[64,1024]{1,0:T(8,128)(2,1)S(1)} collective-permute-done((bf16[64,1024]{1,0:T(8,128)(2,1)S(1)}, bf16[64,1024]{1,0:T(8,128)(2,1)S(1)}, u32[]{:S(2)}, u32[]{:S(2)}) %collective-permute-start.10) | collective-permute-done | bytes 131104 | tf_op jit(solution)/shard_map/ppermute | solution.py:42
  37.4 0.8 %collective-permute-start.15 = (bf16[64,1024]{1,0:T(8,128)(2,1)S(1)}, bf16[64,1024]{1,0:T(8,128)(2,1)S(1)}, u32[]{:S(2)}, u32[]{:S(2)}) collective-permute-start(bf16[64,1024]{1,0:T(8,128)(2,1)S(1)} %collective-permute-done.10.refs_5_), channel_id=1, source_target_pairs={{0,2},{1,3},{2,0},{3,1},{4,6},{5,7},{6,4},{7,5},{8,10},{9,11},{10,... | collective-permute-start | bytes 393224 | tf_op jit(solution)/shard_map/ppermute | solution.py:42
  38.3 1.5 %collective-permute-done.12.refs_7_ = bf16[64,1024]{1,0:T(8,128)(2,1)S(1)} collective-permute-done((bf16[64,1024]{1,0:T(8,128)(2,1)S(1)}, bf16[64,1024]{1,0:T(8,128)(2,1)S(1)}, u32[]{:S(2)}, u32[]{:S(2)}) %collective-permute-start.12) | collective-permute-done | bytes 131104 | tf_op jit(solution)/shard_map/ppermute | solution.py:42
  39.8 0.7 %collective-permute-start.13 = (bf16[64,1024]{1,0:T(8,128)(2,1)S(1)}, bf16[64,1024]{1,0:T(8,128)(2,1)S(1)}, u32[]{:S(2)}, u32[]{:S(2)}) collective-permute-start(bf16[64,1024]{1,0:T(8,128)(2,1)S(1)} %collective-permute-done.12.refs_7_), channel_id=1, source_target_pairs={{0,1},{1,0},{2,3},{3,2},{4,5},{5,4},{6,7},{7,6},{8,9},{9,8},{10,11... | collective-permute-start | bytes 393224 | tf_op jit(solution)/shard_map/ppermute | solution.py:31
  40.5 0.0 collective-permute-start.11
  40.5 1.9 %collective-permute-done.15.refs_4_ = bf16[64,1024]{1,0:T(8,128)(2,1)S(1)} collective-permute-done((bf16[64,1024]{1,0:T(8,128)(2,1)S(1)}, bf16[64,1024]{1,0:T(8,128)(2,1)S(1)}, u32[]{:S(2)}, u32[]{:S(2)}) %collective-permute-start.15) | collective-permute-done | bytes 131104 | tf_op jit(solution)/shard_map/ppermute | solution.py:42
  42.4 1.3 %collective-permute-start.16 = (bf16[64,1024]{1,0:T(8,128)(2,1)S(1)}, bf16[64,1024]{1,0:T(8,128)(2,1)S(1)}, u32[]{:S(2)}, u32[]{:S(2)}) collective-permute-start(bf16[64,1024]{1,0:T(8,128)(2,1)S(1)} %collective-permute-done.15.refs_4_), channel_id=1, source_target_pairs={{0,1},{1,0},{2,3},{3,2},{4,5},{5,4},{6,7},{7,6},{8,9},{9,8},{10,11... | collective-permute-start | bytes 393224 | tf_op jit(solution)/shard_map/ppermute | solution.py:31
  43.7 0.0 collective-permute-done.13.refs_8_
  43.7 0.0 collective-permute-done.11.refs_6_
  43.7 0.8 %combine_first.1 = (f32[256,1024]{1,0:T(8,128)S(1)}, f32[256,128]{1,0:T(8,128)S(1)}) custom-call(bf16[256,128]{1,0:T(8,128)(2,1)S(1)} %get-tuple-element.41.refs_0_, bf16[256,128]{1,0:T(8,128)(2,1)S(1)} %collective-permute-done.6.refs_1_, bf16[256,128]{1,0:T(8,128)(2,1)S(1)} %get-tuple-element.39.refs_2_.refs_0_, ...), custom_call_target="tpu_custom_call" | custom-call | flops 268435456 | bytes 2097152 | tf_op jit(solution)/shard_map/combine_first/pallas_call | solution.py:18
  44.5 0.2 collective-permute-done.16.refs_5_
  44.7 1.2 %combine_last.1 = f32[256,1024]{1,0:T(8,128)} custom-call(bf16[256,128]{1,0:T(8,128)(2,1)S(1)} %get-tuple-element.39.refs_2_.refs_0_, bf16[256,128]{1,0:T(8,128)(2,1)S(1)} %collective-permute-done.7.refs_3_.refs_1_, f32[256,1024]{1,0:T(8,128)S(1)} %get-tuple-element.48.refs_2_, f32[256,128]{1,0:T(8,128)S(1)} %get-tuple-element.49.refs_3_, ...), custom_call_target="tpu_custom_call" | custom-call | tf_op jit(solution)/shard_map/combine_last/pallas_call | solution.py:300
  (3 shorter events, 0.0 us)
Async XLA Ops:
  0.0 4.1 %collective-permute-start = (bf16[256,1024]{1,0:T(8,128)(2,1)}, bf16[256,1024]{1,0:T(8,128)(2,1)S(1)}, u32[]{:S(2)}, u32[]{:S(2)}) collective-permute-start(bf16[256,1024]{1,0:T(8,128)(2,1)} %refs_0_.1), channel_id=1, source_target_pairs={{0,1},{1,0},{2,3},{3,2},{4,5},{5,4},{6,7},{7,6},{8,9},{9,8},{10,11... | collective-permute-start | bytes 1572872 | tf_op jit(solution)/shard_map/ppermute | solution.py:31
  0.5 1.0 %copy-start.2 = (bf16[1024,256]{1,0:T(8,128)(2,1)S(1)}, bf16[1024,256]{1,0:T(8,128)(2,1)}, u32[]{:S(2)}) copy-start(bf16[1024,256]{1,0:T(8,128)(2,1)} %key_ref.1) | copy-start | bytes 1572868
  1.6 9.5 %collective-permute-start.3 = (bf16[1024,128]{1,0:T(8,128)(2,1)S(1)}, bf16[1024,128]{1,0:T(8,128)(2,1)S(1)}, u32[]{:S(2)}, u32[]{:S(2)}) collective-permute-start(bf16[1024,128]{1,0:T(8,128)(2,1)S(1)} %keys.1.refs_2_), channel_id=1, source_target_pairs={{0,2},{2,0},{1,3},{3,1},{4,6},{6,4},{5,7},{7,5},{8,10},{10,8},{9,1... | collective-permute-start | bytes 786440 | tf_op jit(solution)/shard_map/ppermute | solution.py:31
  4.1 1.0 %copy-start.3 = (bf16[256,1024]{1,0:T(8,128)(2,1)S(1)}, bf16[256,1024]{1,0:T(8,128)(2,1)}, u32[]{:S(2)}) copy-start(bf16[256,1024]{1,0:T(8,128)(2,1)} %refs_0_.1) | copy-start | bytes 1572868
  6.2 14.7 %collective-permute-start.1 = (bf16[72,1024]{1,0:T(8,128)(2,1)S(1)}, bf16[72,1024]{1,0:T(8,128)(2,1)S(1)}, u32[]{:S(2)}, u32[]{:S(2)}) collective-permute-start(bf16[72,1024]{1,0:T(8,128)(2,1)S(1)} %get-tuple-element.28), channel_id=1, source_target_pairs={{0,0},{1,9},{2,2},{3,11},{4,4},{5,13},{6,6},{7,15},{8,1},{9,8},{10... | collective-permute-start | bytes 442376 | tf_op jit(solution)/shard_map/ppermute | solution.py:54
  6.9 14.0 %collective-permute-start.2 = (bf16[72,1024]{1,0:T(8,128)(2,1)S(1)}, bf16[72,1024]{1,0:T(8,128)(2,1)S(1)}, u32[]{:S(2)}, u32[]{:S(2)}) collective-permute-start(bf16[72,1024]{1,0:T(8,128)(2,1)S(1)} %get-tuple-element.29), channel_id=1, source_target_pairs={{0,4},{1,13},{2,6},{3,15},{4,0},{5,9},{6,2},{7,11},{8,5},{9,12},{1... | collective-permute-start | bytes 442376 | tf_op jit(solution)/shard_map/ppermute | solution.py:54
  11.9 9.0 %collective-permute-start.4 = (bf16[72,1024]{1,0:T(8,128)(2,1)S(1)}, bf16[72,1024]{1,0:T(8,128)(2,1)S(1)}, u32[]{:S(2)}, u32[]{:S(2)}) collective-permute-start(bf16[72,1024]{1,0:T(8,128)(2,1)S(1)} %get-tuple-element.33), channel_id=1, source_target_pairs={{0,2},{1,11},{2,0},{3,9},{4,6},{5,15},{6,4},{7,13},{8,3},{9,10},{1... | collective-permute-start | bytes 442376 | tf_op jit(solution)/shard_map/ppermute | solution.py:54
  13.7 7.2 %collective-permute-start.5 = (bf16[72,1024]{1,0:T(8,128)(2,1)S(1)}, bf16[72,1024]{1,0:T(8,128)(2,1)S(1)}, u32[]{:S(2)}, u32[]{:S(2)}) collective-permute-start(bf16[72,1024]{1,0:T(8,128)(2,1)S(1)} %get-tuple-element.34), channel_id=1, source_target_pairs={{0,6},{1,15},{2,4},{3,13},{4,2},{5,11},{6,0},{7,9},{8,7},{9,14},{1... | collective-permute-start | bytes 442376 | tf_op jit(solution)/shard_map/ppermute | solution.py:54
  15.3 2.8 %collective-permute-start.7 = (bf16[256,128]{1,0:T(8,128)(2,1)S(1)}, bf16[256,128]{1,0:T(8,128)(2,1)S(1)}, u32[]{:S(2)}, u32[]{:S(2)}) collective-permute-start(bf16[256,128]{1,0:T(8,128)(2,1)S(1)} %get-tuple-element.38.after_ref), channel_id=1, source_target_pairs={{0,1},{1,0},{2,3},{3,2},{4,5},{5,4},{6,7},{7,6},{8,9},{9,8},{10,11... | collective-permute-start | bytes 196616 | tf_op jit(solution)/shard_map/ppermute | solution.py:31
  18.1 2.8 %collective-permute-start.6 = (bf16[256,128]{1,0:T(8,128)(2,1)S(1)}, bf16[256,128]{1,0:T(8,128)(2,1)S(1)}, u32[]{:S(2)}, u32[]{:S(2)}) collective-permute-start(bf16[256,128]{1,0:T(8,128)(2,1)S(1)} %get-tuple-element.36), channel_id=1, source_target_pairs={{0,1},{1,0},{2,3},{3,2},{4,5},{5,4},{6,7},{7,6},{8,9},{9,8},{10,11... | collective-permute-start | bytes 196616 | tf_op jit(solution)/shard_map/ppermute | solution.py:31
  18.4 2.2 %copy-start = (bf16[1,1,2048,1024]{3,2,1,0:T(8,128)(2,1)S(1)}, bf16[1,1,2048,1024]{3,2,1,0:T(8,128)(2,1)}, u32[]{:S(2)}) copy-start(bf16[1,1,2048,1024]{3,2,1,0:T(8,128)(2,1)} %param.7) | copy-start | bytes 12582916
  20.6 4.5 %copy-start.1 = (bf16[1,1,1024,2048]{3,2,1,0:T(8,128)(2,1)S(1)}, bf16[1,1,1024,2048]{3,2,1,0:T(8,128)(2,1)}, u32[]{:S(2)}) copy-start(bf16[1,1,1024,2048]{3,2,1,0:T(8,128)(2,1)} %param.6) | copy-start | bytes 12582916
  21.0 4.1 %collective-permute-start.8 = (f32[72,1024]{1,0:T(8,128)S(1)}, f32[72,1024]{1,0:T(8,128)S(1)}, u32[]{:S(2)}, u32[]{:S(2)}) collective-permute-start(f32[72,1024]{1,0:T(8,128)S(1)} %sum_pieces.1.mine_ref), channel_id=1, source_target_pairs={{0,1},{1,0},{2,3},{3,2},{4,5},{5,4},{6,7},{7,6},{8,9},{9,8},{10,11... | collective-permute-start | bytes 884744 | tf_op jit(solution)/shard_map/ppermute | solution.py:31
  26.8 1.6 %collective-permute-start.9 = (f32[64,1024]{1,0:T(8,128)S(1)}, f32[64,1024]{1,0:T(8,128)S(1)}, u32[]{:S(2)}, u32[]{:S(2)}) collective-permute-start(f32[64,1024]{1,0:T(8,128)S(1)} %expert.1.part_ref), channel_id=1, source_target_pairs={{0,1},{1,0},{2,3},{3,2},{4,5},{5,4},{6,7},{7,6},{8,9},{9,8},{10,11... | collective-permute-start | bytes 786440 | tf_op jit(solution)/shard_map/ppermute | solution.py:31
  28.4 6.8 %collective-permute-start.14 = (bf16[64,1024]{1,0:T(8,128)(2,1)S(1)}, bf16[64,1024]{1,0:T(8,128)(2,1)S(1)}, u32[]{:S(2)}, u32[]{:S(2)}) collective-permute-start(bf16[64,1024]{1,0:T(8,128)(2,1)S(1)} %slot_outputs.1.refs_4_), channel_id=1, source_target_pairs={{0,6},{1,7},{2,4},{3,5},{4,2},{5,3},{6,0},{7,1},{8,14},{9,15},{10,... | collective-permute-start | bytes 393224 | tf_op jit(solution)/shard_map/ppermute | solution.py:42
  31.3 6.2 %collective-permute-start.10 = (bf16[64,1024]{1,0:T(8,128)(2,1)S(1)}, bf16[64,1024]{1,0:T(8,128)(2,1)S(1)}, u32[]{:S(2)}, u32[]{:S(2)}) collective-permute-start(bf16[64,1024]{1,0:T(8,128)(2,1)S(1)} %slot_outputs.1.refs_4_), channel_id=1, source_target_pairs={{0,8},{1,13},{2,10},{3,15},{4,12},{5,9},{6,14},{7,11},{8,0},{9,5},... | collective-permute-start | bytes 393224 | tf_op jit(solution)/shard_map/ppermute | solution.py:42
  32.5 7.3 %collective-permute-start.12 = (bf16[64,1024]{1,0:T(8,128)(2,1)S(1)}, bf16[64,1024]{1,0:T(8,128)(2,1)S(1)}, u32[]{:S(2)}, u32[]{:S(2)}) collective-permute-start(bf16[64,1024]{1,0:T(8,128)(2,1)S(1)} %slot_outputs.1.refs_4_), channel_id=1, source_target_pairs={{0,4},{1,3},{2,6},{3,1},{4,0},{5,7},{6,2},{7,5},{8,12},{9,11},{10,... | collective-permute-start | bytes 393224 | tf_op jit(solution)/shard_map/ppermute | solution.py:42
  37.4 5.0 %collective-permute-start.15 = (bf16[64,1024]{1,0:T(8,128)(2,1)S(1)}, bf16[64,1024]{1,0:T(8,128)(2,1)S(1)}, u32[]{:S(2)}, u32[]{:S(2)}) collective-permute-start(bf16[64,1024]{1,0:T(8,128)(2,1)S(1)} %collective-permute-done.10.refs_5_), channel_id=1, source_target_pairs={{0,2},{1,3},{2,0},{3,1},{4,6},{5,7},{6,4},{7,5},{8,10},{9,11},{10,... | collective-permute-start | bytes 393224 | tf_op jit(solution)/shard_map/ppermute | solution.py:42
  39.8 4.0 %collective-permute-start.13 = (bf16[64,1024]{1,0:T(8,128)(2,1)S(1)}, bf16[64,1024]{1,0:T(8,128)(2,1)S(1)}, u32[]{:S(2)}, u32[]{:S(2)}) collective-permute-start(bf16[64,1024]{1,0:T(8,128)(2,1)S(1)} %collective-permute-done.12.refs_7_), channel_id=1, source_target_pairs={{0,1},{1,0},{2,3},{3,2},{4,5},{5,4},{6,7},{7,6},{8,9},{9,8},{10,11... | collective-permute-start | bytes 393224 | tf_op jit(solution)/shard_map/ppermute | solution.py:31
  40.5 3.2 %collective-permute-start.11 = (bf16[64,1024]{1,0:T(8,128)(2,1)S(1)}, bf16[64,1024]{1,0:T(8,128)(2,1)S(1)}, u32[]{:S(2)}, u32[]{:S(2)}) collective-permute-start(bf16[64,1024]{1,0:T(8,128)(2,1)S(1)} %collective-permute-done.10.refs_5_), channel_id=1, source_target_pairs={{0,1},{1,0},{2,3},{3,2},{4,5},{5,4},{6,7},{7,6},{8,9},{9,8},{10,11... | collective-permute-start | bytes 393224 | tf_op jit(solution)/shard_map/ppermute | solution.py:31
  42.4 2.3 %collective-permute-start.16 = (bf16[64,1024]{1,0:T(8,128)(2,1)S(1)}, bf16[64,1024]{1,0:T(8,128)(2,1)S(1)}, u32[]{:S(2)}, u32[]{:S(2)}) collective-permute-start(bf16[64,1024]{1,0:T(8,128)(2,1)S(1)} %collective-permute-done.15.refs_4_), channel_id=1, source_target_pairs={{0,1},{1,0},{2,3},{3,2},{4,5},{5,4},{6,7},{7,6},{8,9},{9,8},{10,11... | collective-permute-start | bytes 393224 | tf_op jit(solution)/shard_map/ppermute | solution.py:31

commit v6 on v5

--- a/solution.py
+++ b/solution.py
@@ -231,7 +231,7 @@
         lows_shape + [((count, 128), f32)] * 2 + [((count, width), bf16)] + [piece] * (rows // 2),
         tokens, beside, keys, name="dispatch_own", flops=mac, nbytes=4 * count * width, scratch=scratch,
     )
-    sent = [spread(value, step, 0) for step, value in enumerate(pieces)]
+    sent = [spread(value, step, 0) for step, value in list(enumerate(pieces))[::-1]]
     lows = [low_mine, swap(low_send, "hid", 1)]
     for across in range(1, blocks):
         low_mine, low_send, *pieces = call(
@@ -258,7 +258,7 @@
     )
 
     far = [(over, 0) for over in range(2, rows)]
-    near = [(1, 0)] + [(0, across) for across in range(1, blocks)]
+    near = [(0, 1), (1, 1)] if blocks == 2 else [(1, 0)] + [(0, across) for across in range(1, blocks)]
     flights = []
 
     def fly(value, moves, came=None):
@@ -274,7 +274,7 @@
     for at in range(0, len(near), 2):
         fly(full, near[at : at + 2])
     for across in range(1, blocks):
-        fly(full, [(1, across)] * 2)
+        fly(full, [(1, 0)] * 2) if blocks == 2 else fly(full, [(1, across)] * 2)
     direct = len(flights)
     held = lax.optimization_barrier([got for got, _ in passed] + [got for got, came in flights if came[0] == came[1]])
     passed = [(got, moves) for got, (_, moves) in zip(held, passed)]

time: 46.3 us -> 45.9 us (level)
  starting transfers between devices: 23.3 us -> 19.7 us
  waiting for transfers between devices: 12.2 us -> 15.5 us
    ppermute x4, waiting for transfers between devices: 6.18 us -> 9.16 us  [swap_by_core(): return lax.ppermute(value, AXES, pairs)]
    ppermute x9, starting transfers between devices: 10.6 us -> 8.33 us  [swap(): lax.ppermute(value, axis, [(i, i ^ step) for i in range(lax.axis_size(axi...]
    ppermute x4, starting transfers between devices: 7.04 us -> 5.71 us  [swap_by_core(): return lax.ppermute(value, AXES, pairs)]
  transfers between devices with their start and end apart: 17 -> 17, of which waited for: 9 -> 8; matrix products, arithmetic and copies ran while one was open for 0% -> 0% of each run, Pallas kernels for 7% -> 7%
where the time goes in v6:
time: 45.9 us; the launch traced here: 45.7 us
  starting transfers between devices  19.7 us (43%)
  waiting for transfers between devices  15.5 us (34%)
  Pallas kernels  6.05 us (13%)
  local copies, waits for them, and re-layouts  4.27 us (9%)
    ppermute x4, waiting for transfers between devices, swap_by_core(): return lax.ppermute(value, AXES, pairs)  9.16 us
    ppermute x9, starting transfers between devices, swap(): lax.ppermute(value, axis, [(i, i ^ step) for i in range(lax.axis_size(axi...  8.33 us
    ppermute x9, waiting for transfers between devices, swap(): lax.ppermute(value, axis, [(i, i ^ step) for i in range(lax.axis_size(axi...  6.38 us
    ppermute x4, starting transfers between devices, swap_by_core(): return lax.ppermute(value, AXES, pairs)  5.71 us
    ppermute x4, starting transfers between devices, spread(): return lax.ppermute(value, AXES, pairs)  5.64 us
    pallas_call x8, Pallas kernels, call(): pl.pallas_call(body, out_shape=[jax.ShapeDtypeStruct(s, d) for s, d in ou...  4.82 us
    unnamed x8, local copies, waits for them, and re-layouts  4.27 us
    pallas_call x1, Pallas kernels, local(): pl.pallas_call(functools.partial(combine_last_body, blocks, slots, owned,...  1.23 us
  transfers between devices with their start and end apart: 17, of which 8 were waited for; matrix products, arithmetic and copies ran while one was open for 0% of the time, Pallas kernels for 7%

profile of v6, /device:TPU:0, one launch (start us, length us, event | category | flops | bytes accessed | tf_op | source)
XLA Modules:
  0.0 45.7 jit_solution(14686053461898012199)
XLA Ops:
  0.0 0.5 collective-permute-start
  0.5 0.0 copy-start.2
  0.5 1.0 %copy-done.2 = bf16[1024,256]{1,0:T(8,128)(2,1)S(1)} copy-done((bf16[1024,256]{1,0:T(8,128)(2,1)S(1)}, bf16[1024,256]{1,0:T(8,128)(2,1)}, u32[]{:S(2)}) %copy-start.2) | copy-done | bytes 524312
  1.5 0.1 keys.1.refs_2_
  1.6 2.6 %collective-permute-start.3 = (bf16[1024,128]{1,0:T(8,128)(2,1)S(1)}, bf16[1024,128]{1,0:T(8,128)(2,1)S(1)}, u32[]{:S(2)}, u32[]{:S(2)}) collective-permute-start(bf16[1024,128]{1,0:T(8,128)(2,1)S(1)} %keys.1.refs_2_), channel_id=1, source_target_pairs={{0,2},{2,0},{1,3},{3,1},{4,6},{6,4},{5,7},{7,5},{8,10},{10,8},{9,1... | collective-permute-start | bytes 786440 | tf_op jit(solution)/shard_map/ppermute | solution.py:31
  4.1 0.0 collective-permute-done.refs_1_
  4.1 0.0 copy-start.3
  4.1 1.0 %copy-done.3 = bf16[256,1024]{1,0:T(8,128)(2,1)S(1)} copy-done((bf16[256,1024]{1,0:T(8,128)(2,1)S(1)}, bf16[256,1024]{1,0:T(8,128)(2,1)}, u32[]{:S(2)}) %copy-start.3) | copy-done | bytes 524312
  5.2 1.1 %dispatch_own.1 = (bf16[256,128]{1,0:T(8,128)(2,1)S(1)}, bf16[256,128]{1,0:T(8,128)(2,1)S(1)}, f32[256,128]{1,0:T(8,128)S(1)}, f32[256,128]{1,0:T(8,128)S(1)}, b...) custom-call(bf16[256,1024]{1,0:T(8,128)(2,1)S(1)} %copy-done.3, ...), custom_call_target="tpu_custom_call" | custom-call | flops 268435456 | bytes 1048576 | tf_op jit(solution)/shard_map/dispatch_own/pallas_call | solution.py:18
  6.2 1.6 %collective-permute-start.1 = (bf16[72,1024]{1,0:T(8,128)(2,1)S(1)}, bf16[72,1024]{1,0:T(8,128)(2,1)S(1)}, u32[]{:S(2)}, u32[]{:S(2)}) collective-permute-start(bf16[72,1024]{1,0:T(8,128)(2,1)S(1)} %get-tuple-element.28), channel_id=1, source_target_pairs={{0,4},{1,13},{2,6},{3,15},{4,0},{5,9},{6,2},{7,11},{8,5},{9,12},{1... | collective-permute-start | bytes 442376 | tf_op jit(solution)/shard_map/ppermute | solution.py:54
  7.9 0.7 %collective-permute-start.2 = (bf16[72,1024]{1,0:T(8,128)(2,1)S(1)}, bf16[72,1024]{1,0:T(8,128)(2,1)S(1)}, u32[]{:S(2)}, u32[]{:S(2)}) collective-permute-start(bf16[72,1024]{1,0:T(8,128)(2,1)S(1)} %get-tuple-element.29), channel_id=1, source_target_pairs={{0,0},{1,9},{2,2},{3,11},{4,4},{5,13},{6,6},{7,15},{8,1},{9,8},{10... | collective-permute-start | bytes 442376 | tf_op jit(solution)/shard_map/ppermute | solution.py:54
  8.5 2.6 %collective-permute-done.3.refs_2_ = bf16[1024,128]{1,0:T(8,128)(2,1)S(1)} collective-permute-done((bf16[1024,128]{1,0:T(8,128)(2,1)S(1)}, bf16[1024,128]{1,0:T(8,128)(2,1)S(1)}, u32[]{:S(2)}, u32[]{:S(2)}) %collective-permute-start.3) | collective-permute-done | bytes 262176 | tf_op jit(solution)/shard_map/ppermute | solution.py:31
  11.1 0.8 %dispatch_other.1 = (bf16[256,128]{1,0:T(8,128)(2,1)S(1)}, bf16[256,128]{1,0:T(8,128)(2,1)S(1)}, bf16[72,1024]{1,0:T(8,128)(2,1)S(1)}, bf16[72,1024]{1,0:T(8,128)(2,1)S(1)}) custom-call(bf16[256,1024]{1,0:T(8,128)(2,1)S(1)} %get-tuple-element.30.refs_0_, bf16[256,1024]{1,0:T(8,128)(2,1)S(1)} %collective-permute-done.refs_1_, ...), custom_call_target="tpu_custom_call" | custom-call | flops 268435456 | bytes 1048576 | tf_op jit(solution)/shard_map/dispatch_other/pallas_call | solution.py:18
  11.9 1.8 %collective-permute-start.4 = (bf16[72,1024]{1,0:T(8,128)(2,1)S(1)}, bf16[72,1024]{1,0:T(8,128)(2,1)S(1)}, u32[]{:S(2)}, u32[]{:S(2)}) collective-permute-start(bf16[72,1024]{1,0:T(8,128)(2,1)S(1)} %get-tuple-element.33), channel_id=1, source_target_pairs={{0,2},{1,11},{2,0},{3,9},{4,6},{5,15},{6,4},{7,13},{8,3},{9,10},{1... | collective-permute-start | bytes 442376 | tf_op jit(solution)/shard_map/ppermute | solution.py:54
  13.7 1.6 %collective-permute-start.5 = (bf16[72,1024]{1,0:T(8,128)(2,1)S(1)}, bf16[72,1024]{1,0:T(8,128)(2,1)S(1)}, u32[]{:S(2)}, u32[]{:S(2)}) collective-permute-start(bf16[72,1024]{1,0:T(8,128)(2,1)S(1)} %get-tuple-element.34), channel_id=1, source_target_pairs={{0,6},{1,15},{2,4},{3,13},{4,2},{5,11},{6,0},{7,9},{8,7},{9,14},{1... | collective-permute-start | bytes 442376 | tf_op jit(solution)/shard_map/ppermute | solution.py:54
  15.3 1.9 %collective-permute-start.7 = (bf16[256,128]{1,0:T(8,128)(2,1)S(1)}, bf16[256,128]{1,0:T(8,128)(2,1)S(1)}, u32[]{:S(2)}, u32[]{:S(2)}) collective-permute-start(bf16[256,128]{1,0:T(8,128)(2,1)S(1)} %get-tuple-element.38.after_ref), channel_id=1, source_target_pairs={{0,1},{1,0},{2,3},{3,2},{4,5},{5,4},{6,7},{7,6},{8,9},{9,8},{10,11... | collective-permute-start | bytes 196616 | tf_op jit(solution)/shard_map/ppermute | solution.py:31
  17.2 0.9 %collective-permute-done.7.refs_3_.refs_1_ = bf16[256,128]{1,0:T(8,128)(2,1)S(1)} collective-permute-done((bf16[256,128]{1,0:T(8,128)(2,1)S(1)}, bf16[256,128]{1,0:T(8,128)(2,1)S(1)}, u32[]{:S(2)}, u32[]{:S(2)}) %collective-permute-start.7) | collective-permute-done | bytes 65568 | tf_op jit(solution)/shard_map/ppermute | solution.py:31
  18.1 0.4 collective-permute-start.6
  18.4 2.2 %copy-done = bf16[1,1,2048,1024]{3,2,1,0:T(8,128)(2,1)S(1)} copy-done((bf16[1,1,2048,1024]{3,2,1,0:T(8,128)(2,1)S(1)}, bf16[1,1,2048,1024]{3,2,1,0:T(8,128)(2,1)}, u32[]{:S(2)}) %copy-start) | copy-done | bytes 4194328
  20.6 0.3 stage.1.out_w_ref
  20.9 0.0 collective-permute-done.6.refs_1_
  20.9 0.0 collective-permute-done.1.refs_0_
  20.9 0.0 collective-permute-done.2.refs_1_
  20.9 0.0 collective-permute-done.4.refs_2_
  21.0 0.0 collective-permute-done.5.refs_3_
  21.0 0.1 sum_pieces.1.mine_ref
  21.0 2.1 %collective-permute-start.8 = (f32[72,1024]{1,0:T(8,128)S(1)}, f32[72,1024]{1,0:T(8,128)S(1)}, u32[]{:S(2)}, u32[]{:S(2)}) collective-permute-start(f32[72,1024]{1,0:T(8,128)S(1)} %sum_pieces.1.mine_ref), channel_id=1, source_target_pairs={{0,1},{1,0},{2,3},{3,2},{4,5},{5,4},{6,7},{7,6},{8,9},{9,8},{10,11... | collective-permute-start | bytes 884744 | tf_op jit(solution)/shard_map/ppermute | solution.py:31
  23.2 1.2 %collective-permute-done.8.other_ref = f32[72,1024]{1,0:T(8,128)S(1)} collective-permute-done((f32[72,1024]{1,0:T(8,128)S(1)}, f32[72,1024]{1,0:T(8,128)S(1)}, u32[]{:S(2)}, u32[]{:S(2)}) %collective-permute-start.8) | collective-permute-done | bytes 294944 | tf_op jit(solution)/shard_map/ppermute | solution.py:31
  24.4 0.0 copy-done.1
  24.4 1.7 %expert.1.part_ref = f32[64,1024]{1,0:T(8,128)S(1)} custom-call(f32[72,1024]{1,0:T(8,128)S(1)} %sum_pieces.1.mine_ref, f32[72,1024]{1,0:T(8,128)S(1)} %collective-permute-done.8.other_ref, bf16[1024,2048]{1,0:T(8,128)(2,1)S(1)} %bitcast.3, bf16[2048,1024]{1,0:T(8,128)(2,1)S(1)} %stage.1.out_w_ref), custom_call_target="tpu_custom_call" | custom-call | flops 536870912 | bytes 8388608 | tf_op jit(solution)/shard_map/expert/pallas_call | solution.py:18
  26.1 0.4 collective-permute-start.9
  26.5 1.2 %collective-permute-done.9.recv_ref = f32[64,1024]{1,0:T(8,128)S(1)} collective-permute-done((f32[64,1024]{1,0:T(8,128)S(1)}, f32[64,1024]{1,0:T(8,128)S(1)}, u32[]{:S(2)}, u32[]{:S(2)}) %collective-permute-start.9) | collective-permute-done | bytes 262176 | tf_op jit(solution)/shard_map/ppermute | solution.py:31
  27.7 2.0 %collective-permute-start.14 = (bf16[64,1024]{1,0:T(8,128)(2,1)S(1)}, bf16[64,1024]{1,0:T(8,128)(2,1)S(1)}, u32[]{:S(2)}, u32[]{:S(2)}) collective-permute-start(bf16[64,1024]{1,0:T(8,128)(2,1)S(1)} %slot_outputs.1.refs_4_), channel_id=1, source_target_pairs={{0,4},{1,5},{2,6},{3,7},{4,0},{5,1},{6,2},{7,3},{8,12},{9,13},{10,... | collective-permute-start | bytes 393224 | tf_op jit(solution)/shard_map/ppermute | solution.py:42
  29.7 1.2 %collective-permute-start.10 = (bf16[64,1024]{1,0:T(8,128)(2,1)S(1)}, bf16[64,1024]{1,0:T(8,128)(2,1)S(1)}, u32[]{:S(2)}, u32[]{:S(2)}) collective-permute-start(bf16[64,1024]{1,0:T(8,128)(2,1)S(1)} %slot_outputs.1.refs_4_), channel_id=1, source_target_pairs={{0,8},{1,13},{2,10},{3,15},{4,12},{5,9},{6,14},{7,11},{8,0},{9,5},... | collective-permute-start | bytes 393224 | tf_op jit(solution)/shard_map/ppermute | solution.py:42
  30.8 1.5 %collective-permute-start.12 = (bf16[64,1024]{1,0:T(8,128)(2,1)S(1)}, bf16[64,1024]{1,0:T(8,128)(2,1)S(1)}, u32[]{:S(2)}, u32[]{:S(2)}) collective-permute-start(bf16[64,1024]{1,0:T(8,128)(2,1)S(1)} %slot_outputs.1.refs_4_), channel_id=1, source_target_pairs={{0,2},{1,7},{2,0},{3,5},{4,6},{5,3},{6,4},{7,1},{8,10},{9,15},{10,... | collective-permute-start | bytes 393224 | tf_op jit(solution)/shard_map/ppermute | solution.py:42
  32.3 1.3 %collective-permute-done.14.refs_9_ = bf16[64,1024]{1,0:T(8,128)(2,1)S(1)} collective-permute-done((bf16[64,1024]{1,0:T(8,128)(2,1)S(1)}, bf16[64,1024]{1,0:T(8,128)(2,1)S(1)}, u32[]{:S(2)}, u32[]{:S(2)}) %collective-permute-start.14) | collective-permute-done | bytes 131104 | tf_op jit(solution)/shard_map/ppermute | solution.py:42
  33.7 4.4 %collective-permute-done.10.refs_5_ = bf16[64,1024]{1,0:T(8,128)(2,1)S(1)} collective-permute-done((bf16[64,1024]{1,0:T(8,128)(2,1)S(1)}, bf16[64,1024]{1,0:T(8,128)(2,1)S(1)}, u32[]{:S(2)}, u32[]{:S(2)}) %collective-permute-start.10) | collective-permute-done | bytes 131104 | tf_op jit(solution)/shard_map/ppermute | solution.py:42
  38.1 1.1 %collective-permute-start.15 = (bf16[64,1024]{1,0:T(8,128)(2,1)S(1)}, bf16[64,1024]{1,0:T(8,128)(2,1)S(1)}, u32[]{:S(2)}, u32[]{:S(2)}) collective-permute-start(bf16[64,1024]{1,0:T(8,128)(2,1)S(1)} %collective-permute-done.10.refs_5_), channel_id=1, source_target_pairs={{0,2},{1,3},{2,0},{3,1},{4,6},{5,7},{6,4},{7,5},{8,10},{9,11},{10,... | collective-permute-start | bytes 393224 | tf_op jit(solution)/shard_map/ppermute | solution.py:42
  39.2 0.0 collective-permute-done.12.refs_7_
  39.2 0.0 collective-permute-start.13
  39.2 0.5 %collective-permute-start.11 = (bf16[64,1024]{1,0:T(8,128)(2,1)S(1)}, bf16[64,1024]{1,0:T(8,128)(2,1)S(1)}, u32[]{:S(2)}, u32[]{:S(2)}) collective-permute-start(bf16[64,1024]{1,0:T(8,128)(2,1)S(1)} %collective-permute-done.10.refs_5_), channel_id=1, source_target_pairs={{0,1},{1,0},{2,3},{3,2},{4,5},{5,4},{6,7},{7,6},{8,9},{9,8},{10,11... | collective-permute-start | bytes 393224 | tf_op jit(solution)/shard_map/ppermute | solution.py:31
  39.7 3.4 %collective-permute-done.15.refs_4_ = bf16[64,1024]{1,0:T(8,128)(2,1)S(1)} collective-permute-done((bf16[64,1024]{1,0:T(8,128)(2,1)S(1)}, bf16[64,1024]{1,0:T(8,128)(2,1)S(1)}, u32[]{:S(2)}, u32[]{:S(2)}) %collective-permute-start.15) | collective-permute-done | bytes 131104 | tf_op jit(solution)/shard_map/ppermute | solution.py:42
  43.1 0.0 collective-permute-start.16
  43.1 0.0 collective-permute-done.13.refs_8_
  43.1 0.0 collective-permute-done.11.refs_6_
  43.1 0.8 %combine_first.1 = (f32[256,1024]{1,0:T(8,128)S(1)}, f32[256,128]{1,0:T(8,128)S(1)}) custom-call(bf16[256,128]{1,0:T(8,128)(2,1)S(1)} %get-tuple-element.41.refs_0_, bf16[256,128]{1,0:T(8,128)(2,1)S(1)} %collective-permute-done.6.refs_1_, bf16[256,128]{1,0:T(8,128)(2,1)S(1)} %get-tuple-element.39.refs_2_.refs_0_, ...), custom_call_target="tpu_custom_call" | custom-call | flops 268435456 | bytes 2097152 | tf_op jit(solution)/shard_map/combine_first/pallas_call | solution.py:18
  43.9 0.5 %collective-permute-done.16.refs_5_ = bf16[64,1024]{1,0:T(8,128)(2,1)S(1)} collective-permute-done((bf16[64,1024]{1,0:T(8,128)(2,1)S(1)}, bf16[64,1024]{1,0:T(8,128)(2,1)S(1)}, u32[]{:S(2)}, u32[]{:S(2)}) %collective-permute-start.16) | collective-permute-done | bytes 131104 | tf_op jit(solution)/shard_map/ppermute | solution.py:31
  44.4 1.2 %combine_last.1 = f32[256,1024]{1,0:T(8,128)} custom-call(bf16[256,128]{1,0:T(8,128)(2,1)S(1)} %get-tuple-element.39.refs_2_.refs_0_, bf16[256,128]{1,0:T(8,128)(2,1)S(1)} %collective-permute-done.7.refs_3_.refs_1_, f32[256,1024]{1,0:T(8,128)S(1)} %get-tuple-element.48.refs_2_, f32[256,128]{1,0:T(8,128)S(1)} %get-tuple-element.49.refs_3_, ...), custom_call_target="tpu_custom_call" | custom-call | tf_op jit(solution)/shard_map/combine_last/pallas_call | solution.py:300
  (3 shorter events, 0.0 us)
Async XLA Ops:
  0.0 4.1 %collective-permute-start = (bf16[256,1024]{1,0:T(8,128)(2,1)}, bf16[256,1024]{1,0:T(8,128)(2,1)S(1)}, u32[]{:S(2)}, u32[]{:S(2)}) collective-permute-start(bf16[256,1024]{1,0:T(8,128)(2,1)} %refs_0_.1), channel_id=1, source_target_pairs={{0,1},{1,0},{2,3},{3,2},{4,5},{5,4},{6,7},{7,6},{8,9},{9,8},{10,11... | collective-permute-start | bytes 1572872 | tf_op jit(solution)/shard_map/ppermute | solution.py:31
  0.5 1.0 %copy-start.2 = (bf16[1024,256]{1,0:T(8,128)(2,1)S(1)}, bf16[1024,256]{1,0:T(8,128)(2,1)}, u32[]{:S(2)}) copy-start(bf16[1024,256]{1,0:T(8,128)(2,1)} %key_ref.1) | copy-start | bytes 1572868
  1.6 9.5 %collective-permute-start.3 = (bf16[1024,128]{1,0:T(8,128)(2,1)S(1)}, bf16[1024,128]{1,0:T(8,128)(2,1)S(1)}, u32[]{:S(2)}, u32[]{:S(2)}) collective-permute-start(bf16[1024,128]{1,0:T(8,128)(2,1)S(1)} %keys.1.refs_2_), channel_id=1, source_target_pairs={{0,2},{2,0},{1,3},{3,1},{4,6},{6,4},{5,7},{7,5},{8,10},{10,8},{9,1... | collective-permute-start | bytes 786440 | tf_op jit(solution)/shard_map/ppermute | solution.py:31
  4.1 1.0 %copy-start.3 = (bf16[256,1024]{1,0:T(8,128)(2,1)S(1)}, bf16[256,1024]{1,0:T(8,128)(2,1)}, u32[]{:S(2)}) copy-start(bf16[256,1024]{1,0:T(8,128)(2,1)} %refs_0_.1) | copy-start | bytes 1572868
  6.2 14.7 %collective-permute-start.1 = (bf16[72,1024]{1,0:T(8,128)(2,1)S(1)}, bf16[72,1024]{1,0:T(8,128)(2,1)S(1)}, u32[]{:S(2)}, u32[]{:S(2)}) collective-permute-start(bf16[72,1024]{1,0:T(8,128)(2,1)S(1)} %get-tuple-element.28), channel_id=1, source_target_pairs={{0,4},{1,13},{2,6},{3,15},{4,0},{5,9},{6,2},{7,11},{8,5},{9,12},{1... | collective-permute-start | bytes 442376 | tf_op jit(solution)/shard_map/ppermute | solution.py:54
  7.9 13.1 %collective-permute-start.2 = (bf16[72,1024]{1,0:T(8,128)(2,1)S(1)}, bf16[72,1024]{1,0:T(8,128)(2,1)S(1)}, u32[]{:S(2)}, u32[]{:S(2)}) collective-permute-start(bf16[72,1024]{1,0:T(8,128)(2,1)S(1)} %get-tuple-element.29), channel_id=1, source_target_pairs={{0,0},{1,9},{2,2},{3,11},{4,4},{5,13},{6,6},{7,15},{8,1},{9,8},{10... | collective-permute-start | bytes 442376 | tf_op jit(solution)/shard_map/ppermute | solution.py:54
  11.9 9.0 %collective-permute-start.4 = (bf16[72,1024]{1,0:T(8,128)(2,1)S(1)}, bf16[72,1024]{1,0:T(8,128)(2,1)S(1)}, u32[]{:S(2)}, u32[]{:S(2)}) collective-permute-start(bf16[72,1024]{1,0:T(8,128)(2,1)S(1)} %get-tuple-element.33), channel_id=1, source_target_pairs={{0,2},{1,11},{2,0},{3,9},{4,6},{5,15},{6,4},{7,13},{8,3},{9,10},{1... | collective-permute-start | bytes 442376 | tf_op jit(solution)/shard_map/ppermute | solution.py:54
  13.7 7.2 %collective-permute-start.5 = (bf16[72,1024]{1,0:T(8,128)(2,1)S(1)}, bf16[72,1024]{1,0:T(8,128)(2,1)S(1)}, u32[]{:S(2)}, u32[]{:S(2)}) collective-permute-start(bf16[72,1024]{1,0:T(8,128)(2,1)S(1)} %get-tuple-element.34), channel_id=1, source_target_pairs={{0,6},{1,15},{2,4},{3,13},{4,2},{5,11},{6,0},{7,9},{8,7},{9,14},{1... | collective-permute-start | bytes 442376 | tf_op jit(solution)/shard_map/ppermute | solution.py:54
  15.3 2.8 %collective-permute-start.7 = (bf16[256,128]{1,0:T(8,128)(2,1)S(1)}, bf16[256,128]{1,0:T(8,128)(2,1)S(1)}, u32[]{:S(2)}, u32[]{:S(2)}) collective-permute-start(bf16[256,128]{1,0:T(8,128)(2,1)S(1)} %get-tuple-element.38.after_ref), channel_id=1, source_target_pairs={{0,1},{1,0},{2,3},{3,2},{4,5},{5,4},{6,7},{7,6},{8,9},{9,8},{10,11... | collective-permute-start | bytes 196616 | tf_op jit(solution)/shard_map/ppermute | solution.py:31
  18.1 2.8 %collective-permute-start.6 = (bf16[256,128]{1,0:T(8,128)(2,1)S(1)}, bf16[256,128]{1,0:T(8,128)(2,1)S(1)}, u32[]{:S(2)}, u32[]{:S(2)}) collective-permute-start(bf16[256,128]{1,0:T(8,128)(2,1)S(1)} %get-tuple-element.36), channel_id=1, source_target_pairs={{0,1},{1,0},{2,3},{3,2},{4,5},{5,4},{6,7},{7,6},{8,9},{9,8},{10,11... | collective-permute-start | bytes 196616 | tf_op jit(solution)/shard_map/ppermute | solution.py:31
  18.4 2.2 %copy-start = (bf16[1,1,2048,1024]{3,2,1,0:T(8,128)(2,1)S(1)}, bf16[1,1,2048,1024]{3,2,1,0:T(8,128)(2,1)}, u32[]{:S(2)}) copy-start(bf16[1,1,2048,1024]{3,2,1,0:T(8,128)(2,1)} %param.7) | copy-start | bytes 12582916
  20.6 3.8 %copy-start.1 = (bf16[1,1,1024,2048]{3,2,1,0:T(8,128)(2,1)S(1)}, bf16[1,1,1024,2048]{3,2,1,0:T(8,128)(2,1)}, u32[]{:S(2)}) copy-start(bf16[1,1,1024,2048]{3,2,1,0:T(8,128)(2,1)} %param.6) | copy-start | bytes 12582916
  21.0 3.3 %collective-permute-start.8 = (f32[72,1024]{1,0:T(8,128)S(1)}, f32[72,1024]{1,0:T(8,128)S(1)}, u32[]{:S(2)}, u32[]{:S(2)}) collective-permute-start(f32[72,1024]{1,0:T(8,128)S(1)} %sum_pieces.1.mine_ref), channel_id=1, source_target_pairs={{0,1},{1,0},{2,3},{3,2},{4,5},{5,4},{6,7},{7,6},{8,9},{9,8},{10,11... | collective-permute-start | bytes 884744 | tf_op jit(solution)/shard_map/ppermute | solution.py:31
  26.1 1.6 %collective-permute-start.9 = (f32[64,1024]{1,0:T(8,128)S(1)}, f32[64,1024]{1,0:T(8,128)S(1)}, u32[]{:S(2)}, u32[]{:S(2)}) collective-permute-start(f32[64,1024]{1,0:T(8,128)S(1)} %expert.1.part_ref), channel_id=1, source_target_pairs={{0,1},{1,0},{2,3},{3,2},{4,5},{5,4},{6,7},{7,6},{8,9},{9,8},{10,11... | collective-permute-start | bytes 786440 | tf_op jit(solution)/shard_map/ppermute | solution.py:31
  27.7 6.0 %collective-permute-start.14 = (bf16[64,1024]{1,0:T(8,128)(2,1)S(1)}, bf16[64,1024]{1,0:T(8,128)(2,1)S(1)}, u32[]{:S(2)}, u32[]{:S(2)}) collective-permute-start(bf16[64,1024]{1,0:T(8,128)(2,1)S(1)} %slot_outputs.1.refs_4_), channel_id=1, source_target_pairs={{0,4},{1,5},{2,6},{3,7},{4,0},{5,1},{6,2},{7,3},{8,12},{9,13},{10,... | collective-permute-start | bytes 393224 | tf_op jit(solution)/shard_map/ppermute | solution.py:42
  29.7 8.5 %collective-permute-start.10 = (bf16[64,1024]{1,0:T(8,128)(2,1)S(1)}, bf16[64,1024]{1,0:T(8,128)(2,1)S(1)}, u32[]{:S(2)}, u32[]{:S(2)}) collective-permute-start(bf16[64,1024]{1,0:T(8,128)(2,1)S(1)} %slot_outputs.1.refs_4_), channel_id=1, source_target_pairs={{0,8},{1,13},{2,10},{3,15},{4,12},{5,9},{6,14},{7,11},{8,0},{9,5},... | collective-permute-start | bytes 393224 | tf_op jit(solution)/shard_map/ppermute | solution.py:42
  30.8 8.4 %collective-permute-start.12 = (bf16[64,1024]{1,0:T(8,128)(2,1)S(1)}, bf16[64,1024]{1,0:T(8,128)(2,1)S(1)}, u32[]{:S(2)}, u32[]{:S(2)}) collective-permute-start(bf16[64,1024]{1,0:T(8,128)(2,1)S(1)} %slot_outputs.1.refs_4_), channel_id=1, source_target_pairs={{0,2},{1,7},{2,0},{3,5},{4,6},{5,3},{6,4},{7,1},{8,10},{9,15},{10,... | collective-permute-start | bytes 393224 | tf_op jit(solution)/shard_map/ppermute | solution.py:42
  38.1 5.0 %collective-permute-start.15 = (bf16[64,1024]{1,0:T(8,128)(2,1)S(1)}, bf16[64,1024]{1,0:T(8,128)(2,1)S(1)}, u32[]{:S(2)}, u32[]{:S(2)}) collective-permute-start(bf16[64,1024]{1,0:T(8,128)(2,1)S(1)} %collective-permute-done.10.refs_5_), channel_id=1, source_target_pairs={{0,2},{1,3},{2,0},{3,1},{4,6},{5,7},{6,4},{7,5},{8,10},{9,11},{10,... | collective-permute-start | bytes 393224 | tf_op jit(solution)/shard_map/ppermute | solution.py:42
  39.2 3.9 %collective-permute-start.13 = (bf16[64,1024]{1,0:T(8,128)(2,1)S(1)}, bf16[64,1024]{1,0:T(8,128)(2,1)S(1)}, u32[]{:S(2)}, u32[]{:S(2)}) collective-permute-start(bf16[64,1024]{1,0:T(8,128)(2,1)S(1)} %collective-permute-done.12.refs_7_), channel_id=1, source_target_pairs={{0,1},{1,0},{2,3},{3,2},{4,5},{5,4},{6,7},{7,6},{8,9},{9,8},{10,11... | collective-permute-start | bytes 393224 | tf_op jit(solution)/shard_map/ppermute | solution.py:31
  39.2 3.9 %collective-permute-start.11 = (bf16[64,1024]{1,0:T(8,128)(2,1)S(1)}, bf16[64,1024]{1,0:T(8,128)(2,1)S(1)}, u32[]{:S(2)}, u32[]{:S(2)}) collective-permute-start(bf16[64,1024]{1,0:T(8,128)(2,1)S(1)} %collective-permute-done.10.refs_5_), channel_id=1, source_target_pairs={{0,1},{1,0},{2,3},{3,2},{4,5},{5,4},{6,7},{7,6},{8,9},{9,8},{10,11... | collective-permute-start | bytes 393224 | tf_op jit(solution)/shard_map/ppermute | solution.py:31
  43.1 1.3 %collective-permute-start.16 = (bf16[64,1024]{1,0:T(8,128)(2,1)S(1)}, bf16[64,1024]{1,0:T(8,128)(2,1)S(1)}, u32[]{:S(2)}, u32[]{:S(2)}) collective-permute-start(bf16[64,1024]{1,0:T(8,128)(2,1)S(1)} %collective-permute-done.15.refs_4_), channel_id=1, source_target_pairs={{0,1},{1,0},{2,3},{3,2},{4,5},{5,4},{6,7},{7,6},{8,9},{9,8},{10,11... | collective-permute-start | bytes 393224 | tf_op jit(solution)/shard_map/ppermute | solution.py:31
